TPU v7x, 128 devices: a whole 4x4x4 slice. The times are simulated.
128 devices in a mesh: seq: 16 (over x, z), exp: 8 (over y, core).
Axes of the slice: x: 4, y: 4, z: 4, core: 2. Of those that a mesh axis runs over, the one named last changes fastest.
Arguments:
- ssd_input: bfloat16 [8192, 2, 4096], P('seq', None, 'exp'), may hold values from -6 to 6
- ssd_gate: bfloat16 [8192, 2, 4096], P('seq', None, 'exp'), may hold values from -6 to 6
- state_write: bfloat16 [8192, 2, 1024], P('seq', None, 'exp'), may hold values from -2 to 2
- state_read: bfloat16 [8192, 2, 1024], P('seq', None, 'exp'), may hold values from -2 to 2
- step_size: float32 [64, 2, 8192], P('exp', None, 'seq'), may hold values from 0.02 to 0.1
- decay_log: float32 [64, 2, 8192], P('exp', None, 'seq'), may hold values from -0.78 to 0
- skip_gain: float32 [64], P('exp'), may hold values from 0.5 to 2
- norm_gain: float32 [4096], P('exp'), may hold values from 0.5 to 1.5
- w_out: bfloat16 [4096, 2048], P('exp'), may hold values from -0.09375 to 0.09375
- resid: bfloat16 [8192, 2, 2048], P(('seq', 'exp')), may hold values from -6 to 6
- moe_gain: float32 [2048], replicated, may hold values from 0.5 to 1.5
- w_gate: bfloat16 [16, 2048, 7168], P('seq', None, 'exp'), may hold values from -0.125 to 0.125
- w_up: bfloat16 [16, 2048, 7168], P('seq', None, 'exp'), may hold values from -0.125 to 0.125
- w_down: bfloat16 [16, 7168, 2048], P('seq', 'exp'), may hold values from -0.0625 to 0.0625
- routes: int32 [8192, 2, 2], P(('seq', 'exp')), may hold values from 0 to 15, all different within a row; in each aligned block of 128 rows (0 to 127, 128 to 255, ..., all dimensions but the last counted through in order) at most 17 rows name the same one
- gates: float32 [8192, 2, 2], P(('seq', 'exp')), may hold values from 0.2 to 1
- directions: float32 [4, 2048], replicated, may hold values from -6 to 6
Outputs:
- steered: bfloat16 [8192, 2, 2048], P(('seq', 'exp'))
Inputs may be any that keep to these rules, and one draw needn't show every extreme that they name: `routes`: in every aligned block of 128 rows, rows taken in the order position then sequence (the rows of one device), each expert is named by at most 17 picks, a bound that some block reaches; the two ids of a row differ.
All inputs are finite; a program needn't handle non-finite values.
Results may differ from a plain program's by a relative error of at most 0.023.
Values may be sent and summed in bfloat16 or wider, within the bound.
No kernel may reach another device: no remote copies, remote signals or barrier semaphores. Data moves between devices by JAX's collectives and lax.ppermute only.
A program may use at most 128 MiB of HBM per device.

v0:
```python
import functools

import jax
import jax.numpy as jnp
from jax import lax
from jax.experimental import pallas as pl
from jax.experimental.pallas import tpu as pltpu
from jax.sharding import PartitionSpec as P

D = 2048
HEADS = 64
HEAD_DIM = 64
STATE = 128
GROUPS = 8
BLOCK = 256
FOLD = 16
F32 = jnp.float32
BF16 = jnp.bfloat16


def dot_last(left, right, **options):
    return lax.dot_general(
        left, right, (((1,), (1,)), ((), ())), preferred_element_type=F32, **options
    )


def two_parts(values):
    high = values.astype(BF16)
    return high, (values - high.astype(F32)).astype(BF16)


def triangle():
    row = lax.broadcasted_iota(jnp.int32, (BLOCK, BLOCK), 0)
    col = lax.broadcasted_iota(jnp.int32, (BLOCK, BLOCK), 1)
    return row >= col


def spread_heads(columns, heads):
    rows = columns.shape[0]
    lane = lax.broadcasted_iota(jnp.int32, (rows, 2 * HEAD_DIM), 1)
    pieces = []
    for head in range(0, heads, 2):
        left = jnp.broadcast_to(columns[:, head : head + 1], (rows, 2 * HEAD_DIM))
        right = jnp.broadcast_to(columns[:, head + 1 : head + 2], (rows, 2 * HEAD_DIM))
        pieces.append(jnp.where(lane < HEAD_DIM, left, right))
    return jnp.concatenate(pieces, axis=1)


def over_rows(values):
    heads = values.shape[0]
    return jnp.broadcast_to(values[:, None, :], (heads, HEAD_DIM, STATE)).reshape(
        heads * HEAD_DIM, STATE
    )


def contrib_kernel(decay, step, inputs, writes, parcel, first, total, running):
    block = pl.program_id(1)
    heads = decay.shape[1]
    ones = triangle().astype(F32)
    decays = decay[0]
    cum_row = dot_last(decays, ones, precision=lax.Precision.HIGHEST)
    end_row = jnp.broadcast_to(cum_row[:, BLOCK - 1 :], (heads, STATE))
    to_end_row = jnp.exp(cum_row[:, BLOCK - 1 :] - cum_row) * step[0]
    to_end = jnp.transpose(to_end_row)
    scaled = (inputs[0].astype(F32) * spread_heads(to_end, heads)).astype(BF16)
    contrib = lax.dot_general(
        scaled, writes[0], (((0,), (0,)), ((), ())), preferred_element_type=F32
    )

    @pl.when(block == 0)
    def _():
        first[0] = contrib
        running[...] = contrib
        total[...] = end_row

    @pl.when(block > 0)
    def _():
        running[...] = over_rows(jnp.exp(end_row)) * running[...] + contrib
        total[...] = total[...] + end_row

    @pl.when(block == pl.num_programs(1) - 1)
    def _():
        carried = jnp.exp(total[...])
        high, rest = two_parts(carried)
        middle, low = two_parts(carried - high.astype(F32))
        row = lax.broadcasted_iota(jnp.int32, (heads, 8, STATE), 1)
        wide = lambda part: jnp.broadcast_to(part.astype(F32)[:, None, :], (heads, 8, STATE))
        extra = jnp.where(
            row == 0,
            wide(high),
            jnp.where(row == 1, wide(middle), jnp.where(row == 2, wide(low), 0.0)),
        )
        parcel[:, :HEAD_DIM, :] = running[...].reshape(heads, HEAD_DIM, STATE).astype(BF16)
        parcel[:, HEAD_DIM:, :] = extra.astype(BF16)


def contrib_call(decays, steps, inputs, writes):
    seqs, heads, length = decays.shape
    width = inputs.shape[2]
    blocks = length // BLOCK
    return pl.pallas_call(
        contrib_kernel,
        grid=(seqs, blocks),
        in_specs=[
            pl.BlockSpec((1, heads, BLOCK), lambda b, c: (b, 0, c)),
            pl.BlockSpec((1, heads, BLOCK), lambda b, c: (b, 0, c)),
            pl.BlockSpec((1, BLOCK, width), lambda b, c: (b, c, 0)),
            pl.BlockSpec((1, BLOCK, STATE), lambda b, c: (b, c, 0)),
        ],
        out_specs=[
            pl.BlockSpec((heads, HEAD_DIM + 8, STATE), lambda b, c: (b, 0, 0)),
            pl.BlockSpec((1, width, STATE), lambda b, c: (b, 0, 0)),
        ],
        out_shape=[
            jax.ShapeDtypeStruct((seqs * heads, HEAD_DIM + 8, STATE), BF16),
            jax.ShapeDtypeStruct((seqs, width, STATE), F32),
        ],
        scratch_shapes=[pltpu.VMEM((heads, STATE), F32), pltpu.VMEM((width, STATE), F32)],
        compiler_params=pltpu.CompilerParams(
            dimension_semantics=("arbitrary", "arbitrary"), vmem_limit_bytes=28 * 2**20
        ),
        cost_estimate=pl.CostEstimate(flops=10**9, bytes_accessed=2 * 2**20, transcendentals=8192),
        name="contrib",
    )(decays, steps, inputs, writes)


def within_kernel(decay, step, inputs, writes, reads, skip, within):
    heads = decay.shape[1]
    causal = triangle()
    ones = causal.astype(F32)
    log2e = 1.4426950408889634
    decays = decay[0]
    cum_row = dot_last(decays, ones, precision=lax.Precision.HIGHEST) * log2e
    cum_col = jnp.transpose(cum_row)
    steps = step[0]
    scores = dot_last(reads[0], writes[0])
    scores = jnp.where(causal, scores, 0.0)
    quad = 4 * HEAD_DIM
    lane = lax.broadcasted_iota(jnp.int32, (BLOCK, quad), 1)
    for start in range(0, heads, 4):
        columns = inputs[0][:, start * HEAD_DIM : start * HEAD_DIM + quad]
        total = skip[:, start * HEAD_DIM : start * HEAD_DIM + quad] * columns.astype(F32)
        for offset in range(4):
            head = start + offset
            gap = jnp.minimum(cum_col[:, head : head + 1] - cum_row[head : head + 1, :], 0.0)
            weights = (jnp.exp2(gap) * steps[head : head + 1, :] * scores).astype(BF16)
            own = (lane >= offset * HEAD_DIM) & (lane < (offset + 1) * HEAD_DIM)
            total = total + jnp.dot(
                weights,
                jnp.where(own, columns, jnp.zeros_like(columns)),
                preferred_element_type=F32,
            )
        within[0, :, start * HEAD_DIM : start * HEAD_DIM + quad] = total


def within_call(which, decays, steps, inputs, writes, reads, skip):
    seqs, heads, length = decays.shape
    width = inputs.shape[2]
    return pl.pallas_call(
        within_kernel,
        grid=(length // BLOCK,),
        in_specs=[
            pl.BlockSpec((1, heads, BLOCK), lambda c: (which, 0, c)),
            pl.BlockSpec((1, heads, BLOCK), lambda c: (which, 0, c)),
            pl.BlockSpec((1, BLOCK, width), lambda c: (which, c, 0)),
            pl.BlockSpec((1, BLOCK, STATE), lambda c: (which, c, 0)),
            pl.BlockSpec((1, BLOCK, STATE), lambda c: (which, c, 0)),
            pl.BlockSpec((1, width), lambda c: (0, 0)),
        ],
        out_specs=pl.BlockSpec((1, BLOCK, width), lambda c: (0, c, 0)),
        out_shape=jax.ShapeDtypeStruct((1, length, width), F32),
        compiler_params=pltpu.CompilerParams(
            dimension_semantics=("arbitrary",), vmem_limit_bytes=28 * 2**20
        ),
        cost_estimate=pl.CostEstimate(
            flops=3 * 10**9, bytes_accessed=2 * 2**20, transcendentals=2**20
        ),
        name="within",
    )(decays, steps, inputs, writes, reads, skip)


def scan_kernel(parcels, states):
    ranks = parcels.shape[0]
    state = jnp.zeros((HEAD_DIM, STATE), F32)
    for rank in range(ranks):
        states[rank] = state.astype(BF16)
        if rank < ranks - 1:
            extra = parcels[rank, HEAD_DIM:, :].astype(F32)
            factor = extra[0:1] + extra[1:2] + extra[2:3]
            state = factor * state + parcels[rank, :HEAD_DIM, :].astype(F32)


def scan_call(parcels):
    ranks = parcels.shape[0]
    return pl.pallas_call(
        scan_kernel,
        out_shape=jax.ShapeDtypeStruct((ranks, HEAD_DIM, STATE), BF16),
        cost_estimate=pl.CostEstimate(flops=10**6, bytes_accessed=2**19, transcendentals=0),
        name="scan",
    )(parcels)


def mixer_kernel(
    place, decay, reads, entering, first, within, gate, gain, weight, kept, passed, held, sems
):
    block = pl.program_id(0)
    blocks = pl.num_programs(0)
    heads = decay.shape[1]
    width = gate.shape[2]
    chips, keep = kept.shape[0], kept.shape[1]
    ones = triangle().astype(F32)
    decays = decay[0]
    before = block > 0
    cum_row = dot_last(decays[:, BLOCK:], ones, precision=lax.Precision.HIGHEST)
    head_row = dot_last(decays[:, :BLOCK], ones, precision=lax.Precision.HIGHEST)
    prefix = jnp.exp(jnp.broadcast_to(head_row[:, BLOCK - 1 :], (heads, STATE)))
    arrived = entering[...].astype(F32).reshape(width, STATE)
    begin = jnp.where(before, over_rows(prefix) * arrived + first[0], arrived)
    cum = jnp.transpose(jnp.exp(jnp.where(before, cum_row, head_row)))
    high, low = two_parts(begin)
    vectors = reads[0]
    readout = dot_last(vectors, high) + dot_last(vectors, low)
    ssd_out = within[0] + spread_heads(cum, heads) * readout
    gates = gate[0].astype(F32)
    gated = ssd_out * (gates / (1.0 + jnp.exp(-gates)))
    factor = lax.rsqrt(jnp.mean(gated * gated, axis=-1, keepdims=True) + 1e-05)
    normed = (gated * factor * gain[...]).astype(BF16)
    product = jnp.dot(normed, weight[...], preferred_element_type=F32).astype(BF16)
    held[block] = product.reshape(held.shape[1], keep, D)
    pieces = held.shape[1]
    chip, core = lax.div(place[0], 2), lax.rem(place[0], 2)

    def piece(step, index, target):
        distance = lax.rem(step * (pieces // 2) + index // 2 - chip + chips, chips)
        return pltpu.make_async_copy(
            held.at[step, index], target.at[distance], sems.at[step, index]
        )

    for index in range(pieces):

        @pl.when(core == index % 2)
        def _():
            piece(block, index, kept).start()

        @pl.when(core != index % 2)
        def _():
            piece(block, index, passed).start()

    @pl.when(block == blocks - 1)
    def _():
        for step in range(held.shape[0]):
            for index in range(pieces):
                piece(step, index, kept).wait()


def mixer_call(which, place, decays, reads, entering, first, within, gate, gain, weight, columns):
    seqs, heads, length = decays.shape
    width = gate.shape[2]
    blocks = length // BLOCK
    keep = length // columns
    anywhere = pl.BlockSpec(memory_space=pl.ANY)
    return pl.pallas_call(
        mixer_kernel,
        grid=(blocks,),
        in_specs=[
            pl.BlockSpec(memory_space=pltpu.SMEM),
            pl.BlockSpec((1, heads, length), lambda c: (which, 0, 0)),
            pl.BlockSpec((1, BLOCK, STATE), lambda c: (which, c, 0)),
            pl.BlockSpec((heads, HEAD_DIM, STATE), lambda c: (which, 0, 0)),
            pl.BlockSpec((1, width, STATE), lambda c: (which, 0, 0)),
            pl.BlockSpec((1, BLOCK, width), lambda c: (0, c, 0)),
            pl.BlockSpec((1, BLOCK, width), lambda c: (which, c, 0)),
            pl.BlockSpec((1, width), lambda c: (0, 0)),
            pl.BlockSpec((width, D), lambda c: (0, 0)),
        ],
        out_specs=[anywhere, anywhere],
        out_shape=[jax.ShapeDtypeStruct((columns // 2, keep, D), BF16)] * 2,
        scratch_shapes=[
            pltpu.VMEM((blocks, columns // blocks, keep, D), BF16),
            pltpu.SemaphoreType.DMA((blocks, columns // blocks)),
        ],
        compiler_params=pltpu.CompilerParams(
            dimension_semantics=("arbitrary",), vmem_limit_bytes=28 * 2**20
        ),
        cost_estimate=pl.CostEstimate(
            flops=2 * 10**9, bytes_accessed=6 * 2**20, transcendentals=2**18
        ),
        name="mixer",
    )(place, decays, reads, entering, first, within, gate, gain, weight)


def unfold(rows, folded):
    pieces = [folded[pl.ds(part, rows, stride=FOLD), :].astype(BF16) for part in range(FOLD)]
    return jnp.concatenate(pieces, axis=1)


def fold(values, folded):
    rows = values.shape[0]
    for part in range(FOLD):
        folded[pl.ds(part, rows, stride=FOLD), :] = values[:, part * 128 : (part + 1) * 128]


def dispatch_kernel(
    residual, gain, places, own_top, got_top, own_bottom, got_bottom, *refs
):
    others = refs[:4]
    hidden, packed, folded = refs[4:]
    half = own_top.shape[1]
    for index, (own, got) in enumerate(((own_top, got_top), (own_bottom, got_bottom))):
        span = pl.ds(index * half, half)
        hidden[span, :] = (
            residual[span, :].astype(F32)
            + (own[0].astype(F32) + got[0].astype(F32))
            + others[2 * index][...].astype(F32)
            + others[2 * index + 1][...].astype(F32)
        )
    state = hidden[...]
    scale = lax.rsqrt(jnp.mean(state * state, axis=-1, keepdims=True) + 1e-05)
    moe_in = (state * scale * gain[...]).astype(BF16)
    rows = packed.shape[0]
    slot = lax.broadcasted_iota(jnp.int32, (rows + rows // FOLD, state.shape[0]), 0)
    chosen = (slot == places[0:1, :]) | (slot == places[1:2, :])
    select = jnp.where(chosen, 1.0, 0.0).astype(BF16)
    slots = jnp.dot(select, moe_in, preferred_element_type=F32)
    packed[:, :D] = slots[:rows].astype(BF16)
    fold(slots[rows:], folded)
    packed[:, D:] = folded[...].astype(BF16)


def dispatch_call(residual, gain, places, owns, others, experts):
    rows, half = residual.shape[0], residual.shape[0] // 2
    count = experts * FOLD
    whole = lambda shape: pl.BlockSpec(shape, lambda i: (0,) * len(shape))
    return pl.pallas_call(
        dispatch_kernel,
        grid=(1,),
        in_specs=[whole(residual.shape), whole(gain.shape), whole(places.shape)]
        + [whole((1, half, D))] * 4
        + [whole((half, D))] * 4,
        out_specs=[whole((rows, D)), whole((count, D + 128))],
        out_shape=[
            jax.ShapeDtypeStruct((rows, D), F32),
            jax.ShapeDtypeStruct((count, D + 128), BF16),
        ],
        scratch_shapes=[pltpu.VMEM((count, 128), F32)],
        compiler_params=pltpu.CompilerParams(vmem_limit_bytes=24 * 2**20),
        cost_estimate=pl.CostEstimate(
            flops=2 * 10**8, bytes_accessed=5 * 2**20, transcendentals=0
        ),
        name="dispatch",
    )(residual, gain, places, *owns, *others)


def combine_kernel(returned, places, gates, hidden, directions, out, folded, values):
    slots, rows = values.shape[0], hidden.shape[0]
    count = returned.shape[0]
    folded[...] = returned[:, D:].astype(F32)
    values[:count, :] = returned[:, :D]
    values[count:, :] = unfold(slots - count, folded)
    slot = lax.broadcasted_iota(jnp.int32, (rows, slots), 1)
    zero = jnp.zeros((rows, slots), F32)
    mix = jnp.where(slot == places[:, 0:1], gates[:, 0:1], zero) + jnp.where(
        slot == places[:, 1:2], gates[:, 1:2], zero
    )
    high, rest = two_parts(mix)
    middle, low = two_parts(mix - high.astype(F32))
    parts = jnp.concatenate([high, middle, low], axis=0)
    product = jnp.dot(parts, values[...], preferred_element_type=F32)
    combined = hidden[...] + (
        product[:rows] + product[rows : 2 * rows] + product[2 * rows :]
    )
    for index in range(directions.shape[0]):
        direction = directions[index : index + 1, :]
        norm = jnp.sum(direction * direction, axis=1, keepdims=True) + 1e-06
        along = jnp.sum(combined * direction, axis=1, keepdims=True) / norm
        combined = combined - along * direction
    out[...] = combined.astype(BF16)


def combine_call(returned, places, gates, hidden, directions):
    rows = hidden.shape[0]
    count = returned.shape[0]
    return pl.pallas_call(
        combine_kernel,
        out_shape=jax.ShapeDtypeStruct((rows, D), BF16),
        scratch_shapes=[
            pltpu.VMEM((count, 128), F32),
            pltpu.VMEM((count + count // FOLD, D), BF16),
        ],
        compiler_params=pltpu.CompilerParams(vmem_limit_bytes=24 * 2**20),
        cost_estimate=pl.CostEstimate(flops=10**9, bytes_accessed=4 * 2**20, transcendentals=0),
        name="combine",
    )(returned, places, gates, hidden, directions)


def expert_kernel(counts, *refs):
    number = len(counts)
    parts = refs[:number]
    gate, up, down, kept, passed = refs[number : number + 5]
    values, extra, folded, hidden, tail, main_sems, extra_sems = refs[number + 5 :]
    places = [sum(counts[:index]) for index in range(number)]
    count = sum(counts)
    lone = count // FOLD
    loads, extras = [], []
    for index, (part, place, size) in enumerate(zip(parts, places, counts)):
        span = pl.ds(place, size)
        extras.append(
            pltpu.make_async_copy(
                part.at[:, pl.ds(D, 128)], extra.at[span, :], extra_sems.at[index]
            )
        )
        loads.append(
            pltpu.make_async_copy(
                part.at[:, pl.ds(0, D)], values.at[span, :], main_sems.at[index]
            )
        )
    for load in extras + loads:
        load.start()
    for load in extras:
        load.wait()
    folded[...] = extra[...].astype(F32)
    values[count:, :] = unfold(lone, folded)
    for load in loads:
        load.wait()
    units = down.shape[0]
    whole = units // 256 * 256

    def open_units(start, size):
        span = pl.ds(start, size)
        first = jnp.dot(values[...], gate[:, span], preferred_element_type=F32)
        second = jnp.dot(values[...], up[:, span], preferred_element_type=F32)
        hidden[:, span] = (first / (1.0 + jnp.exp(-first)) * second).astype(BF16)

    @pl.loop(0, whole // 256)
    def _(index):
        open_units(pl.multiple_of(index * 256, 256), 256)

    if units > whole:
        open_units(whole, units - whole)
    half = kept.shape[0]

    @pl.loop(0, D // 256)
    def _(index):
        span = pl.ds(pl.multiple_of(index * 256, 256), 256)
        result = jnp.dot(hidden[...], down[:, span], preferred_element_type=F32)
        kept[:, span] = result[:half].astype(BF16)
        passed[:, span] = result[half:count].astype(BF16)
        tail[:, span] = result[count:]

    fold(tail[...], folded)
    kept[:, D:] = folded[:half, :].astype(BF16)
    passed[:, D:] = folded[half:, :].astype(BF16)


def expert_call(parts, gate, up, down):
    counts = tuple(part.shape[0] for part in parts)
    count = sum(counts)
    rows = count + count // FOLD
    units = down.shape[0]
    anywhere = pl.BlockSpec(memory_space=pl.ANY)
    near = pl.BlockSpec(memory_space=pltpu.VMEM)
    return pl.pallas_call(
        functools.partial(expert_kernel, counts),
        in_specs=[anywhere] * len(parts) + [near] * 3,
        out_specs=[near, near],
        out_shape=[jax.ShapeDtypeStruct((count // 2, D + 128), BF16)] * 2,
        scratch_shapes=[
            pltpu.VMEM((rows, D), BF16),
            pltpu.VMEM((count, 128), BF16),
            pltpu.VMEM((count, 128), F32),
            pltpu.VMEM((rows, units), BF16),
            pltpu.VMEM((count // FOLD, D), F32),
            pltpu.SemaphoreType.DMA((len(parts),)),
            pltpu.SemaphoreType.DMA((len(parts),)),
        ],
        compiler_params=pltpu.CompilerParams(vmem_limit_bytes=24 * 2**20),
        cost_estimate=pl.CostEstimate(
            flops=6 * rows * D * units,
            bytes_accessed=4 * rows * D + 6 * D * units,
            transcendentals=rows * units,
        ),
        name="expert",
    )(*parts, gate, up, down)


def from_before(values):
    size = lax.axis_size("exp")
    return lax.ppermute(values, "exp", [(i, (i + 2) % size) for i in range(size)])


def from_after(values):
    size = lax.axis_size("exp")
    return lax.ppermute(values, "exp", [(i, (i - 2) % size) for i in range(size)])


def from_sibling(values):
    size = lax.axis_size("exp")
    return lax.ppermute(values, "exp", [(i, i ^ 1) for i in range(size)])


def add_up(*terms):
    total = terms[0].astype(F32)
    for term in terms[1:]:
        total = total + term.astype(F32)
    return total.astype(BF16)


def after(values, *earlier):
    return lax.optimization_barrier((tuple(values), earlier))[0]


def expert_layer(own, gate, up, down):
    half = own.shape[0] // 2
    top, bottom = own[:half], own[half:]
    own_other = from_sibling(own)
    before_top = from_before(top)
    after_bottom = from_after(bottom)
    call = functools.partial(expert_call, gate=gate, up=up, down=down)
    kept_own, passed = call((own, own_other))
    before_top, after_bottom, kept_own, passed, top, bottom = after(
        (before_top, after_bottom, kept_own, passed, top, bottom)
    )
    got_own = from_sibling(passed)
    others = from_sibling(before_top), from_sibling(after_bottom)
    far_top = from_before(before_top)
    far_bottom = from_after(after_bottom)
    before_bottom = from_before(bottom)
    after_top = from_after(top)
    kept, passed = call((before_top, after_bottom, *others))
    far_top, far_bottom, got_own, kept, passed = after(
        (far_top, far_bottom, got_own, kept, passed)
    )
    got = from_sibling(passed)
    others = from_sibling(far_top), from_sibling(far_bottom)
    near_top, near_bottom = add_up(kept[:half], got[:half]), add_up(kept[half:], got[half:])
    near_top, near_bottom, far_top, far_bottom = after(
        (near_top, near_bottom, far_top, far_bottom)
    )
    top_after = from_after(near_top)
    bottom_before = from_before(near_bottom)
    kept, passed = call((far_top, far_bottom, *others))
    after_top, before_bottom, kept, passed = after((after_top, before_bottom, kept, passed))
    late = from_sibling(after_top), from_sibling(before_bottom)
    got = from_sibling(passed)
    far_top, far_bottom = add_up(kept[:half], got[:half]), add_up(kept[half:], got[half:])
    far_top, far_bottom, after_top, before_bottom = after(
        (far_top, far_bottom, after_top, before_bottom)
    )
    relay_top = from_before(far_top)
    relay_bottom = from_after(far_bottom)
    kept, passed = call((after_top, before_bottom, *late))
    relay_top, relay_bottom, top_after, bottom_before, kept, passed = after(
        (relay_top, relay_bottom, top_after, bottom_before, kept, passed)
    )
    got = from_sibling(passed)
    top_before = from_before(add_up(kept[:half], got[:half], relay_top))
    bottom_after = from_after(add_up(kept[half:], got[half:], relay_bottom))
    return jnp.concatenate(
        [
            add_up(kept_own[:half], got_own[:half], top_after, top_before),
            add_up(kept_own[half:], got_own[half:], bottom_before, bottom_after),
        ],
        axis=0,
    )


def on_device(
    ssd_input,
    ssd_gate,
    state_write,
    state_read,
    step_size,
    decay_log,
    skip_gain,
    norm_gain,
    w_out,
    resid,
    moe_gain,
    w_gate,
    w_up,
    w_down,
    routes,
    gates,
    directions,
):
    length_dev, seqs, width_dev = ssd_input.shape
    heads_dev = decay_log.shape[0]
    experts = lax.axis_size("seq")
    columns = lax.axis_size("exp")
    rows_keep = length_dev * seqs // columns

    def swap(values):
        return jnp.transpose(values, (1, 0, 2))

    decays, steps = swap(decay_log), swap(step_size)
    inputs, writes, reads = swap(ssd_input), swap(state_write), swap(state_read)
    parcel, first = contrib_call(decays, steps, inputs, writes)
    parcels = lax.all_to_all(parcel, "seq", split_axis=0, concat_axis=0, tiled=True)
    skip = jnp.repeat(skip_gain, HEAD_DIM)[None, :]
    within_early = within_call(0, decays, steps, inputs, writes, reads, skip)
    (parcels,) = after((parcels,), within_early)
    entering = lax.all_to_all(
        scan_call(parcels), "seq", split_axis=0, concat_axis=0, tiled=True
    )
    within_late = within_call(1, decays, steps, inputs, writes, reads, skip)
    gating = swap(ssd_gate)
    (entering,) = after((entering,), within_late, gating)
    place = lax.axis_index("exp").astype(jnp.int32)[None]
    shared = (decays, reads, entering, first)
    kept, passed = mixer_call(
        0, place, *shared, within_early, gating, norm_gain[None, :], w_out, columns
    )
    got = from_sibling(passed)
    (gating,) = after((gating,), kept)
    kept_late, passed = mixer_call(
        1, place, *shared, within_late, gating, norm_gain[None, :], w_out, columns
    )
    got_late = from_sibling(passed)
    relay_top = from_before(add_up(kept[2], got[2]))
    top_after = from_after(add_up(kept[3], got[3]))
    relay_bottom = from_after(add_up(kept_late[2], got_late[2]))
    bottom_before = from_before(add_up(kept_late[1], got_late[1]))
    top_before = from_before(add_up(kept[1], got[1], relay_top))
    bottom_after = from_after(add_up(kept_late[3], got_late[3], relay_bottom))
    capacity = max(2, 2 * rows_keep * 17 // (16 * experts))
    assert capacity == FOLD + 1
    picks = swap(routes).reshape(-1)
    onehot = (picks[:, None] == jnp.arange(experts, dtype=jnp.int32)[None, :]).astype(jnp.int32)
    before = jnp.cumsum(onehot, axis=0) - onehot
    ranked = jnp.sum(before * onehot, axis=1)
    places = jnp.where(
        ranked < FOLD, picks * FOLD + ranked, experts * FOLD + picks
    ).reshape(rows_keep, 2)
    hidden_state, packed = dispatch_call(
        swap(resid).reshape(rows_keep, D),
        moe_gain[None, :],
        places.T,
        (kept, got, kept_late, got_late),
        (top_after, top_before, bottom_before, bottom_after),
        experts,
    )
    arrived = lax.all_to_all(
        packed.reshape(experts, FOLD, D + 128), "seq", split_axis=0, concat_axis=0, tiled=True
    )
    summed = expert_layer(arrived.reshape(packed.shape), w_gate[0], w_up[0], w_down[0])
    returned = lax.all_to_all(
        summed.reshape(experts, FOLD, D + 128), "seq", split_axis=0, concat_axis=0, tiled=True
    )
    combined = combine_call(
        returned.reshape(packed.shape),
        places,
        swap(gates).reshape(rows_keep, 2),
        hidden_state,
        directions,
    )
    return swap(combined.reshape(seqs, length_dev // columns, D))


def solution(mesh):
    in_specs = (
        P("seq", None, "exp"),
        P("seq", None, "exp"),
        P("seq", None, "exp"),
        P("seq", None, "exp"),
        P("exp", None, "seq"),
        P("exp", None, "seq"),
        P("exp"),
        P("exp"),
        P("exp", None),
        P(("seq", "exp"), None, None),
        P(),
        P("seq", None, "exp"),
        P("seq", None, "exp"),
        P("seq", "exp", None),
        P(("seq", "exp"), None, None),
        P(("seq", "exp"), None, None),
        P(),
    )
    out_specs = P(("seq", "exp"), None, None)
    return jax.shard_map(
        on_device, mesh=mesh, in_specs=in_specs, out_specs=out_specs, check_vma=False
    )
```

profile of v0, /device:TPU:0, one launch (start us, length us, event | category | flops | bytes accessed | tf_op | source)
XLA Modules:
  0.0 232.8 jit_solution(4325844711812329887)
XLA Ops:
  0.0 1.4 copy.55
  1.6 5.8 %contrib.1 = (bf16[16,72,128]{2,1,0:T(8,128)(2,1)}, f32[2,512,128]{2,1,0:T(8,128)S(1)}) custom-call(f32[2,8,512]{2,1,0:T(8,128)S(1)} %get-tuple-element.118.decay, f32[2,8,512]{2,1,0:T(8,128)S(1)} %get-tuple-element.117.step, bf16[2,512,512]{2,1,0:T(8,128)(2,1)S(1)} %bitcast.88, bf16[2,512,128]{2,1,0:T(8,128)(2,1)S(1)} %bitcast.96), custom_call_target="tpu_custom_call" | custom-call | flops 1000000000 | bytes 2097152 | tf_op jit(solution)/shard_map/contrib/pallas_call | solution.py:101
  7.4 8.1 %all-to-all-start = ((bf16[16,72,128]{2,1,0:T(8,128)(2,1)}), bf16[16,72,128]{2,1,0:T(8,128)(2,1)}, u32[]{:S(2)}, u32[]{:S(2)}) async-start(bf16[16,72,128]{2,1,0:T(8,128)(2,1)} %get-tuple-element.53), calls=%async_computation | async-start | bytes 589824 | tf_op jit(solution)/shard_map/all_to_all | solution.py:598
  15.7 1.4 copy.54
  17.1 3.0 %within.2 = f32[1,512,512]{2,1,0:T(8,128)S(1)} custom-call(f32[2,8,512]{2,1,0:T(8,128)S(1)} %get-tuple-element.118.decay, f32[2,8,512]{2,1,0:T(8,128)S(1)} %get-tuple-element.117.step, bf16[2,512,512]{2,1,0:T(8,128)(2,1)S(1)} %bitcast.89, bf16[2,512,128]{2,1,0:T(8,128)(2,1)S(1)} %bitcast.97, bf16[2,512,128]{2,1,0:T(8,128)(2,1)S(1)} %bitcast.92, ...), custom_call_target="tpu_custom_call" | custom-call | flops 3000000000 | bytes 2097152 | tf_op jit(solution)/shard_map/within/pallas_call | solution.py:159
  21.1 3.3 %all-to-all-done.parcels = bf16[16,72,128]{2,1,0:T(8,128)(2,1)} async-done(((bf16[16,72,128]{2,1,0:T(8,128)(2,1)}), bf16[16,72,128]{2,1,0:T(8,128)(2,1)}, u32[]{:S(2)}, u32[]{:S(2)}) %all-to-all-start) | async-done | bytes 294944 | tf_op jit(solution)/shard_map/all_to_all | solution.py:598
  24.4 1.7 scan.1
  26.1 3.8 %all-to-all-start.1 = ((bf16[16,64,128]{2,1,0:T(8,128)(2,1)}), bf16[16,64,128]{2,1,0:T(8,128)(2,1)S(1)}, u32[]{:S(2)}, u32[]{:S(2)}) async-start(bf16[16,64,128]{2,1,0:T(8,128)(2,1)} %scan.1), calls=%async_computation.1 | async-start | bytes 524288 | tf_op jit(solution)/shard_map/all_to_all | solution.py:602
  30.0 3.0 %within.3 = f32[1,512,512]{2,1,0:T(8,128)S(1)} custom-call(f32[2,8,512]{2,1,0:T(8,128)S(1)} %get-tuple-element.118.decay, f32[2,8,512]{2,1,0:T(8,128)S(1)} %get-tuple-element.117.step, bf16[2,512,512]{2,1,0:T(8,128)(2,1)S(1)} %bitcast.90, bf16[2,512,128]{2,1,0:T(8,128)(2,1)S(1)} %bitcast.98, bf16[2,512,128]{2,1,0:T(8,128)(2,1)S(1)} %bitcast.93, ...), custom_call_target="tpu_custom_call" | custom-call | flops 3000000000 | bytes 2097152 | tf_op jit(solution)/shard_map/within/pallas_call | solution.py:159
  34.0 4.5 %all-to-all-done.1.entering = bf16[16,64,128]{2,1,0:T(8,128)(2,1)S(1)} async-done(((bf16[16,64,128]{2,1,0:T(8,128)(2,1)}), bf16[16,64,128]{2,1,0:T(8,128)(2,1)S(1)}, u32[]{:S(2)}, u32[]{:S(2)}) %all-to-all-start.1) | async-done | bytes 262176 | tf_op jit(solution)/shard_map/all_to_all | solution.py:602
  38.5 1.7 copy-done.10
  40.2 1.2 copy-done.19
  42.5 4.9 %mixer.2 = (bf16[4,64,2048]{2,1,0:T(8,128)(2,1)S(1)}, bf16[4,64,2048]{2,1,0:T(8,128)(2,1)}) custom-call(s32[1]{0:T(128)} %bitcast.8.place, f32[2,8,512]{2,1,0:T(8,128)S(1)} %get-tuple-element.118.decay, bf16[2,512,128]{2,1,0:T(8,128)(2,1)S(1)} %bitcast.94, bf16[16,64,128]{2,1,0:T(8,128)(2,1)S(1)} %all-to-all-done.1.entering, f32[2,512,128]{2,1,0:T(8,128)S(1)} %copy-done.21, ...), custom_call_target="tpu_custom_call" | custom-call | flops 2000000000 | bytes 6291456 | tf_op jit(solution)/shard_map/mixer/pallas_call | solution.py:262
  47.6 1.2 copy-done.2
  49.7 4.9 %mixer.3 = (bf16[4,64,2048]{2,1,0:T(8,128)(2,1)S(1)}, bf16[4,64,2048]{2,1,0:T(8,128)(2,1)}) custom-call(s32[1]{0:T(128)} %bitcast.8.place, f32[2,8,512]{2,1,0:T(8,128)S(1)} %get-tuple-element.118.decay, bf16[2,512,128]{2,1,0:T(8,128)(2,1)S(1)} %bitcast.95, bf16[16,64,128]{2,1,0:T(8,128)(2,1)S(1)} %copy-done.4, f32[2,512,128]{2,1,0:T(8,128)S(1)} %copy-done.22, ...), custom_call_target="tpu_custom_call" | custom-call | flops 2000000000 | bytes 6291456 | tf_op jit(solution)/shard_map/mixer/pallas_call | solution.py:262
  57.3 3.0 %collective-permute-start.2 = (bf16[64,2048]{1,0:T(8,128)(2,1)}, bf16[64,2048]{1,0:T(8,128)(2,1)S(1)}, u32[]{:S(2)}, u32[]{:S(2)}) collective-permute-start(bf16[64,2048]{1,0:T(8,128)(2,1)} %get-tuple-element.112), channel_id=1, source_target_pairs={{0,6},{1,7},{2,0},{3,1},{4,2},{5,3},{6,4},{7,5},{8,14},{9,15},{10,... | collective-permute-start | bytes 786440 | tf_op jit(solution)/shard_map/ppermute | solution.py:493
  60.3 1.9 fusion.5
  62.8 2.7 %collective-permute-start.6 = (bf16[64,2048]{1,0:T(8,128)(2,1)S(1)}, bf16[64,2048]{1,0:T(8,128)(2,1)S(1)}, u32[]{:S(2)}, u32[]{:S(2)}) collective-permute-start(bf16[64,2048]{1,0:T(8,128)(2,1)S(1)} %get-tuple-element.109), channel_id=1, source_target_pairs={{0,6},{1,7},{2,0},{3,1},{4,2},{5,3},{6,4},{7,5},{8,14},{9,15},{10,... | collective-permute-start | bytes 786440 | tf_op jit(solution)/shard_map/ppermute | solution.py:493
  65.5 5.2 %collective-permute-done.3 = bf16[64,2048]{1,0:T(8,128)(2,1)S(1)} collective-permute-done((bf16[64,2048]{1,0:T(8,128)(2,1)S(1)}, bf16[64,2048]{1,0:T(8,128)(2,1)S(1)}, u32[]{:S(2)}, u32[]{:S(2)}) %collective-permute-start.3) | collective-permute-done | bytes 262176 | tf_op jit(solution)/shard_map/ppermute | solution.py:488
  71.9 1.8 fusion
  73.7 3.7 %collective-permute-start.7 = (bf16[64,2048]{1,0:T(8,128)(2,1)}, bf16[64,2048]{1,0:T(8,128)(2,1)}, u32[]{:S(2)}, u32[]{:S(2)}) collective-permute-start(bf16[64,2048]{1,0:T(8,128)(2,1)} %fusion), channel_id=1, source_target_pairs={{0,6},{1,7},{2,0},{3,1},{4,2},{5,3},{6,4},{7,5},{8,14},{9,15},{10,... | collective-permute-start | bytes 786440 | tf_op jit(solution)/shard_map/ppermute | solution.py:493
  81.0 1.6 collective-permute-done.7.refs_3_
  83.7 2.2 dispatch.1
  86.0 20.0 %all_to_all.20 = bf16[16,16,2176]{2,1,0:T(8,128)(2,1)S(1)} all-to-all(bf16[16,16,2176]{2,1,0:T(8,128)(2,1)S(1)} %bitcast.85), channel_id=1, replica_groups=mesh['seq'=16,'exp'=8] {'seq'}, dimensions={0} | all-to-all | bytes 2228224 | tf_op jit(solution)/shard_map/all_to_all | solution.py:642
  106.2 3.8 %collective-permute-start.9 = (bf16[128,2176]{1,0:T(8,128)(2,1)S(1)}, bf16[128,2176]{1,0:T(8,128)(2,1)S(1)}, u32[]{:S(2)}, u32[]{:S(2)}) collective-permute-start(bf16[128,2176]{1,0:T(8,128)(2,1)S(1)} %bitcast.116), channel_id=1, source_target_pairs={{0,6},{1,7},{2,0},{3,1},{4,2},{5,3},{6,4},{7,5},{8,14},{9,15},{10,... | collective-permute-start | bytes 1671176 | tf_op jit(solution)/shard_map/ppermute | solution.py:493
  109.9 2.0 copy-done.8
  112.0 9.5 %expert.4 = (bf16[256,2176]{1,0:T(8,128)(2,1)S(1)}, bf16[256,2176]{1,0:T(8,128)(2,1)S(1)}) custom-call(bf16[256,2176]{1,0:T(8,128)(2,1)S(1)} %bitcast.82, bf16[256,2176]{1,0:T(8,128)(2,1)S(1)} %collective-permute-done.10.refs_1_, bf16[2048,896]{1,0:T(8,128)(2,1)S(1)} %bitcast.102, bf16[2048,896]{1,0:T(8,128)(2,1)S(1)} %bitcast.106, ...), custom_call_target="tpu_custom_call" | custom-call | flops 5989466112 | bytes 15466496 | tf_op jit(solution)/shard_map/expert/pallas_call | solution.py:462
  121.5 1.6 collective-permute-done.8.refs_0_
  123.7 1.1 collective-permute-start.11
  124.8 2.1 collective-permute-start.12
  126.9 9.5 %expert.5 = (bf16[256,2176]{1,0:T(8,128)(2,1)S(1)}, bf16[256,2176]{1,0:T(8,128)(2,1)S(1)}) custom-call(bf16[128,2176]{1,0:T(8,128)(2,1)S(1)} %collective-permute-done.8.refs_0_, bf16[128,2176]{1,0:T(8,128)(2,1)S(1)} %collective-permute-done.9.refs_1_, bf16[128,2176]{1,0:T(8,128)(2,1)S(1)} %collective-permute-done.14.refs_2_, ...), custom_call_target="tpu_custom_call" | custom-call | flops 5989466112 | bytes 15466496 | tf_op jit(solution)/shard_map/expert/pallas_call | solution.py:462
  136.5 3.5 %collective-permute-done.11.refs_0_ = bf16[128,2176]{1,0:T(8,128)(2,1)S(1)} collective-permute-done((bf16[128,2176]{1,0:T(8,128)(2,1)S(1)}, bf16[128,2176]{1,0:T(8,128)(2,1)S(1)}, u32[]{:S(2)}, u32[]{:S(2)}) %collective-permute-start.11) | collective-permute-done | bytes 557088 | tf_op jit(solution)/shard_map/ppermute | solution.py:488
  140.0 2.9 %collective-permute-start.16 = (bf16[128,2176]{1,0:T(8,128)(2,1)S(1)}, bf16[128,2176]{1,0:T(8,128)(2,1)S(1)}, u32[]{:S(2)}, u32[]{:S(2)}) collective-permute-start(bf16[128,2176]{1,0:T(8,128)(2,1)S(1)} %bitcast.119), channel_id=1, source_target_pairs={{0,6},{1,7},{2,0},{3,1},{4,2},{5,3},{6,4},{7,5},{8,14},{9,15},{10,... | collective-permute-start | bytes 1671176 | tf_op jit(solution)/shard_map/ppermute | solution.py:493
  143.7 1.2 collective-permute-done.19.refs_2_
  145.7 9.6 %expert.6 = (bf16[256,2176]{1,0:T(8,128)(2,1)S(1)}, bf16[256,2176]{1,0:T(8,128)(2,1)S(1)}) custom-call(bf16[128,2176]{1,0:T(8,128)(2,1)S(1)} %collective-permute-done.11.refs_0_, bf16[128,2176]{1,0:T(8,128)(2,1)S(1)} %collective-permute-done.12.refs_1_, bf16[128,2176]{1,0:T(8,128)(2,1)S(1)} %collective-permute-done.19.refs_2_, ...), custom_call_target="tpu_custom_call" | custom-call | flops 5989466112 | bytes 15466496 | tf_op jit(solution)/shard_map/expert/pallas_call | solution.py:462
  155.5 3.4 %collective-permute-done.17.refs_1_ = bf16[128,2176]{1,0:T(8,128)(2,1)S(1)} collective-permute-done((bf16[128,2176]{1,0:T(8,128)(2,1)S(1)}, bf16[128,2176]{1,0:T(8,128)(2,1)S(1)}, u32[]{:S(2)}, u32[]{:S(2)}) %collective-permute-start.17) | collective-permute-done | bytes 557088 | tf_op jit(solution)/shard_map/ppermute | solution.py:488
  159.2 1.7 collective-permute-start.25
  162.9 2.3 %collective-permute-start.23 = (bf16[128,2176]{1,0:T(8,128)(2,1)S(1)}, bf16[128,2176]{1,0:T(8,128)(2,1)S(1)}, u32[]{:S(2)}, u32[]{:S(2)}) collective-permute-start(bf16[128,2176]{1,0:T(8,128)(2,1)S(1)} %get-tuple-element.87), channel_id=1, source_target_pairs={{0,6},{1,7},{2,0},{3,1},{4,2},{5,3},{6,4},{7,5},{8,14},{9,15},{10,... | collective-permute-start | bytes 1671176 | tf_op jit(solution)/shard_map/ppermute | solution.py:493
  165.2 9.6 %expert.7 = (bf16[256,2176]{1,0:T(8,128)(2,1)S(1)}, bf16[256,2176]{1,0:T(8,128)(2,1)S(1)}) custom-call(bf16[128,2176]{1,0:T(8,128)(2,1)S(1)} %collective-permute-done.16.refs_0_, bf16[128,2176]{1,0:T(8,128)(2,1)S(1)} %collective-permute-done.17.refs_1_, bf16[128,2176]{1,0:T(8,128)(2,1)S(1)} %collective-permute-done.26.refs_2_, ...), custom_call_target="tpu_custom_call" | custom-call | flops 5989466112 | bytes 15466496 | tf_op jit(solution)/shard_map/expert/pallas_call | solution.py:462
  175.9 11.2 %collective-permute-done.22 = bf16[128,2176]{1,0:T(8,128)(2,1)S(1)} collective-permute-done((bf16[128,2176]{1,0:T(8,128)(2,1)S(1)}, bf16[128,2176]{1,0:T(8,128)(2,1)S(1)}, u32[]{:S(2)}, u32[]{:S(2)}) %collective-permute-start.22) | collective-permute-done | bytes 557088 | tf_op jit(solution)/shard_map/ppermute | solution.py:488
  187.1 2.8 %collective-permute-done.28 = bf16[256,2176]{1,0:T(8,128)(2,1)S(1)} collective-permute-done((bf16[256,2176]{1,0:T(8,128)(2,1)S(1)}, bf16[256,2176]{1,0:T(8,128)(2,1)S(1)}, u32[]{:S(2)}, u32[]{:S(2)}) %collective-permute-start.28) | collective-permute-done | bytes 1114144 | tf_op jit(solution)/shard_map/ppermute | solution.py:498
  190.9 2.7 %collective-permute-start.30 = (bf16[128,2176]{1,0:T(8,128)(2,1)S(1)}, bf16[128,2176]{1,0:T(8,128)(2,1)S(1)}, u32[]{:S(2)}, u32[]{:S(2)}) collective-permute-start(bf16[128,2176]{1,0:T(8,128)(2,1)S(1)} %get-tuple-element.104), channel_id=1, source_target_pairs={{0,6},{1,7},{2,0},{3,1},{4,2},{5,3},{6,4},{7,5},{8,14},{9,15},{10,... | collective-permute-start | bytes 1671176 | tf_op jit(solution)/shard_map/ppermute | solution.py:493
  193.6 12.6 %collective-permute-done.29 = bf16[128,2176]{1,0:T(8,128)(2,1)S(1)} collective-permute-done((bf16[128,2176]{1,0:T(8,128)(2,1)S(1)}, bf16[128,2176]{1,0:T(8,128)(2,1)S(1)}, u32[]{:S(2)}, u32[]{:S(2)}) %collective-permute-start.29) | collective-permute-done | bytes 557088 | tf_op jit(solution)/shard_map/ppermute | solution.py:488
  206.8 1.1 pad_maximum_fusion
  207.9 3.8 %all-to-all-start.3 = ((bf16[16,16,2176]{2,1,0:T(8,128)(2,1)}), bf16[16,16,2176]{2,1,0:T(8,128)(2,1)S(1)}, u32[]{:S(2)}, u32[]{:S(2)}) async-start(bf16[16,16,2176]{2,1,0:T(8,128)(2,1)} %bitcast.29), calls=%async_computation.3 | async-start | bytes 2228224 | tf_op jit(solution)/shard_map/all_to_all | solution.py:646
  211.8 18.0 %all-to-all-done.3 = bf16[16,16,2176]{2,1,0:T(8,128)(2,1)S(1)} async-done(((bf16[16,16,2176]{2,1,0:T(8,128)(2,1)}), bf16[16,16,2176]{2,1,0:T(8,128)(2,1)S(1)}, u32[]{:S(2)}, u32[]{:S(2)}) %all-to-all-start.3) | async-done | bytes 1114144 | tf_op jit(solution)/shard_map/all_to_all | solution.py:646
  229.8 1.7 combine.1
  231.5 1.3 copy.56
  (133 shorter events, 20.9 us)
Async XLA Ops:
  1.5 14.0 %copy-start.25 = (bf16[512,2,128]{2,1,0:T(2,128)(2,1)S(1)}, bf16[512,2,128]{2,1,0:T(2,128)(2,1)}, u32[]{:S(2)}) copy-start(bf16[512,2,128]{2,1,0:T(2,128)(2,1)} %param.20) | copy-start | bytes 786436
  7.4 8.2 %copy-start.31 = (f32[8]{0:T(128)S(1)}, f32[8]{0:T(128)}, u32[]{:S(2)}) copy-start(f32[8]{0:T(128)} %param.23) | copy-start | bytes 100
  7.4 17.0 %all-to-all-start = ((bf16[16,72,128]{2,1,0:T(8,128)(2,1)}), bf16[16,72,128]{2,1,0:T(8,128)(2,1)}, u32[]{:S(2)}, u32[]{:S(2)}) async-start(bf16[16,72,128]{2,1,0:T(8,128)(2,1)} %get-tuple-element.53), calls=%async_computation | async-start | bytes 589824 | tf_op jit(solution)/shard_map/all_to_all | solution.py:598
  17.1 21.4 %copy-start.1 = (bf16[512,2,512]{2,0,1:T(8,128)(2,1)}, bf16[512,2,512]{2,0,1:T(8,128)(2,1)S(1)}, u32[]{:S(2)}) copy-start(bf16[512,2,512]{2,0,1:T(8,128)(2,1)S(1)} %copy.54) | copy-start | bytes 3145732
  26.1 12.4 %all-to-all-start.1 = ((bf16[16,64,128]{2,1,0:T(8,128)(2,1)}), bf16[16,64,128]{2,1,0:T(8,128)(2,1)S(1)}, u32[]{:S(2)}, u32[]{:S(2)}) async-start(bf16[16,64,128]{2,1,0:T(8,128)(2,1)} %scan.1), calls=%async_computation.1 | async-start | bytes 524288 | tf_op jit(solution)/shard_map/all_to_all | solution.py:602
  30.0 8.5 %copy-start.15 = (f32[512]{0:T(512)S(1)}, f32[512]{0:T(512)}, u32[]{:S(2)}) copy-start(f32[512]{0:T(512)} %param.24) | copy-start | bytes 6148
  38.5 8.9 %copy-start.3 = (bf16[16,64,128]{2,1,0:T(8,128)(2,1)}, bf16[16,64,128]{2,1,0:T(8,128)(2,1)S(1)}, u32[]{:S(2)}) copy-start(bf16[16,64,128]{2,1,0:T(8,128)(2,1)S(1)} %all-to-all-done.1.entering) | copy-start | bytes 786436
  47.4 9.0 %collective-permute-start = (bf16[4,64,2048]{2,1,0:T(8,128)(2,1)}, bf16[4,64,2048]{2,1,0:T(8,128)(2,1)S(1)}, u32[]{:S(2)}, u32[]{:S(2)}) collective-permute-start(bf16[4,64,2048]{2,1,0:T(8,128)(2,1)} %get-tuple-element.58), channel_id=1, source_target_pairs={{0,1},{1,0},{2,3},{3,2},{4,5},{5,4},{6,7},{7,6},{8,9},{9,8},{10,11... | collective-permute-start | bytes 3145736 | tf_op jit(solution)/shard_map/ppermute | solution.py:498
  54.7 5.6 %collective-permute-start.1 = (bf16[4,64,2048]{2,1,0:T(8,128)(2,1)}, bf16[4,64,2048]{2,1,0:T(8,128)(2,1)}, u32[]{:S(2)}, u32[]{:S(2)}) collective-permute-start(bf16[4,64,2048]{2,1,0:T(8,128)(2,1)} %get-tuple-element.61), channel_id=1, source_target_pairs={{0,1},{1,0},{2,3},{3,2},{4,5},{5,4},{6,7},{7,6},{8,9},{9,8},{10,11... | collective-permute-start | bytes 3145736 | tf_op jit(solution)/shard_map/ppermute | solution.py:498
  57.3 23.7 %collective-permute-start.2 = (bf16[64,2048]{1,0:T(8,128)(2,1)}, bf16[64,2048]{1,0:T(8,128)(2,1)S(1)}, u32[]{:S(2)}, u32[]{:S(2)}) collective-permute-start(bf16[64,2048]{1,0:T(8,128)(2,1)} %get-tuple-element.112), channel_id=1, source_target_pairs={{0,6},{1,7},{2,0},{3,1},{4,2},{5,3},{6,4},{7,5},{8,14},{9,15},{10,... | collective-permute-start | bytes 786440 | tf_op jit(solution)/shard_map/ppermute | solution.py:493
  60.3 10.4 %collective-permute-start.3 = (bf16[64,2048]{1,0:T(8,128)(2,1)S(1)}, bf16[64,2048]{1,0:T(8,128)(2,1)S(1)}, u32[]{:S(2)}, u32[]{:S(2)}) collective-permute-start(bf16[64,2048]{1,0:T(8,128)(2,1)S(1)} %get-tuple-element.111), channel_id=1, source_target_pairs={{0,2},{1,3},{2,4},{3,5},{4,6},{5,7},{6,0},{7,1},{8,10},{9,11},{10,... | collective-permute-start | bytes 786440 | tf_op jit(solution)/shard_map/ppermute | solution.py:488
  62.1 15.3 %copy-start.23 = (bf16[64,2,2048]{2,1,0:T(2,128)(2,1)S(1)}, bf16[64,2,2048]{2,1,0:T(2,128)(2,1)}, u32[]{:S(2)}) copy-start(bf16[64,2,2048]{2,1,0:T(2,128)(2,1)} %param.26) | copy-start | bytes 1572868
  62.1 15.2 %slice-start = ((s32[16,3]{0,1:T(4,128)}), s32[16,2]{0,1:T(2,128)S(1)}, s32[]{:S(2)}) async-start(s32[16,3]{0,1:T(4,128)} %copy-done.29), calls=%async_computation.4 | async-start | bytes 2048 | tf_op jit(solution)/shard_map/slice.1
  62.1 18.8 %collective-permute-start.5 = (bf16[64,2048]{1,0:T(8,128)(2,1)}, bf16[64,2048]{1,0:T(8,128)(2,1)}, u32[]{:S(2)}, u32[]{:S(2)}) collective-permute-start(bf16[64,2048]{1,0:T(8,128)(2,1)} %get-tuple-element.110), channel_id=1, source_target_pairs={{0,2},{1,3},{2,4},{3,5},{4,6},{5,7},{6,0},{7,1},{8,10},{9,11},{10,... | collective-permute-start | bytes 786440 | tf_op jit(solution)/shard_map/ppermute | solution.py:488
  62.8 9.1 %collective-permute-start.6 = (bf16[64,2048]{1,0:T(8,128)(2,1)S(1)}, bf16[64,2048]{1,0:T(8,128)(2,1)S(1)}, u32[]{:S(2)}, u32[]{:S(2)}) collective-permute-start(bf16[64,2048]{1,0:T(8,128)(2,1)S(1)} %get-tuple-element.109), channel_id=1, source_target_pairs={{0,6},{1,7},{2,0},{3,1},{4,2},{5,3},{6,4},{7,5},{8,14},{9,15},{10,... | collective-permute-start | bytes 786440 | tf_op jit(solution)/shard_map/ppermute | solution.py:493
  71.5 11.2 %copy-start.5 = (f32[2048]{0:T(1024)S(1)}, f32[2048]{0:T(1024)}, u32[]{:S(2)}) copy-start(f32[2048]{0:T(1024)} %param.27) | copy-start | bytes 24580
  71.5 9.5 %collective-permute-start.4 = (bf16[64,2048]{1,0:T(8,128)(2,1)}, bf16[64,2048]{1,0:T(8,128)(2,1)}, u32[]{:S(2)}, u32[]{:S(2)}) collective-permute-start(bf16[64,2048]{1,0:T(8,128)(2,1)} %fusion.1), channel_id=1, source_target_pairs={{0,2},{1,3},{2,4},{3,5},{4,6},{5,7},{6,0},{7,1},{8,10},{9,11},{10,... | collective-permute-start | bytes 786440 | tf_op jit(solution)/shard_map/ppermute | solution.py:488
  73.7 9.0 %collective-permute-start.7 = (bf16[64,2048]{1,0:T(8,128)(2,1)}, bf16[64,2048]{1,0:T(8,128)(2,1)}, u32[]{:S(2)}, u32[]{:S(2)}) collective-permute-start(bf16[64,2048]{1,0:T(8,128)(2,1)} %fusion), channel_id=1, source_target_pairs={{0,6},{1,7},{2,0},{3,1},{4,2},{5,3},{6,4},{7,5},{8,14},{9,15},{10,... | collective-permute-start | bytes 786440 | tf_op jit(solution)/shard_map/ppermute | solution.py:493
  83.7 26.2 %copy-start.7 = (bf16[1,2048,896]{2,1,0:T(8,128)(2,1)S(1)}, bf16[1,2048,896]{2,1,0:T(8,128)(2,1)}, u32[]{:S(2)}) copy-start(bf16[1,2048,896]{2,1,0:T(8,128)(2,1)} %param.29) | copy-start | bytes 11010052
  86.0 20.0 %copy-start.12 = (f32[128,2048]{1,0:T(8,128)}, f32[128,2048]{1,0:T(8,128)S(1)}, u32[]{:S(2)}) copy-start(f32[128,2048]{1,0:T(8,128)S(1)} %get-tuple-element.100.hidden) | copy-start | bytes 3145732
  86.0 24.0 %copy-start.6 = (bf16[1,2048,896]{2,1,0:T(8,128)(2,1)S(1)}, bf16[1,2048,896]{2,1,0:T(8,128)(2,1)}, u32[]{:S(2)}) copy-start(bf16[1,2048,896]{2,1,0:T(8,128)(2,1)} %param.28) | copy-start | bytes 11010052
  106.0 3.9 %collective-permute-start.10 = (bf16[256,2176]{1,0:T(8,128)(2,1)S(1)}, bf16[256,2176]{1,0:T(8,128)(2,1)S(1)}, u32[]{:S(2)}, u32[]{:S(2)}) collective-permute-start(bf16[256,2176]{1,0:T(8,128)(2,1)S(1)} %bitcast.81), channel_id=1, source_target_pairs={{0,1},{1,0},{2,3},{3,2},{4,5},{5,4},{6,7},{7,6},{8,9},{9,8},{10,11... | collective-permute-start | bytes 3342344 | tf_op jit(solution)/shard_map/ppermute | solution.py:498
  106.1 17.1 %collective-permute-start.8 = (bf16[128,2176]{1,0:T(8,128)(2,1)S(1)}, bf16[128,2176]{1,0:T(8,128)(2,1)S(1)}, u32[]{:S(2)}, u32[]{:S(2)}) collective-permute-start(bf16[128,2176]{1,0:T(8,128)(2,1)S(1)} %bitcast.118), channel_id=1, source_target_pairs={{0,2},{1,3},{2,4},{3,5},{4,6},{5,7},{6,0},{7,1},{8,10},{9,11},{10,... | collective-permute-start | bytes 1671176 | tf_op jit(solution)/shard_map/ppermute | solution.py:488
  106.2 17.0 %collective-permute-start.9 = (bf16[128,2176]{1,0:T(8,128)(2,1)S(1)}, bf16[128,2176]{1,0:T(8,128)(2,1)S(1)}, u32[]{:S(2)}, u32[]{:S(2)}) collective-permute-start(bf16[128,2176]{1,0:T(8,128)(2,1)S(1)} %bitcast.116), channel_id=1, source_target_pairs={{0,6},{1,7},{2,0},{3,1},{4,2},{5,3},{6,4},{7,5},{8,14},{9,15},{10,... | collective-permute-start | bytes 1671176 | tf_op jit(solution)/shard_map/ppermute | solution.py:493
  123.1 3.8 %collective-permute-start.14 = (bf16[128,2176]{1,0:T(8,128)(2,1)S(1)}, bf16[128,2176]{1,0:T(8,128)(2,1)S(1)}, u32[]{:S(2)}, u32[]{:S(2)}) collective-permute-start(bf16[128,2176]{1,0:T(8,128)(2,1)S(1)} %collective-permute-done.8.refs_0_), channel_id=1, source_target_pairs={{0,1},{1,0},{2,3},{3,2},{4,5},{5,4},{6,7},{7,6},{8,9},{9,8},{10,11... | collective-permute-start | bytes 1671176 | tf_op jit(solution)/shard_map/ppermute | solution.py:498
  123.1 3.8 %collective-permute-start.15 = (bf16[128,2176]{1,0:T(8,128)(2,1)S(1)}, bf16[128,2176]{1,0:T(8,128)(2,1)S(1)}, u32[]{:S(2)}, u32[]{:S(2)}) collective-permute-start(bf16[128,2176]{1,0:T(8,128)(2,1)S(1)} %collective-permute-done.9.refs_1_), channel_id=1, source_target_pairs={{0,1},{1,0},{2,3},{3,2},{4,5},{5,4},{6,7},{7,6},{8,9},{9,8},{10,11... | collective-permute-start | bytes 1671176 | tf_op jit(solution)/shard_map/ppermute | solution.py:498
  123.7 16.3 %collective-permute-start.13 = (bf16[256,2176]{1,0:T(8,128)(2,1)S(1)}, bf16[256,2176]{1,0:T(8,128)(2,1)S(1)}, u32[]{:S(2)}, u32[]{:S(2)}) collective-permute-start(bf16[256,2176]{1,0:T(8,128)(2,1)S(1)} %get-tuple-element.68), channel_id=1, source_target_pairs={{0,1},{1,0},{2,3},{3,2},{4,5},{5,4},{6,7},{7,6},{8,9},{9,8},{10,11... | collective-permute-start | bytes 3342344 | tf_op jit(solution)/shard_map/ppermute | solution.py:498
  123.7 16.3 %collective-permute-start.11 = (bf16[128,2176]{1,0:T(8,128)(2,1)S(1)}, bf16[128,2176]{1,0:T(8,128)(2,1)S(1)}, u32[]{:S(2)}, u32[]{:S(2)}) collective-permute-start(bf16[128,2176]{1,0:T(8,128)(2,1)S(1)} %collective-permute-done.8.refs_0_), channel_id=1, source_target_pairs={{0,2},{1,3},{2,4},{3,5},{4,6},{5,7},{6,0},{7,1},{8,10},{9,11},{10,... | collective-permute-start | bytes 1671176 | tf_op jit(solution)/shard_map/ppermute | solution.py:488
  124.8 15.2 %collective-permute-start.12 = (bf16[128,2176]{1,0:T(8,128)(2,1)S(1)}, bf16[128,2176]{1,0:T(8,128)(2,1)S(1)}, u32[]{:S(2)}, u32[]{:S(2)}) collective-permute-start(bf16[128,2176]{1,0:T(8,128)(2,1)S(1)} %collective-permute-done.9.refs_1_), channel_id=1, source_target_pairs={{0,6},{1,7},{2,0},{3,1},{4,2},{5,3},{6,4},{7,5},{8,14},{9,15},{10,... | collective-permute-start | bytes 1671176 | tf_op jit(solution)/shard_map/ppermute | solution.py:493
  126.9 18.8 %copy-start.9 = (bf16[1,896,2048]{2,1,0:T(8,128)(2,1)S(1)}, bf16[1,896,2048]{2,1,0:T(8,128)(2,1)}, u32[]{:S(2)}) copy-start(bf16[1,896,2048]{2,1,0:T(8,128)(2,1)} %param.30) | copy-start | bytes 11010052
  140.0 3.5 %collective-permute-start.18 = (bf16[256,2176]{1,0:T(8,128)(2,1)S(1)}, bf16[256,2176]{1,0:T(8,128)(2,1)S(1)}, u32[]{:S(2)}, u32[]{:S(2)}) collective-permute-start(bf16[256,2176]{1,0:T(8,128)(2,1)S(1)} %get-tuple-element.75), channel_id=1, source_target_pairs={{0,1},{1,0},{2,3},{3,2},{4,5},{5,4},{6,7},{7,6},{8,9},{9,8},{10,11... | collective-permute-start | bytes 3342344 | tf_op jit(solution)/shard_map/ppermute | solution.py:498
  140.0 15.5 %collective-permute-start.16 = (bf16[128,2176]{1,0:T(8,128)(2,1)S(1)}, bf16[128,2176]{1,0:T(8,128)(2,1)S(1)}, u32[]{:S(2)}, u32[]{:S(2)}) collective-permute-start(bf16[128,2176]{1,0:T(8,128)(2,1)S(1)} %bitcast.119), channel_id=1, source_target_pairs={{0,6},{1,7},{2,0},{3,1},{4,2},{5,3},{6,4},{7,5},{8,14},{9,15},{10,... | collective-permute-start | bytes 1671176 | tf_op jit(solution)/shard_map/ppermute | solution.py:493
  142.9 16.0 %collective-permute-start.17 = (bf16[128,2176]{1,0:T(8,128)(2,1)S(1)}, bf16[128,2176]{1,0:T(8,128)(2,1)S(1)}, u32[]{:S(2)}, u32[]{:S(2)}) collective-permute-start(bf16[128,2176]{1,0:T(8,128)(2,1)S(1)} %bitcast.117), channel_id=1, source_target_pairs={{0,2},{1,3},{2,4},{3,5},{4,6},{5,7},{6,0},{7,1},{8,10},{9,11},{10,... | collective-permute-start | bytes 1671176 | tf_op jit(solution)/shard_map/ppermute | solution.py:488
  143.0 2.0 collective-permute-start.19
  143.2 2.5 %collective-permute-start.20 = (bf16[128,2176]{1,0:T(8,128)(2,1)S(1)}, bf16[128,2176]{1,0:T(8,128)(2,1)S(1)}, u32[]{:S(2)}, u32[]{:S(2)}) collective-permute-start(bf16[128,2176]{1,0:T(8,128)(2,1)S(1)} %collective-permute-done.12.refs_1_), channel_id=1, source_target_pairs={{0,1},{1,0},{2,3},{3,2},{4,5},{5,4},{6,7},{7,6},{8,9},{9,8},{10,11... | collective-permute-start | bytes 1671176 | tf_op jit(solution)/shard_map/ppermute | solution.py:498
  158.9 2.8 %collective-permute-start.21 = (bf16[256,2176]{1,0:T(8,128)(2,1)S(1)}, bf16[256,2176]{1,0:T(8,128)(2,1)S(1)}, u32[]{:S(2)}, u32[]{:S(2)}) collective-permute-start(bf16[256,2176]{1,0:T(8,128)(2,1)S(1)} %get-tuple-element.83), channel_id=1, source_target_pairs={{0,1},{1,0},{2,3},{3,2},{4,5},{5,4},{6,7},{7,6},{8,9},{9,8},{10,11... | collective-permute-start | bytes 3342344 | tf_op jit(solution)/shard_map/ppermute | solution.py:498
  158.9 15.9 %collective-permute-start.24 = (bf16[128,2176]{1,0:T(8,128)(2,1)S(1)}, bf16[128,2176]{1,0:T(8,128)(2,1)S(1)}, u32[]{:S(2)}, u32[]{:S(2)}) collective-permute-start(bf16[128,2176]{1,0:T(8,128)(2,1)S(1)} %get-tuple-element.88), channel_id=1, source_target_pairs={{0,6},{1,7},{2,0},{3,1},{4,2},{5,3},{6,4},{7,5},{8,14},{9,15},{10,... | collective-permute-start | bytes 1671176 | tf_op jit(solution)/shard_map/ppermute | solution.py:493
  159.2 16.7 %collective-permute-start.25 = (bf16[128,2176]{1,0:T(8,128)(2,1)S(1)}, bf16[128,2176]{1,0:T(8,128)(2,1)S(1)}, u32[]{:S(2)}, u32[]{:S(2)}) collective-permute-start(bf16[128,2176]{1,0:T(8,128)(2,1)S(1)} %get-tuple-element.89), channel_id=1, source_target_pairs={{0,2},{1,3},{2,4},{3,5},{4,6},{5,7},{6,0},{7,1},{8,10},{9,11},{10,... | collective-permute-start | bytes 1671176 | tf_op jit(solution)/shard_map/ppermute | solution.py:488
  160.9 2.0 collective-permute-start.26
  161.0 4.3 %collective-permute-start.27 = (bf16[128,2176]{1,0:T(8,128)(2,1)S(1)}, bf16[128,2176]{1,0:T(8,128)(2,1)S(1)}, u32[]{:S(2)}, u32[]{:S(2)}) collective-permute-start(bf16[128,2176]{1,0:T(8,128)(2,1)S(1)} %collective-permute-done.17.refs_1_), channel_id=1, source_target_pairs={{0,1},{1,0},{2,3},{3,2},{4,5},{5,4},{6,7},{7,6},{8,9},{9,8},{10,11... | collective-permute-start | bytes 1671176 | tf_op jit(solution)/shard_map/ppermute | solution.py:498
  161.9 25.2 %collective-permute-start.22 = (bf16[128,2176]{1,0:T(8,128)(2,1)S(1)}, bf16[128,2176]{1,0:T(8,128)(2,1)S(1)}, u32[]{:S(2)}, u32[]{:S(2)}) collective-permute-start(bf16[128,2176]{1,0:T(8,128)(2,1)S(1)} %get-tuple-element.86), channel_id=1, source_target_pairs={{0,2},{1,3},{2,4},{3,5},{4,6},{5,7},{6,0},{7,1},{8,10},{9,11},{10,... | collective-permute-start | bytes 1671176 | tf_op jit(solution)/shard_map/ppermute | solution.py:488
  162.9 24.2 %collective-permute-start.23 = (bf16[128,2176]{1,0:T(8,128)(2,1)S(1)}, bf16[128,2176]{1,0:T(8,128)(2,1)S(1)}, u32[]{:S(2)}, u32[]{:S(2)}) collective-permute-start(bf16[128,2176]{1,0:T(8,128)(2,1)S(1)} %get-tuple-element.87), channel_id=1, source_target_pairs={{0,6},{1,7},{2,0},{3,1},{4,2},{5,3},{6,4},{7,5},{8,14},{9,15},{10,... | collective-permute-start | bytes 1671176 | tf_op jit(solution)/shard_map/ppermute | solution.py:493
  187.1 2.8 %collective-permute-start.28 = (bf16[256,2176]{1,0:T(8,128)(2,1)S(1)}, bf16[256,2176]{1,0:T(8,128)(2,1)S(1)}, u32[]{:S(2)}, u32[]{:S(2)}) collective-permute-start(bf16[256,2176]{1,0:T(8,128)(2,1)S(1)} %get-tuple-element.96), channel_id=1, source_target_pairs={{0,1},{1,0},{2,3},{3,2},{4,5},{5,4},{6,7},{7,6},{8,9},{9,8},{10,11... | collective-permute-start | bytes 3342344 | tf_op jit(solution)/shard_map/ppermute | solution.py:498
  190.3 15.9 %collective-permute-start.29 = (bf16[128,2176]{1,0:T(8,128)(2,1)S(1)}, bf16[128,2176]{1,0:T(8,128)(2,1)S(1)}, u32[]{:S(2)}, u32[]{:S(2)}) collective-permute-start(bf16[128,2176]{1,0:T(8,128)(2,1)S(1)} %get-tuple-element.103), channel_id=1, source_target_pairs={{0,2},{1,3},{2,4},{3,5},{4,6},{5,7},{6,0},{7,1},{8,10},{9,11},{10,... | collective-permute-start | bytes 1671176 | tf_op jit(solution)/shard_map/ppermute | solution.py:488
  190.9 15.3 %collective-permute-start.30 = (bf16[128,2176]{1,0:T(8,128)(2,1)S(1)}, bf16[128,2176]{1,0:T(8,128)(2,1)S(1)}, u32[]{:S(2)}, u32[]{:S(2)}) collective-permute-start(bf16[128,2176]{1,0:T(8,128)(2,1)S(1)} %get-tuple-element.104), channel_id=1, source_target_pairs={{0,6},{1,7},{2,0},{3,1},{4,2},{5,3},{6,4},{7,5},{8,14},{9,15},{10,... | collective-permute-start | bytes 1671176 | tf_op jit(solution)/shard_map/ppermute | solution.py:493
  207.9 21.9 %copy-start.13 = (f32[128,2048]{1,0:T(8,128)S(1)}, f32[128,2048]{1,0:T(8,128)}, u32[]{:S(2)}) copy-start(f32[128,2048]{1,0:T(8,128)} %copy-done.12) | copy-start | bytes 3145732
  207.9 21.9 %copy-start.14 = (f32[4,2048]{1,0:T(4,128)S(1)}, f32[4,2048]{1,0:T(4,128)}, u32[]{:S(2)}) copy-start(f32[4,2048]{1,0:T(4,128)} %directions.1) | copy-start | bytes 98308
  207.9 21.9 %all-to-all-start.3 = ((bf16[16,16,2176]{2,1,0:T(8,128)(2,1)}), bf16[16,16,2176]{2,1,0:T(8,128)(2,1)S(1)}, u32[]{:S(2)}, u32[]{:S(2)}) async-start(bf16[16,16,2176]{2,1,0:T(8,128)(2,1)} %bitcast.29), calls=%async_computation.3 | async-start | bytes 2228224 | tf_op jit(solution)/shard_map/all_to_all | solution.py:646
  (19 other events, 54.0 us)
where the time goes:
time: 234 us; the launch traced here: 233 us
  waiting for transfers between devices  72.7 us (31%)
  Pallas kernels  65.4 us (28%)
  starting transfers between devices  45.8 us (20%)
  blocking collectives  20 us (9%)
  local copies, waits for them, and re-layouts  19 us (8%)
  other arithmetic  9.44 us (4%)
    ppermute x9, waiting for transfers between devices, from_before(): lax.ppermute(values, 'exp', [(i, (i + 2) % size) for i in range(size)])  38.7 us
    pallas_call x4, Pallas kernels, expert_call(): pl.pallas_call(functools.partial(expert_kernel, counts), in_specs=[anywhe...  38.2 us
    ppermute x9, starting transfers between devices, from_after(): lax.ppermute(values, 'exp', [(i, (i - 2) % size) for i in range(size)])  23.5 us
    all_to_all x1, blocking collectives, on_device(): lax.all_to_all(packed.reshape(experts, FOLD, D + 128), 'seq', split_axis=...  20 us
    all_to_all x1, waiting for transfers between devices, on_device(): lax.all_to_all(summed.reshape(experts, FOLD, D + 128), 'seq', split_axis=...  18 us
    unnamed x68, local copies, waits for them, and re-layouts  14.1 us
    pallas_call x2, Pallas kernels, mixer_call(): pl.pallas_call(mixer_kernel, grid=(blocks,), in_specs=[pl.BlockSpec(memor...  9.85 us
    all_to_all x1, starting transfers between devices, on_device(): lax.all_to_all(parcel, 'seq', split_axis=0, concat_axis=0, tiled=True)  8.14 us
  transfers between devices with their start and end apart: 34, of which 18 were waited for; matrix products, arithmetic and copies ran while one was open for 5% of the time, Pallas kernels for 21%

commit v1 on v0

--- a/solution.py
+++ b/solution.py
@@ -117,7 +117,7 @@
         ],
         scratch_shapes=[pltpu.VMEM((heads, STATE), F32), pltpu.VMEM((width, STATE), F32)],
         compiler_params=pltpu.CompilerParams(
-            dimension_semantics=("arbitrary", "arbitrary"), vmem_limit_bytes=28 * 2**20
+            dimension_semantics=("arbitrary", "arbitrary"), vmem_limit_bytes=16 * 2**20
         ),
         cost_estimate=pl.CostEstimate(flops=10**9, bytes_accessed=2 * 2**20, transcendentals=8192),
         name="contrib",
@@ -170,7 +170,7 @@
         out_specs=pl.BlockSpec((1, BLOCK, width), lambda c: (0, c, 0)),
         out_shape=jax.ShapeDtypeStruct((1, length, width), F32),
         compiler_params=pltpu.CompilerParams(
-            dimension_semantics=("arbitrary",), vmem_limit_bytes=28 * 2**20
+            dimension_semantics=("arbitrary",), vmem_limit_bytes=16 * 2**20
         ),
         cost_estimate=pl.CostEstimate(
             flops=3 * 10**9, bytes_accessed=2 * 2**20, transcendentals=2**20
@@ -280,7 +280,7 @@
             pltpu.SemaphoreType.DMA((blocks, columns // blocks)),
         ],
         compiler_params=pltpu.CompilerParams(
-            dimension_semantics=("arbitrary",), vmem_limit_bytes=28 * 2**20
+            dimension_semantics=("arbitrary",), vmem_limit_bytes=16 * 2**20
         ),
         cost_estimate=pl.CostEstimate(
             flops=2 * 10**9, bytes_accessed=6 * 2**20, transcendentals=2**18
@@ -439,9 +439,9 @@
         open_units(whole, units - whole)
     half = kept.shape[0]
 
-    @pl.loop(0, D // 256)
+    @pl.loop(0, D // 1024)
     def _(index):
-        span = pl.ds(pl.multiple_of(index * 256, 256), 256)
+        span = pl.ds(pl.multiple_of(index * 1024, 1024), 1024)
         result = jnp.dot(hidden[...], down[:, span], preferred_element_type=F32)
         kept[:, span] = result[:half].astype(BF16)
         passed[:, span] = result[half:count].astype(BF16)
@@ -483,6 +483,26 @@
     )(*parts, gate, up, down)
 
 
+def settle_kernel(kept, got, top_after, top_before, bottom_before, bottom_after, out):
+    half = top_after.shape[0]
+    for index, others in enumerate(((top_after, top_before), (bottom_before, bottom_after))):
+        span = pl.ds(index * half, half)
+        total = kept[span, :].astype(F32) + got[span, :].astype(F32)
+        for other in others:
+            total = total + other[...].astype(F32)
+        out[span, :] = total.astype(BF16)
+
+
+def settle_call(*arrays):
+    return pl.pallas_call(
+        settle_kernel,
+        out_shape=jax.ShapeDtypeStruct(arrays[0].shape, BF16),
+        compiler_params=pltpu.CompilerParams(vmem_limit_bytes=16 * 2**20),
+        cost_estimate=pl.CostEstimate(flops=2 * 10**6, bytes_accessed=5 * 2**20, transcendentals=0),
+        name="settle",
+    )(*arrays)
+
+
 def from_before(values):
     size = lax.axis_size("exp")
     return lax.ppermute(values, "exp", [(i, (i + 2) % size) for i in range(size)])
@@ -549,18 +569,12 @@
     relay_top = from_before(far_top)
     relay_bottom = from_after(far_bottom)
     kept, passed = call((after_top, before_bottom, *late))
-    relay_top, relay_bottom, top_after, bottom_before, kept, passed = after(
-        (relay_top, relay_bottom, top_after, bottom_before, kept, passed)
-    )
+    relay_top, relay_bottom, kept, passed = after((relay_top, relay_bottom, kept, passed))
     got = from_sibling(passed)
     top_before = from_before(add_up(kept[:half], got[:half], relay_top))
     bottom_after = from_after(add_up(kept[half:], got[half:], relay_bottom))
-    return jnp.concatenate(
-        [
-            add_up(kept_own[:half], got_own[:half], top_after, top_before),
-            add_up(kept_own[half:], got_own[half:], bottom_before, bottom_after),
-        ],
-        axis=0,
+    return settle_call(
+        kept_own, got_own, top_after, top_before, bottom_before, bottom_after
     )
 
 
@@ -611,7 +625,7 @@
         0, place, *shared, within_early, gating, norm_gain[None, :], w_out, columns
     )
     got = from_sibling(passed)
-    (gating,) = after((gating,), kept)
+    (place,) = after((place,), kept)
     kept_late, passed = mixer_call(
         1, place, *shared, within_late, gating, norm_gain[None, :], w_out, columns
     )

time: 234 us -> 236 us (level)
  waiting for transfers between devices: 72.7 us -> 77.8 us
  Pallas kernels: 65.4 us -> 62.6 us
    ppermute x9, waiting for transfers between devices: 2.3 us -> 12.5 us  [from_after(): lax.ppermute(values, 'exp', [(i, (i - 2) % size) for i in range(size)])]
    pallas_call x4, Pallas kernels: 38.2 us -> 33.8 us  [expert_call(): pl.pallas_call(functools.partial(expert_kernel, counts), in_specs=[anywhe...]
    ppermute x9, starting transfers between devices: 23.5 us -> 27.7 us  [from_after(): lax.ppermute(values, 'exp', [(i, (i - 2) % size) for i in range(size)])]
    ppermute x9, waiting for transfers between devices: 38.7 us -> 35.1 us  [from_before(): lax.ppermute(values, 'exp', [(i, (i + 2) % size) for i in range(size)])]
    convert_element_type x8 -> x7, other arithmetic: 6.74 us -> 6.18 us  [add_up(): return total.astype(BF16)]
    unnamed x68 -> x66, local copies, waits for them, and re-layouts: 14.1 us -> 14.1 us
  transfers between devices with their start and end apart: 34 -> 34, of which waited for: 18 -> 17; matrix products, arithmetic and copies ran while one was open for 5% -> 5% of each run, Pallas kernels for 21% -> 19%
where the time goes in v1:
time: 236 us; the launch traced here: 235 us
  waiting for transfers between devices  77.8 us (33%)
  Pallas kernels  62.6 us (27%)
  starting transfers between devices  47.7 us (20%)
  blocking collectives  20 us (8%)
  local copies, waits for them, and re-layouts  19 us (8%)
  other arithmetic  7.79 us (3%)
    ppermute x9, waiting for transfers between devices, from_before(): lax.ppermute(values, 'exp', [(i, (i + 2) % size) for i in range(size)])  35.1 us
    pallas_call x4, Pallas kernels, expert_call(): pl.pallas_call(functools.partial(expert_kernel, counts), in_specs=[anywhe...  33.8 us
    ppermute x9, starting transfers between devices, from_after(): lax.ppermute(values, 'exp', [(i, (i - 2) % size) for i in range(size)])  27.7 us
    all_to_all x1, blocking collectives, on_device(): lax.all_to_all(packed.reshape(experts, FOLD, D + 128), 'seq', split_axis=...  20 us
    all_to_all x1, waiting for transfers between devices, on_device(): lax.all_to_all(summed.reshape(experts, FOLD, D + 128), 'seq', split_axis=...  18.1 us
    unnamed x66, local copies, waits for them, and re-layouts  14.1 us
    ppermute x9, waiting for transfers between devices, from_after(): lax.ppermute(values, 'exp', [(i, (i - 2) % size) for i in range(size)])  12.5 us
    pallas_call x2, Pallas kernels, mixer_call(): pl.pallas_call(mixer_kernel, grid=(blocks,), in_specs=[pl.BlockSpec(memor...  9.84 us
  transfers between devices with their start and end apart: 34, of which 17 were waited for; matrix products, arithmetic and copies ran while one was open for 5% of the time, Pallas kernels for 19%

profile of v1, /device:TPU:0, one launch (start us, length us, event | category | flops | bytes accessed | tf_op | source)
XLA Modules:
  0.0 235.4 jit_solution(1493115844299336143)
XLA Ops:
  0.0 1.4 copy.55
  1.6 5.8 %contrib.1 = (bf16[16,72,128]{2,1,0:T(8,128)(2,1)}, f32[2,512,128]{2,1,0:T(8,128)S(1)}) custom-call(f32[2,8,512]{2,1,0:T(8,128)S(1)} %get-tuple-element.112.decay, f32[2,8,512]{2,1,0:T(8,128)S(1)} %get-tuple-element.111.step, bf16[2,512,512]{2,1,0:T(8,128)(2,1)S(1)} %bitcast.88, bf16[2,512,128]{2,1,0:T(8,128)(2,1)S(1)} %bitcast.96), custom_call_target="tpu_custom_call" | custom-call | flops 1000000000 | bytes 2097152 | tf_op jit(solution)/shard_map/contrib/pallas_call | solution.py:101
  7.4 8.1 %all-to-all-start = ((bf16[16,72,128]{2,1,0:T(8,128)(2,1)}), bf16[16,72,128]{2,1,0:T(8,128)(2,1)}, u32[]{:S(2)}, u32[]{:S(2)}) async-start(bf16[16,72,128]{2,1,0:T(8,128)(2,1)} %get-tuple-element.51), calls=%async_computation | async-start | bytes 589824 | tf_op jit(solution)/shard_map/all_to_all | solution.py:612
  15.7 1.4 copy.54
  17.1 3.0 %within.2 = f32[1,512,512]{2,1,0:T(8,128)S(1)} custom-call(f32[2,8,512]{2,1,0:T(8,128)S(1)} %get-tuple-element.112.decay, f32[2,8,512]{2,1,0:T(8,128)S(1)} %get-tuple-element.111.step, bf16[2,512,512]{2,1,0:T(8,128)(2,1)S(1)} %bitcast.89, bf16[2,512,128]{2,1,0:T(8,128)(2,1)S(1)} %bitcast.97, bf16[2,512,128]{2,1,0:T(8,128)(2,1)S(1)} %bitcast.92, ...), custom_call_target="tpu_custom_call" | custom-call | flops 3000000000 | bytes 2097152 | tf_op jit(solution)/shard_map/within/pallas_call | solution.py:159
  21.1 3.3 %all-to-all-done.parcels = bf16[16,72,128]{2,1,0:T(8,128)(2,1)} async-done(((bf16[16,72,128]{2,1,0:T(8,128)(2,1)}), bf16[16,72,128]{2,1,0:T(8,128)(2,1)}, u32[]{:S(2)}, u32[]{:S(2)}) %all-to-all-start) | async-done | bytes 294944 | tf_op jit(solution)/shard_map/all_to_all | solution.py:612
  24.4 1.7 scan.1
  26.1 3.9 %all-to-all-start.1 = ((bf16[16,64,128]{2,1,0:T(8,128)(2,1)}), bf16[16,64,128]{2,1,0:T(8,128)(2,1)S(1)}, u32[]{:S(2)}, u32[]{:S(2)}) async-start(bf16[16,64,128]{2,1,0:T(8,128)(2,1)} %scan.1), calls=%async_computation.1 | async-start | bytes 524288 | tf_op jit(solution)/shard_map/all_to_all | solution.py:616
  30.0 3.0 %within.3 = f32[1,512,512]{2,1,0:T(8,128)S(1)} custom-call(f32[2,8,512]{2,1,0:T(8,128)S(1)} %get-tuple-element.112.decay, f32[2,8,512]{2,1,0:T(8,128)S(1)} %get-tuple-element.111.step, bf16[2,512,512]{2,1,0:T(8,128)(2,1)S(1)} %bitcast.90, bf16[2,512,128]{2,1,0:T(8,128)(2,1)S(1)} %bitcast.98, bf16[2,512,128]{2,1,0:T(8,128)(2,1)S(1)} %bitcast.93, ...), custom_call_target="tpu_custom_call" | custom-call | flops 3000000000 | bytes 2097152 | tf_op jit(solution)/shard_map/within/pallas_call | solution.py:159
  34.0 4.5 %all-to-all-done.1.entering = bf16[16,64,128]{2,1,0:T(8,128)(2,1)S(1)} async-done(((bf16[16,64,128]{2,1,0:T(8,128)(2,1)}), bf16[16,64,128]{2,1,0:T(8,128)(2,1)S(1)}, u32[]{:S(2)}, u32[]{:S(2)}) %all-to-all-start.1) | async-done | bytes 262176 | tf_op jit(solution)/shard_map/all_to_all | solution.py:616
  38.5 1.7 copy-done.9
  40.2 1.2 copy-done.18
  42.5 4.9 %mixer.2 = (bf16[4,64,2048]{2,1,0:T(8,128)(2,1)S(1)}, bf16[4,64,2048]{2,1,0:T(8,128)(2,1)}) custom-call(s32[1]{0:T(128)} %bitcast.8.place, f32[2,8,512]{2,1,0:T(8,128)S(1)} %get-tuple-element.112.decay, bf16[2,512,128]{2,1,0:T(8,128)(2,1)S(1)} %bitcast.94, bf16[16,64,128]{2,1,0:T(8,128)(2,1)S(1)} %all-to-all-done.1.entering, f32[2,512,128]{2,1,0:T(8,128)S(1)} %copy-done.20, ...), custom_call_target="tpu_custom_call" | custom-call | flops 2000000000 | bytes 6291456 | tf_op jit(solution)/shard_map/mixer/pallas_call | solution.py:262
  49.7 4.9 %mixer.3 = (bf16[4,64,2048]{2,1,0:T(8,128)(2,1)S(1)}, bf16[4,64,2048]{2,1,0:T(8,128)(2,1)}) custom-call(s32[1]{0:T(128)} %bitcast.8.place, f32[2,8,512]{2,1,0:T(8,128)S(1)} %get-tuple-element.112.decay, bf16[2,512,128]{2,1,0:T(8,128)(2,1)S(1)} %bitcast.95, bf16[16,64,128]{2,1,0:T(8,128)(2,1)S(1)} %copy-done.4, f32[2,512,128]{2,1,0:T(8,128)S(1)} %copy-done.21, ...), custom_call_target="tpu_custom_call" | custom-call | flops 2000000000 | bytes 6291456 | tf_op jit(solution)/shard_map/mixer/pallas_call | solution.py:262
  57.3 3.0 %collective-permute-start.2 = (bf16[64,2048]{1,0:T(8,128)(2,1)}, bf16[64,2048]{1,0:T(8,128)(2,1)S(1)}, u32[]{:S(2)}, u32[]{:S(2)}) collective-permute-start(bf16[64,2048]{1,0:T(8,128)(2,1)} %get-tuple-element.106), channel_id=1, source_target_pairs={{0,6},{1,7},{2,0},{3,1},{4,2},{5,3},{6,4},{7,5},{8,14},{9,15},{10,... | collective-permute-start | bytes 786440 | tf_op jit(solution)/shard_map/ppermute | solution.py:513
  60.3 1.9 fusion.5
  62.8 2.7 %collective-permute-start.6 = (bf16[64,2048]{1,0:T(8,128)(2,1)S(1)}, bf16[64,2048]{1,0:T(8,128)(2,1)S(1)}, u32[]{:S(2)}, u32[]{:S(2)}) collective-permute-start(bf16[64,2048]{1,0:T(8,128)(2,1)S(1)} %get-tuple-element.103), channel_id=1, source_target_pairs={{0,6},{1,7},{2,0},{3,1},{4,2},{5,3},{6,4},{7,5},{8,14},{9,15},{10,... | collective-permute-start | bytes 786440 | tf_op jit(solution)/shard_map/ppermute | solution.py:513
  65.5 5.2 %collective-permute-done.3 = bf16[64,2048]{1,0:T(8,128)(2,1)S(1)} collective-permute-done((bf16[64,2048]{1,0:T(8,128)(2,1)S(1)}, bf16[64,2048]{1,0:T(8,128)(2,1)S(1)}, u32[]{:S(2)}, u32[]{:S(2)}) %collective-permute-start.3) | collective-permute-done | bytes 262176 | tf_op jit(solution)/shard_map/ppermute | solution.py:508
  71.9 1.8 fusion
  73.7 3.7 %collective-permute-start.7 = (bf16[64,2048]{1,0:T(8,128)(2,1)}, bf16[64,2048]{1,0:T(8,128)(2,1)}, u32[]{:S(2)}, u32[]{:S(2)}) collective-permute-start(bf16[64,2048]{1,0:T(8,128)(2,1)} %fusion), channel_id=1, source_target_pairs={{0,6},{1,7},{2,0},{3,1},{4,2},{5,3},{6,4},{7,5},{8,14},{9,15},{10,... | collective-permute-start | bytes 786440 | tf_op jit(solution)/shard_map/ppermute | solution.py:513
  81.0 1.6 collective-permute-done.7.refs_3_
  83.7 2.2 dispatch.1
  85.9 20.0 %all_to_all.20 = bf16[16,16,2176]{2,1,0:T(8,128)(2,1)S(1)} all-to-all(bf16[16,16,2176]{2,1,0:T(8,128)(2,1)S(1)} %bitcast.85), channel_id=1, replica_groups=mesh['seq'=16,'exp'=8] {'seq'}, dimensions={0} | all-to-all | bytes 2228224 | tf_op jit(solution)/shard_map/all_to_all | solution.py:656
  106.1 3.8 %collective-permute-start.9 = (bf16[128,2176]{1,0:T(8,128)(2,1)S(1)}, bf16[128,2176]{1,0:T(8,128)(2,1)S(1)}, u32[]{:S(2)}, u32[]{:S(2)}) collective-permute-start(bf16[128,2176]{1,0:T(8,128)(2,1)S(1)} %bitcast.116), channel_id=1, source_target_pairs={{0,6},{1,7},{2,0},{3,1},{4,2},{5,3},{6,4},{7,5},{8,14},{9,15},{10,... | collective-permute-start | bytes 1671176 | tf_op jit(solution)/shard_map/ppermute | solution.py:513
  109.9 2.0 copy-done.8
  111.9 8.4 %expert.4 = (bf16[256,2176]{1,0:T(8,128)(2,1)S(1)}, bf16[256,2176]{1,0:T(8,128)(2,1)S(1)}) custom-call(bf16[256,2176]{1,0:T(8,128)(2,1)S(1)} %bitcast.82, bf16[256,2176]{1,0:T(8,128)(2,1)S(1)} %collective-permute-done.10.refs_1_, bf16[2048,896]{1,0:T(8,128)(2,1)S(1)} %bitcast.102, bf16[2048,896]{1,0:T(8,128)(2,1)S(1)} %bitcast.106, ...), custom_call_target="tpu_custom_call" | custom-call | flops 5989466112 | bytes 15466496 | tf_op jit(solution)/shard_map/expert/pallas_call | solution.py:462
  120.3 2.7 %collective-permute-done.8.refs_0_ = bf16[128,2176]{1,0:T(8,128)(2,1)S(1)} collective-permute-done((bf16[128,2176]{1,0:T(8,128)(2,1)S(1)}, bf16[128,2176]{1,0:T(8,128)(2,1)S(1)}, u32[]{:S(2)}, u32[]{:S(2)}) %collective-permute-start.8) | collective-permute-done | bytes 557088 | tf_op jit(solution)/shard_map/ppermute | solution.py:508
  124.7 2.1 collective-permute-start.12
  126.8 8.4 %expert.5 = (bf16[256,2176]{1,0:T(8,128)(2,1)S(1)}, bf16[256,2176]{1,0:T(8,128)(2,1)S(1)}) custom-call(bf16[128,2176]{1,0:T(8,128)(2,1)S(1)} %collective-permute-done.8.refs_0_, bf16[128,2176]{1,0:T(8,128)(2,1)S(1)} %collective-permute-done.9.refs_1_, bf16[128,2176]{1,0:T(8,128)(2,1)S(1)} %collective-permute-done.14.refs_2_, ...), custom_call_target="tpu_custom_call" | custom-call | flops 5989466112 | bytes 15466496 | tf_op jit(solution)/shard_map/expert/pallas_call | solution.py:462
  135.3 4.6 %collective-permute-done.11.refs_0_ = bf16[128,2176]{1,0:T(8,128)(2,1)S(1)} collective-permute-done((bf16[128,2176]{1,0:T(8,128)(2,1)S(1)}, bf16[128,2176]{1,0:T(8,128)(2,1)S(1)}, u32[]{:S(2)}, u32[]{:S(2)}) %collective-permute-start.11) | collective-permute-done | bytes 557088 | tf_op jit(solution)/shard_map/ppermute | solution.py:508
  139.9 2.9 %collective-permute-start.18 = (bf16[128,2176]{1,0:T(8,128)(2,1)S(1)}, bf16[128,2176]{1,0:T(8,128)(2,1)S(1)}, u32[]{:S(2)}, u32[]{:S(2)}) collective-permute-start(bf16[128,2176]{1,0:T(8,128)(2,1)S(1)} %bitcast.119), channel_id=1, source_target_pairs={{0,6},{1,7},{2,0},{3,1},{4,2},{5,3},{6,4},{7,5},{8,14},{9,15},{10,... | collective-permute-start | bytes 1671176 | tf_op jit(solution)/shard_map/ppermute | solution.py:513
  145.6 8.4 %expert.6 = (bf16[256,2176]{1,0:T(8,128)(2,1)S(1)}, bf16[256,2176]{1,0:T(8,128)(2,1)S(1)}) custom-call(bf16[128,2176]{1,0:T(8,128)(2,1)S(1)} %collective-permute-done.11.refs_0_, bf16[128,2176]{1,0:T(8,128)(2,1)S(1)} %collective-permute-done.12.refs_1_, bf16[128,2176]{1,0:T(8,128)(2,1)S(1)} %collective-permute-done.20.refs_2_, ...), custom_call_target="tpu_custom_call" | custom-call | flops 5989466112 | bytes 15466496 | tf_op jit(solution)/shard_map/expert/pallas_call | solution.py:462
  154.1 1.3 collective-permute-done.18.refs_0_
  155.4 3.4 %collective-permute-done.19.refs_1_ = bf16[128,2176]{1,0:T(8,128)(2,1)S(1)} collective-permute-done((bf16[128,2176]{1,0:T(8,128)(2,1)S(1)}, bf16[128,2176]{1,0:T(8,128)(2,1)S(1)}, u32[]{:S(2)}, u32[]{:S(2)}) %collective-permute-start.19) | collective-permute-done | bytes 557088 | tf_op jit(solution)/shard_map/ppermute | solution.py:508
  159.4 2.2 collective-permute-done.22
  162.0 3.2 %collective-permute-start.24 = (bf16[128,2176]{1,0:T(8,128)(2,1)S(1)}, bf16[128,2176]{1,0:T(8,128)(2,1)S(1)}, u32[]{:S(2)}, u32[]{:S(2)}) collective-permute-start(bf16[128,2176]{1,0:T(8,128)(2,1)S(1)} %get-tuple-element.86), channel_id=1, source_target_pairs={{0,6},{1,7},{2,0},{3,1},{4,2},{5,3},{6,4},{7,5},{8,14},{9,15},{10,... | collective-permute-start | bytes 1671176 | tf_op jit(solution)/shard_map/ppermute | solution.py:513
  165.2 8.4 %expert.7 = (bf16[256,2176]{1,0:T(8,128)(2,1)S(1)}, bf16[256,2176]{1,0:T(8,128)(2,1)S(1)}) custom-call(bf16[128,2176]{1,0:T(8,128)(2,1)S(1)} %collective-permute-done.18.refs_0_, bf16[128,2176]{1,0:T(8,128)(2,1)S(1)} %collective-permute-done.19.refs_1_, bf16[128,2176]{1,0:T(8,128)(2,1)S(1)} %collective-permute-done.25.refs_2_, ...), custom_call_target="tpu_custom_call" | custom-call | flops 5989466112 | bytes 15466496 | tf_op jit(solution)/shard_map/expert/pallas_call | solution.py:462
  173.6 4.2 %collective-permute-done.23 = bf16[128,2176]{1,0:T(8,128)(2,1)S(1)} collective-permute-done((bf16[128,2176]{1,0:T(8,128)(2,1)S(1)}, bf16[128,2176]{1,0:T(8,128)(2,1)S(1)}, u32[]{:S(2)}, u32[]{:S(2)}) %collective-permute-start.23) | collective-permute-done | bytes 557088 | tf_op jit(solution)/shard_map/ppermute | solution.py:508
  177.8 3.0 %collective-permute-start.17 = (bf16[128,2176]{1,0:T(8,128)(2,1)S(1)}, bf16[128,2176]{1,0:T(8,128)(2,1)S(1)}, u32[]{:S(2)}, u32[]{:S(2)}) collective-permute-start(bf16[128,2176]{1,0:T(8,128)(2,1)S(1)} %get-tuple-element.74), channel_id=1, source_target_pairs={{0,6},{1,7},{2,0},{3,1},{4,2},{5,3},{6,4},{7,5},{8,14},{9,15},{10,... | collective-permute-start | bytes 1671176 | tf_op jit(solution)/shard_map/ppermute | solution.py:513
  181.3 3.3 %collective-permute-start.30 = (bf16[128,2176]{1,0:T(8,128)(2,1)S(1)}, bf16[128,2176]{1,0:T(8,128)(2,1)S(1)}, u32[]{:S(2)}, u32[]{:S(2)}) collective-permute-start(bf16[128,2176]{1,0:T(8,128)(2,1)S(1)} %get-tuple-element.97), channel_id=1, source_target_pairs={{0,6},{1,7},{2,0},{3,1},{4,2},{5,3},{6,4},{7,5},{8,14},{9,15},{10,... | collective-permute-start | bytes 1671176 | tf_op jit(solution)/shard_map/ppermute | solution.py:513
  184.6 9.1 %collective-permute-done.17.top_after = bf16[128,2176]{1,0:T(8,128)(2,1)S(1)} collective-permute-done((bf16[128,2176]{1,0:T(8,128)(2,1)S(1)}, bf16[128,2176]{1,0:T(8,128)(2,1)S(1)}, u32[]{:S(2)}, u32[]{:S(2)}) %collective-permute-start.17) | collective-permute-done | bytes 557088 | tf_op jit(solution)/shard_map/ppermute | solution.py:513
  193.7 3.7 %collective-permute-done.29.bottom_before = bf16[128,2176]{1,0:T(8,128)(2,1)S(1)} collective-permute-done((bf16[128,2176]{1,0:T(8,128)(2,1)S(1)}, bf16[128,2176]{1,0:T(8,128)(2,1)S(1)}, u32[]{:S(2)}, u32[]{:S(2)}) %collective-permute-start.29) | collective-permute-done | bytes 557088 | tf_op jit(solution)/shard_map/ppermute | solution.py:508
  197.5 11.2 %collective-permute-done.28.top_before = bf16[128,2176]{1,0:T(8,128)(2,1)S(1)} collective-permute-done((bf16[128,2176]{1,0:T(8,128)(2,1)S(1)}, bf16[128,2176]{1,0:T(8,128)(2,1)S(1)}, u32[]{:S(2)}, u32[]{:S(2)}) %collective-permute-start.28) | collective-permute-done | bytes 557088 | tf_op jit(solution)/shard_map/ppermute | solution.py:508
  208.7 1.6 settle.1
  210.3 3.8 %all-to-all-start.3 = ((bf16[16,16,2176]{2,1,0:T(8,128)(2,1)}), bf16[16,16,2176]{2,1,0:T(8,128)(2,1)S(1)}, u32[]{:S(2)}, u32[]{:S(2)}) async-start(bf16[16,16,2176]{2,1,0:T(8,128)(2,1)} %bitcast.29), calls=%async_computation.3 | async-start | bytes 2228224 | tf_op jit(solution)/shard_map/all_to_all | solution.py:660
  214.2 18.1 %all-to-all-done.3 = bf16[16,16,2176]{2,1,0:T(8,128)(2,1)S(1)} async-done(((bf16[16,16,2176]{2,1,0:T(8,128)(2,1)}), bf16[16,16,2176]{2,1,0:T(8,128)(2,1)S(1)}, u32[]{:S(2)}, u32[]{:S(2)}) %all-to-all-start.3) | async-done | bytes 1114144 | tf_op jit(solution)/shard_map/all_to_all | solution.py:660
  232.4 1.7 combine.1
  234.1 1.3 copy.56
  (130 shorter events, 20.7 us)
Async XLA Ops:
  1.5 14.0 %copy-start.24 = (bf16[512,2,128]{2,1,0:T(2,128)(2,1)S(1)}, bf16[512,2,128]{2,1,0:T(2,128)(2,1)}, u32[]{:S(2)}) copy-start(bf16[512,2,128]{2,1,0:T(2,128)(2,1)} %param.20) | copy-start | bytes 786436
  7.4 8.2 %copy-start.19 = (f32[2,512,128]{2,1,0:T(8,128)}, f32[2,512,128]{2,1,0:T(8,128)S(1)}, u32[]{:S(2)}) copy-start(f32[2,512,128]{2,1,0:T(8,128)S(1)} %get-tuple-element.54.first) | copy-start | bytes 1572868
  7.4 8.2 %copy-start.30 = (f32[8]{0:T(128)S(1)}, f32[8]{0:T(128)}, u32[]{:S(2)}) copy-start(f32[8]{0:T(128)} %param.23) | copy-start | bytes 100
  7.4 17.0 %all-to-all-start = ((bf16[16,72,128]{2,1,0:T(8,128)(2,1)}), bf16[16,72,128]{2,1,0:T(8,128)(2,1)}, u32[]{:S(2)}, u32[]{:S(2)}) async-start(bf16[16,72,128]{2,1,0:T(8,128)(2,1)} %get-tuple-element.51), calls=%async_computation | async-start | bytes 589824 | tf_op jit(solution)/shard_map/all_to_all | solution.py:612
  17.1 21.4 %copy-start.1 = (bf16[512,2,512]{2,0,1:T(8,128)(2,1)}, bf16[512,2,512]{2,0,1:T(8,128)(2,1)S(1)}, u32[]{:S(2)}) copy-start(bf16[512,2,512]{2,0,1:T(8,128)(2,1)S(1)} %copy.54) | copy-start | bytes 3145732
  26.1 12.4 %all-to-all-start.1 = ((bf16[16,64,128]{2,1,0:T(8,128)(2,1)}), bf16[16,64,128]{2,1,0:T(8,128)(2,1)S(1)}, u32[]{:S(2)}, u32[]{:S(2)}) async-start(bf16[16,64,128]{2,1,0:T(8,128)(2,1)} %scan.1), calls=%async_computation.1 | async-start | bytes 524288 | tf_op jit(solution)/shard_map/all_to_all | solution.py:616
  30.0 8.5 %copy-start.14 = (f32[512]{0:T(512)S(1)}, f32[512]{0:T(512)}, u32[]{:S(2)}) copy-start(f32[512]{0:T(512)} %param.24) | copy-start | bytes 6148
  38.5 8.9 %copy-start.3 = (bf16[16,64,128]{2,1,0:T(8,128)(2,1)}, bf16[16,64,128]{2,1,0:T(8,128)(2,1)S(1)}, u32[]{:S(2)}) copy-start(bf16[16,64,128]{2,1,0:T(8,128)(2,1)S(1)} %all-to-all-done.1.entering) | copy-start | bytes 786436
  47.4 9.0 %collective-permute-start = (bf16[4,64,2048]{2,1,0:T(8,128)(2,1)}, bf16[4,64,2048]{2,1,0:T(8,128)(2,1)S(1)}, u32[]{:S(2)}, u32[]{:S(2)}) collective-permute-start(bf16[4,64,2048]{2,1,0:T(8,128)(2,1)} %get-tuple-element.56), channel_id=1, source_target_pairs={{0,1},{1,0},{2,3},{3,2},{4,5},{5,4},{6,7},{7,6},{8,9},{9,8},{10,11... | collective-permute-start | bytes 3145736 | tf_op jit(solution)/shard_map/ppermute | solution.py:518
  54.7 5.6 %collective-permute-start.1 = (bf16[4,64,2048]{2,1,0:T(8,128)(2,1)}, bf16[4,64,2048]{2,1,0:T(8,128)(2,1)}, u32[]{:S(2)}, u32[]{:S(2)}) collective-permute-start(bf16[4,64,2048]{2,1,0:T(8,128)(2,1)} %get-tuple-element.59), channel_id=1, source_target_pairs={{0,1},{1,0},{2,3},{3,2},{4,5},{5,4},{6,7},{7,6},{8,9},{9,8},{10,11... | collective-permute-start | bytes 3145736 | tf_op jit(solution)/shard_map/ppermute | solution.py:518
  57.3 23.7 %collective-permute-start.2 = (bf16[64,2048]{1,0:T(8,128)(2,1)}, bf16[64,2048]{1,0:T(8,128)(2,1)S(1)}, u32[]{:S(2)}, u32[]{:S(2)}) collective-permute-start(bf16[64,2048]{1,0:T(8,128)(2,1)} %get-tuple-element.106), channel_id=1, source_target_pairs={{0,6},{1,7},{2,0},{3,1},{4,2},{5,3},{6,4},{7,5},{8,14},{9,15},{10,... | collective-permute-start | bytes 786440 | tf_op jit(solution)/shard_map/ppermute | solution.py:513
  60.3 10.4 %collective-permute-start.3 = (bf16[64,2048]{1,0:T(8,128)(2,1)S(1)}, bf16[64,2048]{1,0:T(8,128)(2,1)S(1)}, u32[]{:S(2)}, u32[]{:S(2)}) collective-permute-start(bf16[64,2048]{1,0:T(8,128)(2,1)S(1)} %get-tuple-element.105), channel_id=1, source_target_pairs={{0,2},{1,3},{2,4},{3,5},{4,6},{5,7},{6,0},{7,1},{8,10},{9,11},{10,... | collective-permute-start | bytes 786440 | tf_op jit(solution)/shard_map/ppermute | solution.py:508
  62.1 15.3 %copy-start.22 = (bf16[64,2,2048]{2,1,0:T(2,128)(2,1)S(1)}, bf16[64,2,2048]{2,1,0:T(2,128)(2,1)}, u32[]{:S(2)}) copy-start(bf16[64,2,2048]{2,1,0:T(2,128)(2,1)} %param.26) | copy-start | bytes 1572868
  62.1 15.2 %slice-start = ((s32[16,3]{0,1:T(4,128)}), s32[16,2]{0,1:T(2,128)S(1)}, s32[]{:S(2)}) async-start(s32[16,3]{0,1:T(4,128)} %copy-done.28), calls=%async_computation.4 | async-start | bytes 2048 | tf_op jit(solution)/shard_map/slice.1
  62.1 18.8 %collective-permute-start.5 = (bf16[64,2048]{1,0:T(8,128)(2,1)}, bf16[64,2048]{1,0:T(8,128)(2,1)}, u32[]{:S(2)}, u32[]{:S(2)}) collective-permute-start(bf16[64,2048]{1,0:T(8,128)(2,1)} %get-tuple-element.104), channel_id=1, source_target_pairs={{0,2},{1,3},{2,4},{3,5},{4,6},{5,7},{6,0},{7,1},{8,10},{9,11},{10,... | collective-permute-start | bytes 786440 | tf_op jit(solution)/shard_map/ppermute | solution.py:508
  62.8 9.1 %collective-permute-start.6 = (bf16[64,2048]{1,0:T(8,128)(2,1)S(1)}, bf16[64,2048]{1,0:T(8,128)(2,1)S(1)}, u32[]{:S(2)}, u32[]{:S(2)}) collective-permute-start(bf16[64,2048]{1,0:T(8,128)(2,1)S(1)} %get-tuple-element.103), channel_id=1, source_target_pairs={{0,6},{1,7},{2,0},{3,1},{4,2},{5,3},{6,4},{7,5},{8,14},{9,15},{10,... | collective-permute-start | bytes 786440 | tf_op jit(solution)/shard_map/ppermute | solution.py:513
  71.5 11.1 %copy-start.5 = (f32[2048]{0:T(1024)S(1)}, f32[2048]{0:T(1024)}, u32[]{:S(2)}) copy-start(f32[2048]{0:T(1024)} %param.27) | copy-start | bytes 24580
  71.5 9.5 %collective-permute-start.4 = (bf16[64,2048]{1,0:T(8,128)(2,1)}, bf16[64,2048]{1,0:T(8,128)(2,1)}, u32[]{:S(2)}, u32[]{:S(2)}) collective-permute-start(bf16[64,2048]{1,0:T(8,128)(2,1)} %fusion.1), channel_id=1, source_target_pairs={{0,2},{1,3},{2,4},{3,5},{4,6},{5,7},{6,0},{7,1},{8,10},{9,11},{10,... | collective-permute-start | bytes 786440 | tf_op jit(solution)/shard_map/ppermute | solution.py:508
  73.7 9.0 %collective-permute-start.7 = (bf16[64,2048]{1,0:T(8,128)(2,1)}, bf16[64,2048]{1,0:T(8,128)(2,1)}, u32[]{:S(2)}, u32[]{:S(2)}) collective-permute-start(bf16[64,2048]{1,0:T(8,128)(2,1)} %fusion), channel_id=1, source_target_pairs={{0,6},{1,7},{2,0},{3,1},{4,2},{5,3},{6,4},{7,5},{8,14},{9,15},{10,... | collective-permute-start | bytes 786440 | tf_op jit(solution)/shard_map/ppermute | solution.py:513
  83.7 26.2 %copy-start.7 = (bf16[1,2048,896]{2,1,0:T(8,128)(2,1)S(1)}, bf16[1,2048,896]{2,1,0:T(8,128)(2,1)}, u32[]{:S(2)}) copy-start(bf16[1,2048,896]{2,1,0:T(8,128)(2,1)} %param.29) | copy-start | bytes 11010052
  85.9 20.0 %copy-start.11 = (f32[128,2048]{1,0:T(8,128)}, f32[128,2048]{1,0:T(8,128)S(1)}, u32[]{:S(2)}) copy-start(f32[128,2048]{1,0:T(8,128)S(1)} %get-tuple-element.96.hidden) | copy-start | bytes 3145732
  85.9 23.9 %copy-start.6 = (bf16[1,2048,896]{2,1,0:T(8,128)(2,1)S(1)}, bf16[1,2048,896]{2,1,0:T(8,128)(2,1)}, u32[]{:S(2)}) copy-start(bf16[1,2048,896]{2,1,0:T(8,128)(2,1)} %param.28) | copy-start | bytes 11010052
  105.9 3.9 %collective-permute-start.10 = (bf16[256,2176]{1,0:T(8,128)(2,1)S(1)}, bf16[256,2176]{1,0:T(8,128)(2,1)S(1)}, u32[]{:S(2)}, u32[]{:S(2)}) collective-permute-start(bf16[256,2176]{1,0:T(8,128)(2,1)S(1)} %bitcast.81), channel_id=1, source_target_pairs={{0,1},{1,0},{2,3},{3,2},{4,5},{5,4},{6,7},{7,6},{8,9},{9,8},{10,11... | collective-permute-start | bytes 3342344 | tf_op jit(solution)/shard_map/ppermute | solution.py:518
  106.0 17.1 %collective-permute-start.8 = (bf16[128,2176]{1,0:T(8,128)(2,1)S(1)}, bf16[128,2176]{1,0:T(8,128)(2,1)S(1)}, u32[]{:S(2)}, u32[]{:S(2)}) collective-permute-start(bf16[128,2176]{1,0:T(8,128)(2,1)S(1)} %bitcast.118), channel_id=1, source_target_pairs={{0,2},{1,3},{2,4},{3,5},{4,6},{5,7},{6,0},{7,1},{8,10},{9,11},{10,... | collective-permute-start | bytes 1671176 | tf_op jit(solution)/shard_map/ppermute | solution.py:508
  106.1 17.0 %collective-permute-start.9 = (bf16[128,2176]{1,0:T(8,128)(2,1)S(1)}, bf16[128,2176]{1,0:T(8,128)(2,1)S(1)}, u32[]{:S(2)}, u32[]{:S(2)}) collective-permute-start(bf16[128,2176]{1,0:T(8,128)(2,1)S(1)} %bitcast.116), channel_id=1, source_target_pairs={{0,6},{1,7},{2,0},{3,1},{4,2},{5,3},{6,4},{7,5},{8,14},{9,15},{10,... | collective-permute-start | bytes 1671176 | tf_op jit(solution)/shard_map/ppermute | solution.py:513
  123.1 3.8 %collective-permute-start.14 = (bf16[128,2176]{1,0:T(8,128)(2,1)S(1)}, bf16[128,2176]{1,0:T(8,128)(2,1)S(1)}, u32[]{:S(2)}, u32[]{:S(2)}) collective-permute-start(bf16[128,2176]{1,0:T(8,128)(2,1)S(1)} %collective-permute-done.8.refs_0_), channel_id=1, source_target_pairs={{0,1},{1,0},{2,3},{3,2},{4,5},{5,4},{6,7},{7,6},{8,9},{9,8},{10,11... | collective-permute-start | bytes 1671176 | tf_op jit(solution)/shard_map/ppermute | solution.py:518
  123.1 3.8 %collective-permute-start.15 = (bf16[128,2176]{1,0:T(8,128)(2,1)S(1)}, bf16[128,2176]{1,0:T(8,128)(2,1)S(1)}, u32[]{:S(2)}, u32[]{:S(2)}) collective-permute-start(bf16[128,2176]{1,0:T(8,128)(2,1)S(1)} %collective-permute-done.9.refs_1_), channel_id=1, source_target_pairs={{0,1},{1,0},{2,3},{3,2},{4,5},{5,4},{6,7},{7,6},{8,9},{9,8},{10,11... | collective-permute-start | bytes 1671176 | tf_op jit(solution)/shard_map/ppermute | solution.py:518
  123.6 16.3 %collective-permute-start.13 = (bf16[256,2176]{1,0:T(8,128)(2,1)S(1)}, bf16[256,2176]{1,0:T(8,128)(2,1)S(1)}, u32[]{:S(2)}, u32[]{:S(2)}) collective-permute-start(bf16[256,2176]{1,0:T(8,128)(2,1)S(1)} %get-tuple-element.66), channel_id=1, source_target_pairs={{0,1},{1,0},{2,3},{3,2},{4,5},{5,4},{6,7},{7,6},{8,9},{9,8},{10,11... | collective-permute-start | bytes 3342344 | tf_op jit(solution)/shard_map/ppermute | solution.py:518
  123.6 16.3 %collective-permute-start.11 = (bf16[128,2176]{1,0:T(8,128)(2,1)S(1)}, bf16[128,2176]{1,0:T(8,128)(2,1)S(1)}, u32[]{:S(2)}, u32[]{:S(2)}) collective-permute-start(bf16[128,2176]{1,0:T(8,128)(2,1)S(1)} %collective-permute-done.8.refs_0_), channel_id=1, source_target_pairs={{0,2},{1,3},{2,4},{3,5},{4,6},{5,7},{6,0},{7,1},{8,10},{9,11},{10,... | collective-permute-start | bytes 1671176 | tf_op jit(solution)/shard_map/ppermute | solution.py:508
  124.7 15.2 %collective-permute-start.12 = (bf16[128,2176]{1,0:T(8,128)(2,1)S(1)}, bf16[128,2176]{1,0:T(8,128)(2,1)S(1)}, u32[]{:S(2)}, u32[]{:S(2)}) collective-permute-start(bf16[128,2176]{1,0:T(8,128)(2,1)S(1)} %collective-permute-done.9.refs_1_), channel_id=1, source_target_pairs={{0,6},{1,7},{2,0},{3,1},{4,2},{5,3},{6,4},{7,5},{8,14},{9,15},{10,... | collective-permute-start | bytes 1671176 | tf_op jit(solution)/shard_map/ppermute | solution.py:513
  139.9 3.5 %collective-permute-start.16 = (bf16[256,2176]{1,0:T(8,128)(2,1)S(1)}, bf16[256,2176]{1,0:T(8,128)(2,1)S(1)}, u32[]{:S(2)}, u32[]{:S(2)}) collective-permute-start(bf16[256,2176]{1,0:T(8,128)(2,1)S(1)} %get-tuple-element.71), channel_id=1, source_target_pairs={{0,1},{1,0},{2,3},{3,2},{4,5},{5,4},{6,7},{7,6},{8,9},{9,8},{10,11... | collective-permute-start | bytes 3342344 | tf_op jit(solution)/shard_map/ppermute | solution.py:518
  139.9 15.5 %collective-permute-start.18 = (bf16[128,2176]{1,0:T(8,128)(2,1)S(1)}, bf16[128,2176]{1,0:T(8,128)(2,1)S(1)}, u32[]{:S(2)}, u32[]{:S(2)}) collective-permute-start(bf16[128,2176]{1,0:T(8,128)(2,1)S(1)} %bitcast.119), channel_id=1, source_target_pairs={{0,6},{1,7},{2,0},{3,1},{4,2},{5,3},{6,4},{7,5},{8,14},{9,15},{10,... | collective-permute-start | bytes 1671176 | tf_op jit(solution)/shard_map/ppermute | solution.py:513
  142.9 16.0 %collective-permute-start.19 = (bf16[128,2176]{1,0:T(8,128)(2,1)S(1)}, bf16[128,2176]{1,0:T(8,128)(2,1)S(1)}, u32[]{:S(2)}, u32[]{:S(2)}) collective-permute-start(bf16[128,2176]{1,0:T(8,128)(2,1)S(1)} %bitcast.117), channel_id=1, source_target_pairs={{0,2},{1,3},{2,4},{3,5},{4,6},{5,7},{6,0},{7,1},{8,10},{9,11},{10,... | collective-permute-start | bytes 1671176 | tf_op jit(solution)/shard_map/ppermute | solution.py:508
  142.9 2.0 collective-permute-start.20
  143.1 2.5 %collective-permute-start.21 = (bf16[128,2176]{1,0:T(8,128)(2,1)S(1)}, bf16[128,2176]{1,0:T(8,128)(2,1)S(1)}, u32[]{:S(2)}, u32[]{:S(2)}) collective-permute-start(bf16[128,2176]{1,0:T(8,128)(2,1)S(1)} %collective-permute-done.12.refs_1_), channel_id=1, source_target_pairs={{0,1},{1,0},{2,3},{3,2},{4,5},{5,4},{6,7},{7,6},{8,9},{9,8},{10,11... | collective-permute-start | bytes 1671176 | tf_op jit(solution)/shard_map/ppermute | solution.py:518
  158.9 2.8 %collective-permute-start.22 = (bf16[256,2176]{1,0:T(8,128)(2,1)S(1)}, bf16[256,2176]{1,0:T(8,128)(2,1)S(1)}, u32[]{:S(2)}, u32[]{:S(2)}) collective-permute-start(bf16[256,2176]{1,0:T(8,128)(2,1)S(1)} %get-tuple-element.82), channel_id=1, source_target_pairs={{0,1},{1,0},{2,3},{3,2},{4,5},{5,4},{6,7},{7,6},{8,9},{9,8},{10,11... | collective-permute-start | bytes 3342344 | tf_op jit(solution)/shard_map/ppermute | solution.py:518
  158.9 6.3 %collective-permute-start.25 = (bf16[128,2176]{1,0:T(8,128)(2,1)S(1)}, bf16[128,2176]{1,0:T(8,128)(2,1)S(1)}, u32[]{:S(2)}, u32[]{:S(2)}) collective-permute-start(bf16[128,2176]{1,0:T(8,128)(2,1)S(1)} %collective-permute-done.18.refs_0_), channel_id=1, source_target_pairs={{0,1},{1,0},{2,3},{3,2},{4,5},{5,4},{6,7},{7,6},{8,9},{9,8},{10,11... | collective-permute-start | bytes 1671176 | tf_op jit(solution)/shard_map/ppermute | solution.py:518
  159.4 5.8 %collective-permute-start.26 = (bf16[128,2176]{1,0:T(8,128)(2,1)S(1)}, bf16[128,2176]{1,0:T(8,128)(2,1)S(1)}, u32[]{:S(2)}, u32[]{:S(2)}) collective-permute-start(bf16[128,2176]{1,0:T(8,128)(2,1)S(1)} %collective-permute-done.19.refs_1_), channel_id=1, source_target_pairs={{0,1},{1,0},{2,3},{3,2},{4,5},{5,4},{6,7},{7,6},{8,9},{9,8},{10,11... | collective-permute-start | bytes 1671176 | tf_op jit(solution)/shard_map/ppermute | solution.py:518
  161.9 15.9 %collective-permute-start.23 = (bf16[128,2176]{1,0:T(8,128)(2,1)S(1)}, bf16[128,2176]{1,0:T(8,128)(2,1)S(1)}, u32[]{:S(2)}, u32[]{:S(2)}) collective-permute-start(bf16[128,2176]{1,0:T(8,128)(2,1)S(1)} %get-tuple-element.85), channel_id=1, source_target_pairs={{0,2},{1,3},{2,4},{3,5},{4,6},{5,7},{6,0},{7,1},{8,10},{9,11},{10,... | collective-permute-start | bytes 1671176 | tf_op jit(solution)/shard_map/ppermute | solution.py:508
  162.0 15.9 %collective-permute-start.24 = (bf16[128,2176]{1,0:T(8,128)(2,1)S(1)}, bf16[128,2176]{1,0:T(8,128)(2,1)S(1)}, u32[]{:S(2)}, u32[]{:S(2)}) collective-permute-start(bf16[128,2176]{1,0:T(8,128)(2,1)S(1)} %get-tuple-element.86), channel_id=1, source_target_pairs={{0,6},{1,7},{2,0},{3,1},{4,2},{5,3},{6,4},{7,5},{8,14},{9,15},{10,... | collective-permute-start | bytes 1671176 | tf_op jit(solution)/shard_map/ppermute | solution.py:513
  177.8 3.0 %collective-permute-start.27 = (bf16[256,2176]{1,0:T(8,128)(2,1)S(1)}, bf16[256,2176]{1,0:T(8,128)(2,1)S(1)}, u32[]{:S(2)}, u32[]{:S(2)}) collective-permute-start(bf16[256,2176]{1,0:T(8,128)(2,1)S(1)} %get-tuple-element.92), channel_id=1, source_target_pairs={{0,1},{1,0},{2,3},{3,2},{4,5},{5,4},{6,7},{7,6},{8,9},{9,8},{10,11... | collective-permute-start | bytes 3342344 | tf_op jit(solution)/shard_map/ppermute | solution.py:518
  177.8 15.9 %collective-permute-start.17 = (bf16[128,2176]{1,0:T(8,128)(2,1)S(1)}, bf16[128,2176]{1,0:T(8,128)(2,1)S(1)}, u32[]{:S(2)}, u32[]{:S(2)}) collective-permute-start(bf16[128,2176]{1,0:T(8,128)(2,1)S(1)} %get-tuple-element.74), channel_id=1, source_target_pairs={{0,6},{1,7},{2,0},{3,1},{4,2},{5,3},{6,4},{7,5},{8,14},{9,15},{10,... | collective-permute-start | bytes 1671176 | tf_op jit(solution)/shard_map/ppermute | solution.py:513
  180.8 16.7 %collective-permute-start.29 = (bf16[128,2176]{1,0:T(8,128)(2,1)S(1)}, bf16[128,2176]{1,0:T(8,128)(2,1)S(1)}, u32[]{:S(2)}, u32[]{:S(2)}) collective-permute-start(bf16[128,2176]{1,0:T(8,128)(2,1)S(1)} %get-tuple-element.94), channel_id=1, source_target_pairs={{0,2},{1,3},{2,4},{3,5},{4,6},{5,7},{6,0},{7,1},{8,10},{9,11},{10,... | collective-permute-start | bytes 1671176 | tf_op jit(solution)/shard_map/ppermute | solution.py:508
  181.2 27.5 %collective-permute-start.28 = (bf16[128,2176]{1,0:T(8,128)(2,1)S(1)}, bf16[128,2176]{1,0:T(8,128)(2,1)S(1)}, u32[]{:S(2)}, u32[]{:S(2)}) collective-permute-start(bf16[128,2176]{1,0:T(8,128)(2,1)S(1)} %get-tuple-element.98), channel_id=1, source_target_pairs={{0,2},{1,3},{2,4},{3,5},{4,6},{5,7},{6,0},{7,1},{8,10},{9,11},{10,... | collective-permute-start | bytes 1671176 | tf_op jit(solution)/shard_map/ppermute | solution.py:508
  181.3 27.4 %collective-permute-start.30 = (bf16[128,2176]{1,0:T(8,128)(2,1)S(1)}, bf16[128,2176]{1,0:T(8,128)(2,1)S(1)}, u32[]{:S(2)}, u32[]{:S(2)}) collective-permute-start(bf16[128,2176]{1,0:T(8,128)(2,1)S(1)} %get-tuple-element.97), channel_id=1, source_target_pairs={{0,6},{1,7},{2,0},{3,1},{4,2},{5,3},{6,4},{7,5},{8,14},{9,15},{10,... | collective-permute-start | bytes 1671176 | tf_op jit(solution)/shard_map/ppermute | solution.py:513
  210.3 22.1 %copy-start.12 = (f32[128,2048]{1,0:T(8,128)S(1)}, f32[128,2048]{1,0:T(8,128)}, u32[]{:S(2)}) copy-start(f32[128,2048]{1,0:T(8,128)} %copy-done.11) | copy-start | bytes 3145732
  210.3 22.1 %copy-start.13 = (f32[4,2048]{1,0:T(4,128)S(1)}, f32[4,2048]{1,0:T(4,128)}, u32[]{:S(2)}) copy-start(f32[4,2048]{1,0:T(4,128)} %directions.1) | copy-start | bytes 98308
  210.3 22.1 %all-to-all-start.3 = ((bf16[16,16,2176]{2,1,0:T(8,128)(2,1)}), bf16[16,16,2176]{2,1,0:T(8,128)(2,1)S(1)}, u32[]{:S(2)}, u32[]{:S(2)}) async-start(bf16[16,16,2176]{2,1,0:T(8,128)(2,1)} %bitcast.29), calls=%async_computation.3 | async-start | bytes 2228224 | tf_op jit(solution)/shard_map/all_to_all | solution.py:660
  (18 other events, 45.8 us)

commit v2 on v1

--- a/solution.py
+++ b/solution.py
@@ -280,7 +280,7 @@
             pltpu.SemaphoreType.DMA((blocks, columns // blocks)),
         ],
         compiler_params=pltpu.CompilerParams(
-            dimension_semantics=("arbitrary",), vmem_limit_bytes=16 * 2**20
+            dimension_semantics=("arbitrary",), vmem_limit_bytes=48 * 2**20
         ),
         cost_estimate=pl.CostEstimate(
             flops=2 * 10**9, bytes_accessed=6 * 2**20, transcendentals=2**18
@@ -559,7 +559,9 @@
     top_after = from_after(near_top)
     bottom_before = from_before(near_bottom)
     kept, passed = call((far_top, far_bottom, *others))
-    after_top, before_bottom, kept, passed = after((after_top, before_bottom, kept, passed))
+    after_top, before_bottom, top_after, bottom_before, kept, passed = after(
+        (after_top, before_bottom, top_after, bottom_before, kept, passed)
+    )
     late = from_sibling(after_top), from_sibling(before_bottom)
     got = from_sibling(passed)
     far_top, far_bottom = add_up(kept[:half], got[:half]), add_up(kept[half:], got[half:])

time: 236 us -> 238 us (level)
  Pallas kernels: 62.6 us -> 65.9 us
    pallas_call x2, Pallas kernels: 9.84 us -> 13.2 us  [mixer_call(): pl.pallas_call(mixer_kernel, grid=(blocks,), in_specs=[pl.BlockSpec(memor...]
    unnamed x66 -> x62, local copies, waits for them, and re-layouts: 14.1 us -> 12.5 us
  transfers between devices with their start and end apart: 34 -> 34, of which waited for: 17 -> 16; matrix products, arithmetic and copies ran while one was open for 5% -> 5% of each run, Pallas kernels for 19% -> 19%
where the time goes in v2:
time: 238 us; the launch traced here: 237 us
  waiting for transfers between devices  77.5 us (33%)
  Pallas kernels  65.9 us (28%)
  starting transfers between devices  48 us (20%)
  blocking collectives  20 us (8%)
  local copies, waits for them, and re-layouts  17.4 us (7%)
  other arithmetic  7.78 us (3%)
    ppermute x9, waiting for transfers between devices, from_before(): lax.ppermute(values, 'exp', [(i, (i + 2) % size) for i in range(size)])  36.5 us
    pallas_call x4, Pallas kernels, expert_call(): pl.pallas_call(functools.partial(expert_kernel, counts), in_specs=[anywhe...  33.8 us
    ppermute x9, starting transfers between devices, from_after(): lax.ppermute(values, 'exp', [(i, (i - 2) % size) for i in range(size)])  28 us
    all_to_all x1, blocking collectives, on_device(): lax.all_to_all(packed.reshape(experts, FOLD, D + 128), 'seq', split_axis=...  20 us
    all_to_all x1, waiting for transfers between devices, on_device(): lax.all_to_all(summed.reshape(experts, FOLD, D + 128), 'seq', split_axis=...  18 us
    pallas_call x2, Pallas kernels, mixer_call(): pl.pallas_call(mixer_kernel, grid=(blocks,), in_specs=[pl.BlockSpec(memor...  13.2 us
    unnamed x62, local copies, waits for them, and re-layouts  12.5 us
    ppermute x9, waiting for transfers between devices, from_after(): lax.ppermute(values, 'exp', [(i, (i - 2) % size) for i in range(size)])  10.2 us
  transfers between devices with their start and end apart: 34, of which 16 were waited for; matrix products, arithmetic and copies ran while one was open for 5% of the time, Pallas kernels for 19%

profile of v2, /device:TPU:0, one launch (start us, length us, event | category | flops | bytes accessed | tf_op | source)
XLA Modules:
  0.0 237.1 jit_solution(13529485429559469618)
XLA Ops:
  0.0 1.4 copy.55
  1.6 5.8 %contrib.1 = (bf16[16,72,128]{2,1,0:T(8,128)(2,1)}, f32[2,512,128]{2,1,0:T(8,128)S(1)}) custom-call(f32[2,8,512]{2,1,0:T(8,128)S(1)} %get-tuple-element.116.decay, f32[2,8,512]{2,1,0:T(8,128)S(1)} %get-tuple-element.115.step, bf16[2,512,512]{2,1,0:T(8,128)(2,1)S(1)} %bitcast.88, bf16[2,512,128]{2,1,0:T(8,128)(2,1)S(1)} %bitcast.96), custom_call_target="tpu_custom_call" | custom-call | flops 1000000000 | bytes 2097152 | tf_op jit(solution)/shard_map/contrib/pallas_call | solution.py:101
  7.4 8.1 %all-to-all-start = ((bf16[16,72,128]{2,1,0:T(8,128)(2,1)}), bf16[16,72,128]{2,1,0:T(8,128)(2,1)}, u32[]{:S(2)}, u32[]{:S(2)}) async-start(bf16[16,72,128]{2,1,0:T(8,128)(2,1)} %get-tuple-element.53), calls=%async_computation | async-start | bytes 589824 | tf_op jit(solution)/shard_map/all_to_all | solution.py:614
  15.8 1.4 copy.54
  17.2 3.0 %within.2 = f32[1,512,512]{2,1,0:T(8,128)S(1)} custom-call(f32[2,8,512]{2,1,0:T(8,128)S(1)} %get-tuple-element.116.decay, f32[2,8,512]{2,1,0:T(8,128)S(1)} %get-tuple-element.115.step, bf16[2,512,512]{2,1,0:T(8,128)(2,1)S(1)} %bitcast.89, bf16[2,512,128]{2,1,0:T(8,128)(2,1)S(1)} %bitcast.97, bf16[2,512,128]{2,1,0:T(8,128)(2,1)S(1)} %bitcast.92, ...), custom_call_target="tpu_custom_call" | custom-call | flops 3000000000 | bytes 2097152 | tf_op jit(solution)/shard_map/within/pallas_call | solution.py:159
  21.1 3.3 %all-to-all-done.parcels = bf16[16,72,128]{2,1,0:T(8,128)(2,1)} async-done(((bf16[16,72,128]{2,1,0:T(8,128)(2,1)}), bf16[16,72,128]{2,1,0:T(8,128)(2,1)}, u32[]{:S(2)}, u32[]{:S(2)}) %all-to-all-start) | async-done | bytes 294944 | tf_op jit(solution)/shard_map/all_to_all | solution.py:614
  24.4 1.7 scan.1
  26.1 3.9 %all-to-all-start.1 = ((bf16[16,64,128]{2,1,0:T(8,128)(2,1)}), bf16[16,64,128]{2,1,0:T(8,128)(2,1)S(1)}, u32[]{:S(2)}, u32[]{:S(2)}) async-start(bf16[16,64,128]{2,1,0:T(8,128)(2,1)} %scan.1), calls=%async_computation.1 | async-start | bytes 524288 | tf_op jit(solution)/shard_map/all_to_all | solution.py:618
  30.0 3.0 %within.3 = f32[1,512,512]{2,1,0:T(8,128)S(1)} custom-call(f32[2,8,512]{2,1,0:T(8,128)S(1)} %get-tuple-element.116.decay, f32[2,8,512]{2,1,0:T(8,128)S(1)} %get-tuple-element.115.step, bf16[2,512,512]{2,1,0:T(8,128)(2,1)S(1)} %bitcast.90, bf16[2,512,128]{2,1,0:T(8,128)(2,1)S(1)} %bitcast.98, bf16[2,512,128]{2,1,0:T(8,128)(2,1)S(1)} %bitcast.93, ...), custom_call_target="tpu_custom_call" | custom-call | flops 3000000000 | bytes 2097152 | tf_op jit(solution)/shard_map/within/pallas_call | solution.py:159
  34.0 4.6 %all-to-all-done.1.entering = bf16[16,64,128]{2,1,0:T(8,128)(2,1)S(1)} async-done(((bf16[16,64,128]{2,1,0:T(8,128)(2,1)}), bf16[16,64,128]{2,1,0:T(8,128)(2,1)S(1)}, u32[]{:S(2)}, u32[]{:S(2)}) %all-to-all-start.1) | async-done | bytes 262176 | tf_op jit(solution)/shard_map/all_to_all | solution.py:618
  38.5 1.3 copy-done.16
  40.9 6.6 %mixer.2 = (bf16[4,64,2048]{2,1,0:T(8,128)(2,1)S(1)}, bf16[4,64,2048]{2,1,0:T(8,128)(2,1)}) custom-call(s32[1]{0:T(128)} %bitcast.8.place, f32[2,8,512]{2,1,0:T(8,128)S(1)} %get-tuple-element.116.decay, bf16[2,512,128]{2,1,0:T(8,128)(2,1)S(1)} %bitcast.94, bf16[16,64,128]{2,1,0:T(8,128)(2,1)S(1)} %all-to-all-done.1.entering, f32[2,512,128]{2,1,0:T(8,128)S(1)} %copy-done.18, ...), custom_call_target="tpu_custom_call" | custom-call | flops 2000000000 | bytes 6291456 | tf_op jit(solution)/shard_map/mixer/pallas_call | solution.py:262
  47.7 1.2 copy-done.2
  49.8 6.5 %mixer.3 = (bf16[4,64,2048]{2,1,0:T(8,128)(2,1)S(1)}, bf16[4,64,2048]{2,1,0:T(8,128)(2,1)}) custom-call(s32[1]{0:T(128)} %bitcast.8.place, f32[2,8,512]{2,1,0:T(8,128)S(1)} %get-tuple-element.116.decay, bf16[2,512,128]{2,1,0:T(8,128)(2,1)S(1)} %bitcast.95, bf16[16,64,128]{2,1,0:T(8,128)(2,1)S(1)} %copy-done.4, f32[2,512,128]{2,1,0:T(8,128)S(1)} %copy-done.19, ...), custom_call_target="tpu_custom_call" | custom-call | flops 2000000000 | bytes 6291456 | tf_op jit(solution)/shard_map/mixer/pallas_call | solution.py:262
  59.0 3.0 %collective-permute-start.2 = (bf16[64,2048]{1,0:T(8,128)(2,1)}, bf16[64,2048]{1,0:T(8,128)(2,1)S(1)}, u32[]{:S(2)}, u32[]{:S(2)}) collective-permute-start(bf16[64,2048]{1,0:T(8,128)(2,1)} %get-tuple-element.110), channel_id=1, source_target_pairs={{0,6},{1,7},{2,0},{3,1},{4,2},{5,3},{6,4},{7,5},{8,14},{9,15},{10,... | collective-permute-start | bytes 786440 | tf_op jit(solution)/shard_map/ppermute | solution.py:513
  62.0 1.9 fusion.5
  64.5 2.8 %collective-permute-start.6 = (bf16[64,2048]{1,0:T(8,128)(2,1)S(1)}, bf16[64,2048]{1,0:T(8,128)(2,1)S(1)}, u32[]{:S(2)}, u32[]{:S(2)}) collective-permute-start(bf16[64,2048]{1,0:T(8,128)(2,1)S(1)} %get-tuple-element.107), channel_id=1, source_target_pairs={{0,6},{1,7},{2,0},{3,1},{4,2},{5,3},{6,4},{7,5},{8,14},{9,15},{10,... | collective-permute-start | bytes 786440 | tf_op jit(solution)/shard_map/ppermute | solution.py:513
  67.3 5.2 %collective-permute-done.3 = bf16[64,2048]{1,0:T(8,128)(2,1)S(1)} collective-permute-done((bf16[64,2048]{1,0:T(8,128)(2,1)S(1)}, bf16[64,2048]{1,0:T(8,128)(2,1)S(1)}, u32[]{:S(2)}, u32[]{:S(2)}) %collective-permute-start.3) | collective-permute-done | bytes 262176 | tf_op jit(solution)/shard_map/ppermute | solution.py:508
  73.6 1.7 fusion
  75.4 3.7 %collective-permute-start.7 = (bf16[64,2048]{1,0:T(8,128)(2,1)}, bf16[64,2048]{1,0:T(8,128)(2,1)}, u32[]{:S(2)}, u32[]{:S(2)}) collective-permute-start(bf16[64,2048]{1,0:T(8,128)(2,1)} %fusion), channel_id=1, source_target_pairs={{0,6},{1,7},{2,0},{3,1},{4,2},{5,3},{6,4},{7,5},{8,14},{9,15},{10,... | collective-permute-start | bytes 786440 | tf_op jit(solution)/shard_map/ppermute | solution.py:513
  82.7 1.6 collective-permute-done.7.refs_3_
  85.3 2.2 dispatch.1
  87.6 20.0 %all_to_all.20 = bf16[16,16,2176]{2,1,0:T(8,128)(2,1)S(1)} all-to-all(bf16[16,16,2176]{2,1,0:T(8,128)(2,1)S(1)} %bitcast.85), channel_id=1, replica_groups=mesh['seq'=16,'exp'=8] {'seq'}, dimensions={0} | all-to-all | bytes 2228224 | tf_op jit(solution)/shard_map/all_to_all | solution.py:658
  107.8 3.8 %collective-permute-start.9 = (bf16[128,2176]{1,0:T(8,128)(2,1)S(1)}, bf16[128,2176]{1,0:T(8,128)(2,1)S(1)}, u32[]{:S(2)}, u32[]{:S(2)}) collective-permute-start(bf16[128,2176]{1,0:T(8,128)(2,1)S(1)} %bitcast.116), channel_id=1, source_target_pairs={{0,6},{1,7},{2,0},{3,1},{4,2},{5,3},{6,4},{7,5},{8,14},{9,15},{10,... | collective-permute-start | bytes 1671176 | tf_op jit(solution)/shard_map/ppermute | solution.py:513
  111.6 2.0 copy-done.8
  113.6 8.4 %expert.4 = (bf16[256,2176]{1,0:T(8,128)(2,1)S(1)}, bf16[256,2176]{1,0:T(8,128)(2,1)S(1)}) custom-call(bf16[256,2176]{1,0:T(8,128)(2,1)S(1)} %bitcast.82, bf16[256,2176]{1,0:T(8,128)(2,1)S(1)} %collective-permute-done.10.refs_1_, bf16[2048,896]{1,0:T(8,128)(2,1)S(1)} %bitcast.102, bf16[2048,896]{1,0:T(8,128)(2,1)S(1)} %bitcast.106, ...), custom_call_target="tpu_custom_call" | custom-call | flops 5989466112 | bytes 15466496 | tf_op jit(solution)/shard_map/expert/pallas_call | solution.py:462
  122.0 2.7 %collective-permute-done.8.refs_0_ = bf16[128,2176]{1,0:T(8,128)(2,1)S(1)} collective-permute-done((bf16[128,2176]{1,0:T(8,128)(2,1)S(1)}, bf16[128,2176]{1,0:T(8,128)(2,1)S(1)}, u32[]{:S(2)}, u32[]{:S(2)}) %collective-permute-start.8) | collective-permute-done | bytes 557088 | tf_op jit(solution)/shard_map/ppermute | solution.py:508
  126.4 2.1 collective-permute-start.12
  128.5 8.4 %expert.5 = (bf16[256,2176]{1,0:T(8,128)(2,1)S(1)}, bf16[256,2176]{1,0:T(8,128)(2,1)S(1)}) custom-call(bf16[128,2176]{1,0:T(8,128)(2,1)S(1)} %collective-permute-done.8.refs_0_, bf16[128,2176]{1,0:T(8,128)(2,1)S(1)} %collective-permute-done.9.refs_1_, bf16[128,2176]{1,0:T(8,128)(2,1)S(1)} %collective-permute-done.14.refs_2_, ...), custom_call_target="tpu_custom_call" | custom-call | flops 5989466112 | bytes 15466496 | tf_op jit(solution)/shard_map/expert/pallas_call | solution.py:462
  137.0 4.6 %collective-permute-done.11.refs_0_ = bf16[128,2176]{1,0:T(8,128)(2,1)S(1)} collective-permute-done((bf16[128,2176]{1,0:T(8,128)(2,1)S(1)}, bf16[128,2176]{1,0:T(8,128)(2,1)S(1)}, u32[]{:S(2)}, u32[]{:S(2)}) %collective-permute-start.11) | collective-permute-done | bytes 557088 | tf_op jit(solution)/shard_map/ppermute | solution.py:508
  141.6 2.9 %collective-permute-start.16 = (bf16[128,2176]{1,0:T(8,128)(2,1)S(1)}, bf16[128,2176]{1,0:T(8,128)(2,1)S(1)}, u32[]{:S(2)}, u32[]{:S(2)}) collective-permute-start(bf16[128,2176]{1,0:T(8,128)(2,1)S(1)} %bitcast.119), channel_id=1, source_target_pairs={{0,6},{1,7},{2,0},{3,1},{4,2},{5,3},{6,4},{7,5},{8,14},{9,15},{10,... | collective-permute-start | bytes 1671176 | tf_op jit(solution)/shard_map/ppermute | solution.py:513
  145.4 3.3 %collective-permute-start.19 = (bf16[128,2176]{1,0:T(8,128)(2,1)S(1)}, bf16[128,2176]{1,0:T(8,128)(2,1)S(1)}, u32[]{:S(2)}, u32[]{:S(2)}) collective-permute-start(bf16[128,2176]{1,0:T(8,128)(2,1)S(1)} %get-tuple-element.78), channel_id=1, source_target_pairs={{0,6},{1,7},{2,0},{3,1},{4,2},{5,3},{6,4},{7,5},{8,14},{9,15},{10,... | collective-permute-start | bytes 1671176 | tf_op jit(solution)/shard_map/ppermute | solution.py:513
  148.7 8.4 %expert.6 = (bf16[256,2176]{1,0:T(8,128)(2,1)S(1)}, bf16[256,2176]{1,0:T(8,128)(2,1)S(1)}) custom-call(bf16[128,2176]{1,0:T(8,128)(2,1)S(1)} %collective-permute-done.11.refs_0_, bf16[128,2176]{1,0:T(8,128)(2,1)S(1)} %collective-permute-done.12.refs_1_, bf16[128,2176]{1,0:T(8,128)(2,1)S(1)} %collective-permute-done.21.refs_2_, ...), custom_call_target="tpu_custom_call" | custom-call | flops 5989466112 | bytes 15466496 | tf_op jit(solution)/shard_map/expert/pallas_call | solution.py:462
  157.5 3.7 %collective-permute-done.17.refs_1_ = bf16[128,2176]{1,0:T(8,128)(2,1)S(1)} collective-permute-done((bf16[128,2176]{1,0:T(8,128)(2,1)S(1)}, bf16[128,2176]{1,0:T(8,128)(2,1)S(1)}, u32[]{:S(2)}, u32[]{:S(2)}) %collective-permute-start.17) | collective-permute-done | bytes 557088 | tf_op jit(solution)/shard_map/ppermute | solution.py:508
  161.3 7.8 %collective-permute-done.19.top_after = bf16[128,2176]{1,0:T(8,128)(2,1)S(1)} collective-permute-done((bf16[128,2176]{1,0:T(8,128)(2,1)S(1)}, bf16[128,2176]{1,0:T(8,128)(2,1)S(1)}, u32[]{:S(2)}, u32[]{:S(2)}) %collective-permute-start.19) | collective-permute-done | bytes 557088 | tf_op jit(solution)/shard_map/ppermute | solution.py:513
  169.1 3.4 %collective-permute-done.20.bottom_before = bf16[128,2176]{1,0:T(8,128)(2,1)S(1)} collective-permute-done((bf16[128,2176]{1,0:T(8,128)(2,1)S(1)}, bf16[128,2176]{1,0:T(8,128)(2,1)S(1)}, u32[]{:S(2)}, u32[]{:S(2)}) %collective-permute-start.20) | collective-permute-done | bytes 557088 | tf_op jit(solution)/shard_map/ppermute | solution.py:508
  173.0 2.2 collective-permute-done.23
  175.6 3.2 %collective-permute-start.25 = (bf16[128,2176]{1,0:T(8,128)(2,1)S(1)}, bf16[128,2176]{1,0:T(8,128)(2,1)S(1)}, u32[]{:S(2)}, u32[]{:S(2)}) collective-permute-start(bf16[128,2176]{1,0:T(8,128)(2,1)S(1)} %get-tuple-element.90), channel_id=1, source_target_pairs={{0,6},{1,7},{2,0},{3,1},{4,2},{5,3},{6,4},{7,5},{8,14},{9,15},{10,... | collective-permute-start | bytes 1671176 | tf_op jit(solution)/shard_map/ppermute | solution.py:513
  178.8 8.4 %expert.7 = (bf16[256,2176]{1,0:T(8,128)(2,1)S(1)}, bf16[256,2176]{1,0:T(8,128)(2,1)S(1)}) custom-call(bf16[128,2176]{1,0:T(8,128)(2,1)S(1)} %collective-permute-done.16.refs_0_, bf16[128,2176]{1,0:T(8,128)(2,1)S(1)} %collective-permute-done.17.refs_1_, bf16[128,2176]{1,0:T(8,128)(2,1)S(1)} %collective-permute-done.26.refs_2_, ...), custom_call_target="tpu_custom_call" | custom-call | flops 5989466112 | bytes 15466496 | tf_op jit(solution)/shard_map/expert/pallas_call | solution.py:462
  187.3 4.2 %collective-permute-done.24 = bf16[128,2176]{1,0:T(8,128)(2,1)S(1)} collective-permute-done((bf16[128,2176]{1,0:T(8,128)(2,1)S(1)}, bf16[128,2176]{1,0:T(8,128)(2,1)S(1)}, u32[]{:S(2)}, u32[]{:S(2)}) %collective-permute-start.24) | collective-permute-done | bytes 557088 | tf_op jit(solution)/shard_map/ppermute | solution.py:508
  191.5 2.8 %collective-permute-done.28 = bf16[256,2176]{1,0:T(8,128)(2,1)S(1)} collective-permute-done((bf16[256,2176]{1,0:T(8,128)(2,1)S(1)}, bf16[256,2176]{1,0:T(8,128)(2,1)S(1)}, u32[]{:S(2)}, u32[]{:S(2)}) %collective-permute-start.28) | collective-permute-done | bytes 1114144 | tf_op jit(solution)/shard_map/ppermute | solution.py:518
  194.7 3.2 %collective-permute-start.30 = (bf16[128,2176]{1,0:T(8,128)(2,1)S(1)}, bf16[128,2176]{1,0:T(8,128)(2,1)S(1)}, u32[]{:S(2)}, u32[]{:S(2)}) collective-permute-start(bf16[128,2176]{1,0:T(8,128)(2,1)S(1)} %get-tuple-element.101), channel_id=1, source_target_pairs={{0,6},{1,7},{2,0},{3,1},{4,2},{5,3},{6,4},{7,5},{8,14},{9,15},{10,... | collective-permute-start | bytes 1671176 | tf_op jit(solution)/shard_map/ppermute | solution.py:513
  197.9 12.6 %collective-permute-done.29.top_before = bf16[128,2176]{1,0:T(8,128)(2,1)S(1)} collective-permute-done((bf16[128,2176]{1,0:T(8,128)(2,1)S(1)}, bf16[128,2176]{1,0:T(8,128)(2,1)S(1)}, u32[]{:S(2)}, u32[]{:S(2)}) %collective-permute-start.29) | collective-permute-done | bytes 557088 | tf_op jit(solution)/shard_map/ppermute | solution.py:508
  210.6 1.6 settle.1
  212.2 3.8 %all-to-all-start.3 = ((bf16[16,16,2176]{2,1,0:T(8,128)(2,1)}), bf16[16,16,2176]{2,1,0:T(8,128)(2,1)S(1)}, u32[]{:S(2)}, u32[]{:S(2)}) async-start(bf16[16,16,2176]{2,1,0:T(8,128)(2,1)} %bitcast.29), calls=%async_computation.3 | async-start | bytes 2228224 | tf_op jit(solution)/shard_map/all_to_all | solution.py:662
  216.1 18.0 %all-to-all-done.3 = bf16[16,16,2176]{2,1,0:T(8,128)(2,1)S(1)} async-done(((bf16[16,16,2176]{2,1,0:T(8,128)(2,1)}), bf16[16,16,2176]{2,1,0:T(8,128)(2,1)S(1)}, u32[]{:S(2)}, u32[]{:S(2)}) %all-to-all-start.3) | async-done | bytes 1114144 | tf_op jit(solution)/shard_map/all_to_all | solution.py:662
  234.1 1.7 combine.1
  235.8 1.3 copy.56
  (126 shorter events, 17.8 us)
Async XLA Ops:
  1.5 14.0 %copy-start.22 = (bf16[512,2,128]{2,1,0:T(2,128)(2,1)S(1)}, bf16[512,2,128]{2,1,0:T(2,128)(2,1)}, u32[]{:S(2)}) copy-start(bf16[512,2,128]{2,1,0:T(2,128)(2,1)} %param.20) | copy-start | bytes 786436
  7.4 8.2 %copy-start.17 = (f32[2,512,128]{2,1,0:T(8,128)}, f32[2,512,128]{2,1,0:T(8,128)S(1)}, u32[]{:S(2)}) copy-start(f32[2,512,128]{2,1,0:T(8,128)S(1)} %get-tuple-element.56.first) | copy-start | bytes 1572868
  7.4 8.2 %copy-start.28 = (f32[8]{0:T(128)S(1)}, f32[8]{0:T(128)}, u32[]{:S(2)}) copy-start(f32[8]{0:T(128)} %param.23) | copy-start | bytes 100
  7.4 17.0 %all-to-all-start = ((bf16[16,72,128]{2,1,0:T(8,128)(2,1)}), bf16[16,72,128]{2,1,0:T(8,128)(2,1)}, u32[]{:S(2)}, u32[]{:S(2)}) async-start(bf16[16,72,128]{2,1,0:T(8,128)(2,1)} %get-tuple-element.53), calls=%async_computation | async-start | bytes 589824 | tf_op jit(solution)/shard_map/all_to_all | solution.py:614
  17.1 21.4 %copy-start.1 = (bf16[512,2,512]{2,0,1:T(8,128)(2,1)}, bf16[512,2,512]{2,0,1:T(8,128)(2,1)S(1)}, u32[]{:S(2)}) copy-start(bf16[512,2,512]{2,0,1:T(8,128)(2,1)S(1)} %copy.54) | copy-start | bytes 3145732
  26.1 12.4 %all-to-all-start.1 = ((bf16[16,64,128]{2,1,0:T(8,128)(2,1)}), bf16[16,64,128]{2,1,0:T(8,128)(2,1)S(1)}, u32[]{:S(2)}, u32[]{:S(2)}) async-start(bf16[16,64,128]{2,1,0:T(8,128)(2,1)} %scan.1), calls=%async_computation.1 | async-start | bytes 524288 | tf_op jit(solution)/shard_map/all_to_all | solution.py:618
  30.0 8.5 %copy-start.12 = (f32[512]{0:T(512)S(1)}, f32[512]{0:T(512)}, u32[]{:S(2)}) copy-start(f32[512]{0:T(512)} %param.24) | copy-start | bytes 6148
  38.5 9.0 %copy-start.3 = (bf16[16,64,128]{2,1,0:T(8,128)(2,1)}, bf16[16,64,128]{2,1,0:T(8,128)(2,1)S(1)}, u32[]{:S(2)}) copy-start(bf16[16,64,128]{2,1,0:T(8,128)(2,1)S(1)} %all-to-all-done.1.entering) | copy-start | bytes 786436
  47.6 10.6 %collective-permute-start = (bf16[4,64,2048]{2,1,0:T(8,128)(2,1)}, bf16[4,64,2048]{2,1,0:T(8,128)(2,1)S(1)}, u32[]{:S(2)}, u32[]{:S(2)}) collective-permute-start(bf16[4,64,2048]{2,1,0:T(8,128)(2,1)} %get-tuple-element.58), channel_id=1, source_target_pairs={{0,1},{1,0},{2,3},{3,2},{4,5},{5,4},{6,7},{7,6},{8,9},{9,8},{10,11... | collective-permute-start | bytes 3145736 | tf_op jit(solution)/shard_map/ppermute | solution.py:518
  56.4 5.7 %collective-permute-start.1 = (bf16[4,64,2048]{2,1,0:T(8,128)(2,1)}, bf16[4,64,2048]{2,1,0:T(8,128)(2,1)}, u32[]{:S(2)}, u32[]{:S(2)}) collective-permute-start(bf16[4,64,2048]{2,1,0:T(8,128)(2,1)} %get-tuple-element.61), channel_id=1, source_target_pairs={{0,1},{1,0},{2,3},{3,2},{4,5},{5,4},{6,7},{7,6},{8,9},{9,8},{10,11... | collective-permute-start | bytes 3145736 | tf_op jit(solution)/shard_map/ppermute | solution.py:518
  59.0 23.7 %collective-permute-start.2 = (bf16[64,2048]{1,0:T(8,128)(2,1)}, bf16[64,2048]{1,0:T(8,128)(2,1)S(1)}, u32[]{:S(2)}, u32[]{:S(2)}) collective-permute-start(bf16[64,2048]{1,0:T(8,128)(2,1)} %get-tuple-element.110), channel_id=1, source_target_pairs={{0,6},{1,7},{2,0},{3,1},{4,2},{5,3},{6,4},{7,5},{8,14},{9,15},{10,... | collective-permute-start | bytes 786440 | tf_op jit(solution)/shard_map/ppermute | solution.py:513
  62.0 10.4 %collective-permute-start.3 = (bf16[64,2048]{1,0:T(8,128)(2,1)S(1)}, bf16[64,2048]{1,0:T(8,128)(2,1)S(1)}, u32[]{:S(2)}, u32[]{:S(2)}) collective-permute-start(bf16[64,2048]{1,0:T(8,128)(2,1)S(1)} %get-tuple-element.109), channel_id=1, source_target_pairs={{0,2},{1,3},{2,4},{3,5},{4,6},{5,7},{6,0},{7,1},{8,10},{9,11},{10,... | collective-permute-start | bytes 786440 | tf_op jit(solution)/shard_map/ppermute | solution.py:508
  63.9 15.2 %copy-start.20 = (bf16[64,2,2048]{2,1,0:T(2,128)(2,1)S(1)}, bf16[64,2,2048]{2,1,0:T(2,128)(2,1)}, u32[]{:S(2)}) copy-start(bf16[64,2,2048]{2,1,0:T(2,128)(2,1)} %param.26) | copy-start | bytes 1572868
  63.9 15.2 %slice-start = ((s32[16,3]{0,1:T(4,128)}), s32[16,2]{0,1:T(2,128)S(1)}, s32[]{:S(2)}) async-start(s32[16,3]{0,1:T(4,128)} %copy-done.26), calls=%async_computation.4 | async-start | bytes 2048 | tf_op jit(solution)/shard_map/slice.1
  63.9 18.8 %collective-permute-start.5 = (bf16[64,2048]{1,0:T(8,128)(2,1)}, bf16[64,2048]{1,0:T(8,128)(2,1)}, u32[]{:S(2)}, u32[]{:S(2)}) collective-permute-start(bf16[64,2048]{1,0:T(8,128)(2,1)} %get-tuple-element.108), channel_id=1, source_target_pairs={{0,2},{1,3},{2,4},{3,5},{4,6},{5,7},{6,0},{7,1},{8,10},{9,11},{10,... | collective-permute-start | bytes 786440 | tf_op jit(solution)/shard_map/ppermute | solution.py:508
  64.5 9.1 %collective-permute-start.6 = (bf16[64,2048]{1,0:T(8,128)(2,1)S(1)}, bf16[64,2048]{1,0:T(8,128)(2,1)S(1)}, u32[]{:S(2)}, u32[]{:S(2)}) collective-permute-start(bf16[64,2048]{1,0:T(8,128)(2,1)S(1)} %get-tuple-element.107), channel_id=1, source_target_pairs={{0,6},{1,7},{2,0},{3,1},{4,2},{5,3},{6,4},{7,5},{8,14},{9,15},{10,... | collective-permute-start | bytes 786440 | tf_op jit(solution)/shard_map/ppermute | solution.py:513
  73.2 11.0 %copy-start.5 = (f32[2048]{0:T(1024)S(1)}, f32[2048]{0:T(1024)}, u32[]{:S(2)}) copy-start(f32[2048]{0:T(1024)} %param.27) | copy-start | bytes 24580
  73.2 9.4 %collective-permute-start.4 = (bf16[64,2048]{1,0:T(8,128)(2,1)}, bf16[64,2048]{1,0:T(8,128)(2,1)}, u32[]{:S(2)}, u32[]{:S(2)}) collective-permute-start(bf16[64,2048]{1,0:T(8,128)(2,1)} %fusion.1), channel_id=1, source_target_pairs={{0,2},{1,3},{2,4},{3,5},{4,6},{5,7},{6,0},{7,1},{8,10},{9,11},{10,... | collective-permute-start | bytes 786440 | tf_op jit(solution)/shard_map/ppermute | solution.py:508
  75.4 8.9 %collective-permute-start.7 = (bf16[64,2048]{1,0:T(8,128)(2,1)}, bf16[64,2048]{1,0:T(8,128)(2,1)}, u32[]{:S(2)}, u32[]{:S(2)}) collective-permute-start(bf16[64,2048]{1,0:T(8,128)(2,1)} %fusion), channel_id=1, source_target_pairs={{0,6},{1,7},{2,0},{3,1},{4,2},{5,3},{6,4},{7,5},{8,14},{9,15},{10,... | collective-permute-start | bytes 786440 | tf_op jit(solution)/shard_map/ppermute | solution.py:513
  85.3 26.2 %copy-start.7 = (bf16[1,2048,896]{2,1,0:T(8,128)(2,1)S(1)}, bf16[1,2048,896]{2,1,0:T(8,128)(2,1)}, u32[]{:S(2)}) copy-start(bf16[1,2048,896]{2,1,0:T(8,128)(2,1)} %param.29) | copy-start | bytes 11010052
  87.6 20.0 %copy-start.9 = (f32[128,2048]{1,0:T(8,128)}, f32[128,2048]{1,0:T(8,128)S(1)}, u32[]{:S(2)}) copy-start(f32[128,2048]{1,0:T(8,128)S(1)} %get-tuple-element.100.hidden) | copy-start | bytes 3145732
  87.6 24.0 %copy-start.6 = (bf16[1,2048,896]{2,1,0:T(8,128)(2,1)S(1)}, bf16[1,2048,896]{2,1,0:T(8,128)(2,1)}, u32[]{:S(2)}) copy-start(bf16[1,2048,896]{2,1,0:T(8,128)(2,1)} %param.28) | copy-start | bytes 11010052
  107.6 3.9 %collective-permute-start.10 = (bf16[256,2176]{1,0:T(8,128)(2,1)S(1)}, bf16[256,2176]{1,0:T(8,128)(2,1)S(1)}, u32[]{:S(2)}, u32[]{:S(2)}) collective-permute-start(bf16[256,2176]{1,0:T(8,128)(2,1)S(1)} %bitcast.81), channel_id=1, source_target_pairs={{0,1},{1,0},{2,3},{3,2},{4,5},{5,4},{6,7},{7,6},{8,9},{9,8},{10,11... | collective-permute-start | bytes 3342344 | tf_op jit(solution)/shard_map/ppermute | solution.py:518
  107.7 17.1 %collective-permute-start.8 = (bf16[128,2176]{1,0:T(8,128)(2,1)S(1)}, bf16[128,2176]{1,0:T(8,128)(2,1)S(1)}, u32[]{:S(2)}, u32[]{:S(2)}) collective-permute-start(bf16[128,2176]{1,0:T(8,128)(2,1)S(1)} %bitcast.118), channel_id=1, source_target_pairs={{0,2},{1,3},{2,4},{3,5},{4,6},{5,7},{6,0},{7,1},{8,10},{9,11},{10,... | collective-permute-start | bytes 1671176 | tf_op jit(solution)/shard_map/ppermute | solution.py:508
  107.8 17.0 %collective-permute-start.9 = (bf16[128,2176]{1,0:T(8,128)(2,1)S(1)}, bf16[128,2176]{1,0:T(8,128)(2,1)S(1)}, u32[]{:S(2)}, u32[]{:S(2)}) collective-permute-start(bf16[128,2176]{1,0:T(8,128)(2,1)S(1)} %bitcast.116), channel_id=1, source_target_pairs={{0,6},{1,7},{2,0},{3,1},{4,2},{5,3},{6,4},{7,5},{8,14},{9,15},{10,... | collective-permute-start | bytes 1671176 | tf_op jit(solution)/shard_map/ppermute | solution.py:513
  124.8 3.8 %collective-permute-start.14 = (bf16[128,2176]{1,0:T(8,128)(2,1)S(1)}, bf16[128,2176]{1,0:T(8,128)(2,1)S(1)}, u32[]{:S(2)}, u32[]{:S(2)}) collective-permute-start(bf16[128,2176]{1,0:T(8,128)(2,1)S(1)} %collective-permute-done.8.refs_0_), channel_id=1, source_target_pairs={{0,1},{1,0},{2,3},{3,2},{4,5},{5,4},{6,7},{7,6},{8,9},{9,8},{10,11... | collective-permute-start | bytes 1671176 | tf_op jit(solution)/shard_map/ppermute | solution.py:518
  124.8 3.8 %collective-permute-start.15 = (bf16[128,2176]{1,0:T(8,128)(2,1)S(1)}, bf16[128,2176]{1,0:T(8,128)(2,1)S(1)}, u32[]{:S(2)}, u32[]{:S(2)}) collective-permute-start(bf16[128,2176]{1,0:T(8,128)(2,1)S(1)} %collective-permute-done.9.refs_1_), channel_id=1, source_target_pairs={{0,1},{1,0},{2,3},{3,2},{4,5},{5,4},{6,7},{7,6},{8,9},{9,8},{10,11... | collective-permute-start | bytes 1671176 | tf_op jit(solution)/shard_map/ppermute | solution.py:518
  125.3 16.3 %collective-permute-start.13 = (bf16[256,2176]{1,0:T(8,128)(2,1)S(1)}, bf16[256,2176]{1,0:T(8,128)(2,1)S(1)}, u32[]{:S(2)}, u32[]{:S(2)}) collective-permute-start(bf16[256,2176]{1,0:T(8,128)(2,1)S(1)} %get-tuple-element.68), channel_id=1, source_target_pairs={{0,1},{1,0},{2,3},{3,2},{4,5},{5,4},{6,7},{7,6},{8,9},{9,8},{10,11... | collective-permute-start | bytes 3342344 | tf_op jit(solution)/shard_map/ppermute | solution.py:518
  125.3 16.3 %collective-permute-start.11 = (bf16[128,2176]{1,0:T(8,128)(2,1)S(1)}, bf16[128,2176]{1,0:T(8,128)(2,1)S(1)}, u32[]{:S(2)}, u32[]{:S(2)}) collective-permute-start(bf16[128,2176]{1,0:T(8,128)(2,1)S(1)} %collective-permute-done.8.refs_0_), channel_id=1, source_target_pairs={{0,2},{1,3},{2,4},{3,5},{4,6},{5,7},{6,0},{7,1},{8,10},{9,11},{10,... | collective-permute-start | bytes 1671176 | tf_op jit(solution)/shard_map/ppermute | solution.py:508
  126.4 15.2 %collective-permute-start.12 = (bf16[128,2176]{1,0:T(8,128)(2,1)S(1)}, bf16[128,2176]{1,0:T(8,128)(2,1)S(1)}, u32[]{:S(2)}, u32[]{:S(2)}) collective-permute-start(bf16[128,2176]{1,0:T(8,128)(2,1)S(1)} %collective-permute-done.9.refs_1_), channel_id=1, source_target_pairs={{0,6},{1,7},{2,0},{3,1},{4,2},{5,3},{6,4},{7,5},{8,14},{9,15},{10,... | collective-permute-start | bytes 1671176 | tf_op jit(solution)/shard_map/ppermute | solution.py:513
  141.6 3.5 %collective-permute-start.18 = (bf16[256,2176]{1,0:T(8,128)(2,1)S(1)}, bf16[256,2176]{1,0:T(8,128)(2,1)S(1)}, u32[]{:S(2)}, u32[]{:S(2)}) collective-permute-start(bf16[256,2176]{1,0:T(8,128)(2,1)S(1)} %get-tuple-element.75), channel_id=1, source_target_pairs={{0,1},{1,0},{2,3},{3,2},{4,5},{5,4},{6,7},{7,6},{8,9},{9,8},{10,11... | collective-permute-start | bytes 3342344 | tf_op jit(solution)/shard_map/ppermute | solution.py:518
  141.6 15.9 %collective-permute-start.16 = (bf16[128,2176]{1,0:T(8,128)(2,1)S(1)}, bf16[128,2176]{1,0:T(8,128)(2,1)S(1)}, u32[]{:S(2)}, u32[]{:S(2)}) collective-permute-start(bf16[128,2176]{1,0:T(8,128)(2,1)S(1)} %bitcast.119), channel_id=1, source_target_pairs={{0,6},{1,7},{2,0},{3,1},{4,2},{5,3},{6,4},{7,5},{8,14},{9,15},{10,... | collective-permute-start | bytes 1671176 | tf_op jit(solution)/shard_map/ppermute | solution.py:513
  144.6 16.7 %collective-permute-start.17 = (bf16[128,2176]{1,0:T(8,128)(2,1)S(1)}, bf16[128,2176]{1,0:T(8,128)(2,1)S(1)}, u32[]{:S(2)}, u32[]{:S(2)}) collective-permute-start(bf16[128,2176]{1,0:T(8,128)(2,1)S(1)} %bitcast.117), channel_id=1, source_target_pairs={{0,2},{1,3},{2,4},{3,5},{4,6},{5,7},{6,0},{7,1},{8,10},{9,11},{10,... | collective-permute-start | bytes 1671176 | tf_op jit(solution)/shard_map/ppermute | solution.py:508
  144.6 4.1 %collective-permute-start.21 = (bf16[128,2176]{1,0:T(8,128)(2,1)S(1)}, bf16[128,2176]{1,0:T(8,128)(2,1)S(1)}, u32[]{:S(2)}, u32[]{:S(2)}) collective-permute-start(bf16[128,2176]{1,0:T(8,128)(2,1)S(1)} %collective-permute-done.11.refs_0_), channel_id=1, source_target_pairs={{0,1},{1,0},{2,3},{3,2},{4,5},{5,4},{6,7},{7,6},{8,9},{9,8},{10,11... | collective-permute-start | bytes 1671176 | tf_op jit(solution)/shard_map/ppermute | solution.py:518
  144.8 3.9 %collective-permute-start.22 = (bf16[128,2176]{1,0:T(8,128)(2,1)S(1)}, bf16[128,2176]{1,0:T(8,128)(2,1)S(1)}, u32[]{:S(2)}, u32[]{:S(2)}) collective-permute-start(bf16[128,2176]{1,0:T(8,128)(2,1)S(1)} %collective-permute-done.12.refs_1_), channel_id=1, source_target_pairs={{0,1},{1,0},{2,3},{3,2},{4,5},{5,4},{6,7},{7,6},{8,9},{9,8},{10,11... | collective-permute-start | bytes 1671176 | tf_op jit(solution)/shard_map/ppermute | solution.py:518
  145.4 23.7 %collective-permute-start.19 = (bf16[128,2176]{1,0:T(8,128)(2,1)S(1)}, bf16[128,2176]{1,0:T(8,128)(2,1)S(1)}, u32[]{:S(2)}, u32[]{:S(2)}) collective-permute-start(bf16[128,2176]{1,0:T(8,128)(2,1)S(1)} %get-tuple-element.78), channel_id=1, source_target_pairs={{0,6},{1,7},{2,0},{3,1},{4,2},{5,3},{6,4},{7,5},{8,14},{9,15},{10,... | collective-permute-start | bytes 1671176 | tf_op jit(solution)/shard_map/ppermute | solution.py:513
  148.7 23.8 %collective-permute-start.20 = (bf16[128,2176]{1,0:T(8,128)(2,1)S(1)}, bf16[128,2176]{1,0:T(8,128)(2,1)S(1)}, u32[]{:S(2)}, u32[]{:S(2)}) collective-permute-start(bf16[128,2176]{1,0:T(8,128)(2,1)S(1)} %get-tuple-element.79), channel_id=1, source_target_pairs={{0,2},{1,3},{2,4},{3,5},{4,6},{5,7},{6,0},{7,1},{8,10},{9,11},{10,... | collective-permute-start | bytes 1671176 | tf_op jit(solution)/shard_map/ppermute | solution.py:508
  172.5 2.8 %collective-permute-start.23 = (bf16[256,2176]{1,0:T(8,128)(2,1)S(1)}, bf16[256,2176]{1,0:T(8,128)(2,1)S(1)}, u32[]{:S(2)}, u32[]{:S(2)}) collective-permute-start(bf16[256,2176]{1,0:T(8,128)(2,1)S(1)} %get-tuple-element.86), channel_id=1, source_target_pairs={{0,1},{1,0},{2,3},{3,2},{4,5},{5,4},{6,7},{7,6},{8,9},{9,8},{10,11... | collective-permute-start | bytes 3342344 | tf_op jit(solution)/shard_map/ppermute | solution.py:518
  172.5 6.3 %collective-permute-start.26 = (bf16[128,2176]{1,0:T(8,128)(2,1)S(1)}, bf16[128,2176]{1,0:T(8,128)(2,1)S(1)}, u32[]{:S(2)}, u32[]{:S(2)}) collective-permute-start(bf16[128,2176]{1,0:T(8,128)(2,1)S(1)} %collective-permute-done.16.refs_0_), channel_id=1, source_target_pairs={{0,1},{1,0},{2,3},{3,2},{4,5},{5,4},{6,7},{7,6},{8,9},{9,8},{10,11... | collective-permute-start | bytes 1671176 | tf_op jit(solution)/shard_map/ppermute | solution.py:518
  173.0 5.8 %collective-permute-start.27 = (bf16[128,2176]{1,0:T(8,128)(2,1)S(1)}, bf16[128,2176]{1,0:T(8,128)(2,1)S(1)}, u32[]{:S(2)}, u32[]{:S(2)}) collective-permute-start(bf16[128,2176]{1,0:T(8,128)(2,1)S(1)} %collective-permute-done.17.refs_1_), channel_id=1, source_target_pairs={{0,1},{1,0},{2,3},{3,2},{4,5},{5,4},{6,7},{7,6},{8,9},{9,8},{10,11... | collective-permute-start | bytes 1671176 | tf_op jit(solution)/shard_map/ppermute | solution.py:518
  175.5 15.9 %collective-permute-start.24 = (bf16[128,2176]{1,0:T(8,128)(2,1)S(1)}, bf16[128,2176]{1,0:T(8,128)(2,1)S(1)}, u32[]{:S(2)}, u32[]{:S(2)}) collective-permute-start(bf16[128,2176]{1,0:T(8,128)(2,1)S(1)} %get-tuple-element.89), channel_id=1, source_target_pairs={{0,2},{1,3},{2,4},{3,5},{4,6},{5,7},{6,0},{7,1},{8,10},{9,11},{10,... | collective-permute-start | bytes 1671176 | tf_op jit(solution)/shard_map/ppermute | solution.py:508
  175.6 15.9 %collective-permute-start.25 = (bf16[128,2176]{1,0:T(8,128)(2,1)S(1)}, bf16[128,2176]{1,0:T(8,128)(2,1)S(1)}, u32[]{:S(2)}, u32[]{:S(2)}) collective-permute-start(bf16[128,2176]{1,0:T(8,128)(2,1)S(1)} %get-tuple-element.90), channel_id=1, source_target_pairs={{0,6},{1,7},{2,0},{3,1},{4,2},{5,3},{6,4},{7,5},{8,14},{9,15},{10,... | collective-permute-start | bytes 1671176 | tf_op jit(solution)/shard_map/ppermute | solution.py:513
  191.5 2.8 %collective-permute-start.28 = (bf16[256,2176]{1,0:T(8,128)(2,1)S(1)}, bf16[256,2176]{1,0:T(8,128)(2,1)S(1)}, u32[]{:S(2)}, u32[]{:S(2)}) collective-permute-start(bf16[256,2176]{1,0:T(8,128)(2,1)S(1)} %get-tuple-element.96), channel_id=1, source_target_pairs={{0,1},{1,0},{2,3},{3,2},{4,5},{5,4},{6,7},{7,6},{8,9},{9,8},{10,11... | collective-permute-start | bytes 3342344 | tf_op jit(solution)/shard_map/ppermute | solution.py:518
  194.6 15.9 %collective-permute-start.29 = (bf16[128,2176]{1,0:T(8,128)(2,1)S(1)}, bf16[128,2176]{1,0:T(8,128)(2,1)S(1)}, u32[]{:S(2)}, u32[]{:S(2)}) collective-permute-start(bf16[128,2176]{1,0:T(8,128)(2,1)S(1)} %get-tuple-element.102), channel_id=1, source_target_pairs={{0,2},{1,3},{2,4},{3,5},{4,6},{5,7},{6,0},{7,1},{8,10},{9,11},{10,... | collective-permute-start | bytes 1671176 | tf_op jit(solution)/shard_map/ppermute | solution.py:508
  194.7 15.9 %collective-permute-start.30 = (bf16[128,2176]{1,0:T(8,128)(2,1)S(1)}, bf16[128,2176]{1,0:T(8,128)(2,1)S(1)}, u32[]{:S(2)}, u32[]{:S(2)}) collective-permute-start(bf16[128,2176]{1,0:T(8,128)(2,1)S(1)} %get-tuple-element.101), channel_id=1, source_target_pairs={{0,6},{1,7},{2,0},{3,1},{4,2},{5,3},{6,4},{7,5},{8,14},{9,15},{10,... | collective-permute-start | bytes 1671176 | tf_op jit(solution)/shard_map/ppermute | solution.py:513
  212.2 21.9 %copy-start.10 = (f32[128,2048]{1,0:T(8,128)S(1)}, f32[128,2048]{1,0:T(8,128)}, u32[]{:S(2)}) copy-start(f32[128,2048]{1,0:T(8,128)} %copy-done.9) | copy-start | bytes 3145732
  212.2 21.9 %copy-start.11 = (f32[4,2048]{1,0:T(4,128)S(1)}, f32[4,2048]{1,0:T(4,128)}, u32[]{:S(2)}) copy-start(f32[4,2048]{1,0:T(4,128)} %directions.1) | copy-start | bytes 98308
  212.2 21.9 %all-to-all-start.3 = ((bf16[16,16,2176]{2,1,0:T(8,128)(2,1)}), bf16[16,16,2176]{2,1,0:T(8,128)(2,1)S(1)}, u32[]{:S(2)}, u32[]{:S(2)}) async-start(bf16[16,16,2176]{2,1,0:T(8,128)(2,1)} %bitcast.29), calls=%async_computation.3 | async-start | bytes 2228224 | tf_op jit(solution)/shard_map/all_to_all | solution.py:662
  (16 other events, 44.2 us)

commit v3 on v1

--- a/solution.py
+++ b/solution.py
@@ -35,6 +35,18 @@
     return row >= col
 
 
+def running_sums(decays):
+    heads = decays.shape[0]
+    high, rest = two_parts(decays)
+    middle, low = two_parts(decays - high.astype(F32))
+    parts = jnp.concatenate(
+        [high.astype(F32), middle.astype(F32), low.astype(F32)], axis=0
+    ).astype(BF16)
+    ones = jnp.where(triangle(), 1.0, 0.0).astype(BF16)
+    sums = dot_last(parts, ones)
+    return sums[:heads] + sums[heads : 2 * heads] + sums[2 * heads :]
+
+
 def spread_heads(columns, heads):
     rows = columns.shape[0]
     lane = lax.broadcasted_iota(jnp.int32, (rows, 2 * HEAD_DIM), 1)
@@ -56,9 +68,7 @@
 def contrib_kernel(decay, step, inputs, writes, parcel, first, total, running):
     block = pl.program_id(1)
     heads = decay.shape[1]
-    ones = triangle().astype(F32)
-    decays = decay[0]
-    cum_row = dot_last(decays, ones, precision=lax.Precision.HIGHEST)
+    cum_row = running_sums(decay[0])
     end_row = jnp.broadcast_to(cum_row[:, BLOCK - 1 :], (heads, STATE))
     to_end_row = jnp.exp(cum_row[:, BLOCK - 1 :] - cum_row) * step[0]
     to_end = jnp.transpose(to_end_row)
@@ -124,13 +134,17 @@
     )(decays, steps, inputs, writes)
 
 
-def within_kernel(decay, step, inputs, writes, reads, skip, within):
+def within_kernel(decay, step, inputs, writes, reads, skip, first, within, factor):
+    block = pl.program_id(0)
     heads = decay.shape[1]
     causal = triangle()
-    ones = causal.astype(F32)
     log2e = 1.4426950408889634
-    decays = decay[0]
-    cum_row = dot_last(decays, ones, precision=lax.Precision.HIGHEST) * log2e
+    later = block > 0
+    decays = jnp.where(later, decay[0, :, BLOCK:], decay[0, :, :BLOCK])
+    ended = jnp.where(later, jnp.sum(decay[0, :, :BLOCK], axis=1, keepdims=True), 0.0)
+    plain_row = running_sums(decays)
+    factor[0] = jnp.transpose(jnp.exp(plain_row + ended))
+    cum_row = plain_row * log2e
     cum_col = jnp.transpose(cum_row)
     steps = step[0]
     scores = dot_last(reads[0], writes[0])
@@ -152,23 +166,37 @@
             )
         within[0, :, start * HEAD_DIM : start * HEAD_DIM + quad] = total
 
-
-def within_call(which, decays, steps, inputs, writes, reads, skip):
+    @pl.when(later)
+    def _():
+        high, low = two_parts(first[0])
+        readout = dot_last(reads[0], high) + dot_last(reads[0], low)
+        within[0] = within[0] + spread_heads(jnp.exp2(cum_col), heads) * readout
+
+
+def within_call(which, decays, steps, inputs, writes, reads, skip, first):
     seqs, heads, length = decays.shape
     width = inputs.shape[2]
+    assert length == 2 * BLOCK
     return pl.pallas_call(
         within_kernel,
         grid=(length // BLOCK,),
         in_specs=[
-            pl.BlockSpec((1, heads, BLOCK), lambda c: (which, 0, c)),
+            pl.BlockSpec((1, heads, length), lambda c: (which, 0, 0)),
             pl.BlockSpec((1, heads, BLOCK), lambda c: (which, 0, c)),
             pl.BlockSpec((1, BLOCK, width), lambda c: (which, c, 0)),
             pl.BlockSpec((1, BLOCK, STATE), lambda c: (which, c, 0)),
             pl.BlockSpec((1, BLOCK, STATE), lambda c: (which, c, 0)),
             pl.BlockSpec((1, width), lambda c: (0, 0)),
-        ],
-        out_specs=pl.BlockSpec((1, BLOCK, width), lambda c: (0, c, 0)),
-        out_shape=jax.ShapeDtypeStruct((1, length, width), F32),
+            pl.BlockSpec((1, width, STATE), lambda c: (which, 0, 0)),
+        ],
+        out_specs=[
+            pl.BlockSpec((1, BLOCK, width), lambda c: (0, c, 0)),
+            pl.BlockSpec((1, BLOCK, heads), lambda c: (0, c, 0)),
+        ],
+        out_shape=[
+            jax.ShapeDtypeStruct((1, length, width), F32),
+            jax.ShapeDtypeStruct((1, length, heads), F32),
+        ],
         compiler_params=pltpu.CompilerParams(
             dimension_semantics=("arbitrary",), vmem_limit_bytes=16 * 2**20
         ),
@@ -176,7 +204,7 @@
             flops=3 * 10**9, bytes_accessed=2 * 2**20, transcendentals=2**20
         ),
         name="within",
-    )(decays, steps, inputs, writes, reads, skip)
+    )(decays, steps, inputs, writes, reads, skip, first)
 
 
 def scan_kernel(parcels, states):
@@ -201,26 +229,15 @@
 
 
 def mixer_kernel(
-    place, decay, reads, entering, first, within, gate, gain, weight, kept, passed, held, sems
+    place, factors, reads, entering, within, gate, gain, weight, kept, passed, held, sems
 ):
     block = pl.program_id(0)
     blocks = pl.num_programs(0)
-    heads = decay.shape[1]
+    heads = factors.shape[2]
     width = gate.shape[2]
     chips, keep = kept.shape[0], kept.shape[1]
-    ones = triangle().astype(F32)
-    decays = decay[0]
-    before = block > 0
-    cum_row = dot_last(decays[:, BLOCK:], ones, precision=lax.Precision.HIGHEST)
-    head_row = dot_last(decays[:, :BLOCK], ones, precision=lax.Precision.HIGHEST)
-    prefix = jnp.exp(jnp.broadcast_to(head_row[:, BLOCK - 1 :], (heads, STATE)))
-    arrived = entering[...].astype(F32).reshape(width, STATE)
-    begin = jnp.where(before, over_rows(prefix) * arrived + first[0], arrived)
-    cum = jnp.transpose(jnp.exp(jnp.where(before, cum_row, head_row)))
-    high, low = two_parts(begin)
-    vectors = reads[0]
-    readout = dot_last(vectors, high) + dot_last(vectors, low)
-    ssd_out = within[0] + spread_heads(cum, heads) * readout
+    readout = dot_last(reads[0], entering[...].reshape(width, STATE))
+    ssd_out = within[0] + spread_heads(factors[0], heads) * readout
     gates = gate[0].astype(F32)
     gated = ssd_out * (gates / (1.0 + jnp.exp(-gates)))
     factor = lax.rsqrt(jnp.mean(gated * gated, axis=-1, keepdims=True) + 1e-05)
@@ -253,8 +270,8 @@
                 piece(step, index, kept).wait()
 
 
-def mixer_call(which, place, decays, reads, entering, first, within, gate, gain, weight, columns):
-    seqs, heads, length = decays.shape
+def mixer_call(which, place, factors, reads, entering, within, gate, gain, weight, columns):
+    _, length, heads = factors.shape
     width = gate.shape[2]
     blocks = length // BLOCK
     keep = length // columns
@@ -264,10 +281,9 @@
         grid=(blocks,),
         in_specs=[
             pl.BlockSpec(memory_space=pltpu.SMEM),
-            pl.BlockSpec((1, heads, length), lambda c: (which, 0, 0)),
+            pl.BlockSpec((1, BLOCK, heads), lambda c: (0, c, 0)),
             pl.BlockSpec((1, BLOCK, STATE), lambda c: (which, c, 0)),
             pl.BlockSpec((heads, HEAD_DIM, STATE), lambda c: (which, 0, 0)),
-            pl.BlockSpec((1, width, STATE), lambda c: (which, 0, 0)),
             pl.BlockSpec((1, BLOCK, width), lambda c: (0, c, 0)),
             pl.BlockSpec((1, BLOCK, width), lambda c: (which, c, 0)),
             pl.BlockSpec((1, width), lambda c: (0, 0)),
@@ -286,7 +302,7 @@
             flops=2 * 10**9, bytes_accessed=6 * 2**20, transcendentals=2**18
         ),
         name="mixer",
-    )(place, decays, reads, entering, first, within, gate, gain, weight)
+    )(place, factors, reads, entering, within, gate, gain, weight)
 
 
 def unfold(rows, folded):
@@ -569,7 +585,9 @@
     relay_top = from_before(far_top)
     relay_bottom = from_after(far_bottom)
     kept, passed = call((after_top, before_bottom, *late))
-    relay_top, relay_bottom, kept, passed = after((relay_top, relay_bottom, kept, passed))
+    relay_top, relay_bottom, top_after, bottom_before, kept, passed = after(
+        (relay_top, relay_bottom, top_after, bottom_before, kept, passed)
+    )
     got = from_sibling(passed)
     top_before = from_before(add_up(kept[:half], got[:half], relay_top))
     bottom_after = from_after(add_up(kept[half:], got[half:], relay_bottom))
@@ -611,23 +629,26 @@
     parcel, first = contrib_call(decays, steps, inputs, writes)
     parcels = lax.all_to_all(parcel, "seq", split_axis=0, concat_axis=0, tiled=True)
     skip = jnp.repeat(skip_gain, HEAD_DIM)[None, :]
-    within_early = within_call(0, decays, steps, inputs, writes, reads, skip)
+    within_early, factor_early = within_call(
+        0, decays, steps, inputs, writes, reads, skip, first
+    )
     (parcels,) = after((parcels,), within_early)
     entering = lax.all_to_all(
         scan_call(parcels), "seq", split_axis=0, concat_axis=0, tiled=True
     )
-    within_late = within_call(1, decays, steps, inputs, writes, reads, skip)
+    within_late, factor_late = within_call(
+        1, decays, steps, inputs, writes, reads, skip, first
+    )
     gating = swap(ssd_gate)
     (entering,) = after((entering,), within_late, gating)
     place = lax.axis_index("exp").astype(jnp.int32)[None]
-    shared = (decays, reads, entering, first)
     kept, passed = mixer_call(
-        0, place, *shared, within_early, gating, norm_gain[None, :], w_out, columns
+        0, place, factor_early, reads, entering, within_early, gating, norm_gain[None, :], w_out, columns
     )
     got = from_sibling(passed)
     (place,) = after((place,), kept)
     kept_late, passed = mixer_call(
-        1, place, *shared, within_late, gating, norm_gain[None, :], w_out, columns
+        1, place, factor_late, reads, entering, within_late, gating, norm_gain[None, :], w_out, columns
     )
     got_late = from_sibling(passed)
     relay_top = from_before(add_up(kept[2], got[2]))

time: 236 us -> 231 us (0.979)
  Pallas kernels: 62.6 us -> 58.8 us
    ppermute x9, waiting for transfers between devices: 12.5 us -> 4.04 us  [from_after(): lax.ppermute(values, 'exp', [(i, (i - 2) % size) for i in range(size)])]
    ppermute x9, waiting for transfers between devices: 35.1 us -> 41.3 us  [from_before(): lax.ppermute(values, 'exp', [(i, (i + 2) % size) for i in range(size)])]
    ppermute x9, starting transfers between devices: 27.7 us -> 23.6 us  [from_after(): lax.ppermute(values, 'exp', [(i, (i - 2) % size) for i in range(size)])]
    unnamed x66 -> x72, local copies, waits for them, and re-layouts: 14.1 us -> 16.1 us
  transfers between devices with their start and end apart: 34 -> 34, of which waited for: 17 -> 19; matrix products, arithmetic and copies ran while one was open for 5% -> 5% of each run, Pallas kernels for 19% -> 18%
where the time goes in v3:
time: 231 us; the launch traced here: 230 us
  waiting for transfers between devices  76 us (33%)
  Pallas kernels  58.8 us (25%)
  starting transfers between devices  45.8 us (20%)
  local copies, waits for them, and re-layouts  21 us (9%)
  blocking collectives  20.1 us (9%)
  other arithmetic  7.79 us (3%)
    ppermute x9, waiting for transfers between devices, from_before(): lax.ppermute(values, 'exp', [(i, (i + 2) % size) for i in range(size)])  41.3 us
    pallas_call x4, Pallas kernels, expert_call(): pl.pallas_call(functools.partial(expert_kernel, counts), in_specs=[anywhe...  33.8 us
    ppermute x9, starting transfers between devices, from_after(): lax.ppermute(values, 'exp', [(i, (i - 2) % size) for i in range(size)])  23.6 us
    all_to_all x1, blocking collectives, on_device(): lax.all_to_all(packed.reshape(experts, FOLD, D + 128), 'seq', split_axis=...  20.1 us
    all_to_all x1, waiting for transfers between devices, on_device(): lax.all_to_all(summed.reshape(experts, FOLD, D + 128), 'seq', split_axis=...  18 us
    unnamed x72, local copies, waits for them, and re-layouts  16.1 us
    pallas_call x2, Pallas kernels, mixer_call(): pl.pallas_call(mixer_kernel, grid=(blocks,), in_specs=[pl.BlockSpec(memor...  8.37 us
    all_to_all x1, starting transfers between devices, on_device(): lax.all_to_all(parcel, 'seq', split_axis=0, concat_axis=0, tiled=True)  7.97 us
  transfers between devices with their start and end apart: 34, of which 19 were waited for; matrix products, arithmetic and copies ran while one was open for 5% of the time, Pallas kernels for 18%

profile of v3, /device:TPU:0, one launch (start us, length us, event | category | flops | bytes accessed | tf_op | source)
XLA Modules:
  0.0 229.9 jit_solution(4908224316856969596)
XLA Ops:
  0.0 1.4 copy.55
  1.6 4.9 %contrib.1 = (bf16[16,72,128]{2,1,0:T(8,128)(2,1)}, f32[2,512,128]{2,1,0:T(8,128)S(1)}) custom-call(f32[2,8,512]{2,1,0:T(8,128)S(1)} %get-tuple-element.124.decay, f32[2,8,512]{2,1,0:T(8,128)S(1)} %get-tuple-element.123.step, bf16[2,512,512]{2,1,0:T(8,128)(2,1)S(1)} %bitcast.86, bf16[2,512,128]{2,1,0:T(8,128)(2,1)S(1)} %get-tuple-element.126.writes), custom_call_target="tpu_custom_call" | custom-call | flops 1000000000 | bytes 2097152 | tf_op jit(solution)/shard_map/contrib/pallas_call | solution.py:111
  6.5 8.0 %all-to-all-start = ((bf16[16,72,128]{2,1,0:T(8,128)(2,1)}), bf16[16,72,128]{2,1,0:T(8,128)(2,1)S(1)}, u32[]{:S(2)}, u32[]{:S(2)}) async-start(bf16[16,72,128]{2,1,0:T(8,128)(2,1)} %get-tuple-element.59), calls=%async_computation | async-start | bytes 589824 | tf_op jit(solution)/shard_map/all_to_all | solution.py:630
  14.6 1.4 copy.54
  16.1 2.3 within.2
  20.0 3.3 %all-to-all-done.parcels = bf16[16,72,128]{2,1,0:T(8,128)(2,1)S(1)} async-done(((bf16[16,72,128]{2,1,0:T(8,128)(2,1)}), bf16[16,72,128]{2,1,0:T(8,128)(2,1)S(1)}, u32[]{:S(2)}, u32[]{:S(2)}) %all-to-all-start) | async-done | bytes 294944 | tf_op jit(solution)/shard_map/all_to_all | solution.py:630
  24.0 1.7 scan.1
  25.8 3.9 %all-to-all-start.1 = ((bf16[16,64,128]{2,1,0:T(8,128)(2,1)}), bf16[16,64,128]{2,1,0:T(8,128)(2,1)S(1)}, u32[]{:S(2)}, u32[]{:S(2)}) async-start(bf16[16,64,128]{2,1,0:T(8,128)(2,1)} %scan.1), calls=%async_computation.1 | async-start | bytes 524288 | tf_op jit(solution)/shard_map/all_to_all | solution.py:636
  30.7 2.3 within.3
  34.7 3.5 %all-to-all-done.1.entering = bf16[16,64,128]{2,1,0:T(8,128)(2,1)S(1)} async-done(((bf16[16,64,128]{2,1,0:T(8,128)(2,1)}), bf16[16,64,128]{2,1,0:T(8,128)(2,1)S(1)}, u32[]{:S(2)}, u32[]{:S(2)}) %all-to-all-start.1) | async-done | bytes 262176 | tf_op jit(solution)/shard_map/all_to_all | solution.py:636
  38.2 1.6 copy-done.9
  39.8 1.2 copy-done.16
  41.0 4.2 %mixer.2 = (bf16[4,64,2048]{2,1,0:T(8,128)(2,1)S(1)}, bf16[4,64,2048]{2,1,0:T(8,128)(2,1)}) custom-call(s32[1]{0:T(128)} %bitcast.8.place, f32[1,512,8]{2,1,0:T(8,128)S(1)} %copy-done.22, bf16[2,512,128]{2,1,0:T(8,128)(2,1)S(1)} %get-tuple-element.125.reads, bf16[16,64,128]{2,1,0:T(8,128)(2,1)S(1)} %all-to-all-done.1.entering, ...), custom_call_target="tpu_custom_call" | custom-call | flops 2000000000 | bytes 6291456 | tf_op jit(solution)/shard_map/mixer/pallas_call | solution.py:279
  45.4 1.2 copy-done.2
  47.5 4.2 %mixer.3 = (bf16[4,64,2048]{2,1,0:T(8,128)(2,1)S(1)}, bf16[4,64,2048]{2,1,0:T(8,128)(2,1)}) custom-call(s32[1]{0:T(128)} %bitcast.8.place, f32[1,512,8]{2,1,0:T(8,128)S(1)} %copy-done.24, bf16[2,512,128]{2,1,0:T(8,128)(2,1)S(1)} %copy-done.4, bf16[16,64,128]{2,1,0:T(8,128)(2,1)S(1)} %all-to-all-done.1.entering, f32[1,512,512]{2,1,0:T(8,128)S(1)} %copy-done.18, ...), custom_call_target="tpu_custom_call" | custom-call | flops 2000000000 | bytes 6291456 | tf_op jit(solution)/shard_map/mixer/pallas_call | solution.py:279
  54.4 3.0 %collective-permute-start.2 = (bf16[64,2048]{1,0:T(8,128)(2,1)}, bf16[64,2048]{1,0:T(8,128)(2,1)S(1)}, u32[]{:S(2)}, u32[]{:S(2)}) collective-permute-start(bf16[64,2048]{1,0:T(8,128)(2,1)} %get-tuple-element.118), channel_id=1, source_target_pairs={{0,6},{1,7},{2,0},{3,1},{4,2},{5,3},{6,4},{7,5},{8,14},{9,15},{10,... | collective-permute-start | bytes 786440 | tf_op jit(solution)/shard_map/ppermute | solution.py:529
  57.4 1.9 fusion.5
  59.9 2.8 %collective-permute-start.6 = (bf16[64,2048]{1,0:T(8,128)(2,1)S(1)}, bf16[64,2048]{1,0:T(8,128)(2,1)S(1)}, u32[]{:S(2)}, u32[]{:S(2)}) collective-permute-start(bf16[64,2048]{1,0:T(8,128)(2,1)S(1)} %get-tuple-element.115), channel_id=1, source_target_pairs={{0,6},{1,7},{2,0},{3,1},{4,2},{5,3},{6,4},{7,5},{8,14},{9,15},{10,... | collective-permute-start | bytes 786440 | tf_op jit(solution)/shard_map/ppermute | solution.py:529
  62.6 5.2 %collective-permute-done.3 = bf16[64,2048]{1,0:T(8,128)(2,1)S(1)} collective-permute-done((bf16[64,2048]{1,0:T(8,128)(2,1)S(1)}, bf16[64,2048]{1,0:T(8,128)(2,1)S(1)}, u32[]{:S(2)}, u32[]{:S(2)}) %collective-permute-start.3) | collective-permute-done | bytes 262176 | tf_op jit(solution)/shard_map/ppermute | solution.py:524
  69.0 1.7 fusion
  70.8 3.7 %collective-permute-start.7 = (bf16[64,2048]{1,0:T(8,128)(2,1)}, bf16[64,2048]{1,0:T(8,128)(2,1)}, u32[]{:S(2)}, u32[]{:S(2)}) collective-permute-start(bf16[64,2048]{1,0:T(8,128)(2,1)} %fusion), channel_id=1, source_target_pairs={{0,6},{1,7},{2,0},{3,1},{4,2},{5,3},{6,4},{7,5},{8,14},{9,15},{10,... | collective-permute-start | bytes 786440 | tf_op jit(solution)/shard_map/ppermute | solution.py:529
  78.1 1.6 collective-permute-done.7.refs_3_
  80.8 2.3 dispatch.1
  83.0 20.1 %all_to_all.20 = bf16[16,16,2176]{2,1,0:T(8,128)(2,1)S(1)} all-to-all(bf16[16,16,2176]{2,1,0:T(8,128)(2,1)S(1)} %bitcast.83), channel_id=1, replica_groups=mesh['seq'=16,'exp'=8] {'seq'}, dimensions={0} | all-to-all | bytes 2228224 | tf_op jit(solution)/shard_map/all_to_all | solution.py:677
  103.3 3.8 %collective-permute-start.9 = (bf16[128,2176]{1,0:T(8,128)(2,1)S(1)}, bf16[128,2176]{1,0:T(8,128)(2,1)S(1)}, u32[]{:S(2)}, u32[]{:S(2)}) collective-permute-start(bf16[128,2176]{1,0:T(8,128)(2,1)S(1)} %bitcast.107), channel_id=1, source_target_pairs={{0,6},{1,7},{2,0},{3,1},{4,2},{5,3},{6,4},{7,5},{8,14},{9,15},{10,... | collective-permute-start | bytes 1671176 | tf_op jit(solution)/shard_map/ppermute | solution.py:529
  107.1 2.0 copy-done.8
  109.2 8.4 %expert.4 = (bf16[256,2176]{1,0:T(8,128)(2,1)S(1)}, bf16[256,2176]{1,0:T(8,128)(2,1)S(1)}) custom-call(bf16[256,2176]{1,0:T(8,128)(2,1)S(1)} %bitcast.80, bf16[256,2176]{1,0:T(8,128)(2,1)S(1)} %collective-permute-done.10.refs_1_, bf16[2048,896]{1,0:T(8,128)(2,1)S(1)} %bitcast.93, bf16[2048,896]{1,0:T(8,128)(2,1)S(1)} %bitcast.97, bf16[896,2048]{1,0:T(8,128)(2,1)S(1)} %bitcast.101), custom_call_target="tpu_custom_call" | custom-call | flops 5989466112 | bytes 15466496 | tf_op jit(solution)/shard_map/expert/pallas_call | solution.py:478
  117.6 2.7 %collective-permute-done.8.refs_0_ = bf16[128,2176]{1,0:T(8,128)(2,1)S(1)} collective-permute-done((bf16[128,2176]{1,0:T(8,128)(2,1)S(1)}, bf16[128,2176]{1,0:T(8,128)(2,1)S(1)}, u32[]{:S(2)}, u32[]{:S(2)}) %collective-permute-start.8) | collective-permute-done | bytes 557088 | tf_op jit(solution)/shard_map/ppermute | solution.py:524
  122.0 2.1 collective-permute-start.12
  124.1 8.4 %expert.5 = (bf16[256,2176]{1,0:T(8,128)(2,1)S(1)}, bf16[256,2176]{1,0:T(8,128)(2,1)S(1)}) custom-call(bf16[128,2176]{1,0:T(8,128)(2,1)S(1)} %collective-permute-done.8.refs_0_, bf16[128,2176]{1,0:T(8,128)(2,1)S(1)} %collective-permute-done.9.refs_1_, bf16[128,2176]{1,0:T(8,128)(2,1)S(1)} %collective-permute-done.14.refs_2_, ...), custom_call_target="tpu_custom_call" | custom-call | flops 5989466112 | bytes 15466496 | tf_op jit(solution)/shard_map/expert/pallas_call | solution.py:478
  132.5 4.6 %collective-permute-done.11.refs_0_ = bf16[128,2176]{1,0:T(8,128)(2,1)S(1)} collective-permute-done((bf16[128,2176]{1,0:T(8,128)(2,1)S(1)}, bf16[128,2176]{1,0:T(8,128)(2,1)S(1)}, u32[]{:S(2)}, u32[]{:S(2)}) %collective-permute-start.11) | collective-permute-done | bytes 557088 | tf_op jit(solution)/shard_map/ppermute | solution.py:524
  137.2 2.9 %collective-permute-start.16 = (bf16[128,2176]{1,0:T(8,128)(2,1)S(1)}, bf16[128,2176]{1,0:T(8,128)(2,1)S(1)}, u32[]{:S(2)}, u32[]{:S(2)}) collective-permute-start(bf16[128,2176]{1,0:T(8,128)(2,1)S(1)} %bitcast.110), channel_id=1, source_target_pairs={{0,6},{1,7},{2,0},{3,1},{4,2},{5,3},{6,4},{7,5},{8,14},{9,15},{10,... | collective-permute-start | bytes 1671176 | tf_op jit(solution)/shard_map/ppermute | solution.py:529
  142.9 8.4 %expert.6 = (bf16[256,2176]{1,0:T(8,128)(2,1)S(1)}, bf16[256,2176]{1,0:T(8,128)(2,1)S(1)}) custom-call(bf16[128,2176]{1,0:T(8,128)(2,1)S(1)} %collective-permute-done.11.refs_0_, bf16[128,2176]{1,0:T(8,128)(2,1)S(1)} %collective-permute-done.12.refs_1_, bf16[128,2176]{1,0:T(8,128)(2,1)S(1)} %collective-permute-done.19.refs_2_, ...), custom_call_target="tpu_custom_call" | custom-call | flops 5989466112 | bytes 15466496 | tf_op jit(solution)/shard_map/expert/pallas_call | solution.py:478
  151.3 1.3 collective-permute-done.16.refs_0_
  152.7 3.4 %collective-permute-done.17.refs_1_ = bf16[128,2176]{1,0:T(8,128)(2,1)S(1)} collective-permute-done((bf16[128,2176]{1,0:T(8,128)(2,1)S(1)}, bf16[128,2176]{1,0:T(8,128)(2,1)S(1)}, u32[]{:S(2)}, u32[]{:S(2)}) %collective-permute-start.17) | collective-permute-done | bytes 557088 | tf_op jit(solution)/shard_map/ppermute | solution.py:524
  156.4 1.7 collective-permute-start.25
  160.1 2.3 %collective-permute-start.23 = (bf16[128,2176]{1,0:T(8,128)(2,1)S(1)}, bf16[128,2176]{1,0:T(8,128)(2,1)S(1)}, u32[]{:S(2)}, u32[]{:S(2)}) collective-permute-start(bf16[128,2176]{1,0:T(8,128)(2,1)S(1)} %get-tuple-element.95), channel_id=1, source_target_pairs={{0,6},{1,7},{2,0},{3,1},{4,2},{5,3},{6,4},{7,5},{8,14},{9,15},{10,... | collective-permute-start | bytes 1671176 | tf_op jit(solution)/shard_map/ppermute | solution.py:529
  162.4 8.4 %expert.7 = (bf16[256,2176]{1,0:T(8,128)(2,1)S(1)}, bf16[256,2176]{1,0:T(8,128)(2,1)S(1)}) custom-call(bf16[128,2176]{1,0:T(8,128)(2,1)S(1)} %collective-permute-done.16.refs_0_, bf16[128,2176]{1,0:T(8,128)(2,1)S(1)} %collective-permute-done.17.refs_1_, bf16[128,2176]{1,0:T(8,128)(2,1)S(1)} %collective-permute-done.26.refs_2_, ...), custom_call_target="tpu_custom_call" | custom-call | flops 5989466112 | bytes 15466496 | tf_op jit(solution)/shard_map/expert/pallas_call | solution.py:478
  171.5 1.5 collective-permute-done.25.bottom_before
  173.0 11.2 %collective-permute-done.22 = bf16[128,2176]{1,0:T(8,128)(2,1)S(1)} collective-permute-done((bf16[128,2176]{1,0:T(8,128)(2,1)S(1)}, bf16[128,2176]{1,0:T(8,128)(2,1)S(1)}, u32[]{:S(2)}, u32[]{:S(2)}) %collective-permute-start.22) | collective-permute-done | bytes 557088 | tf_op jit(solution)/shard_map/ppermute | solution.py:524
  184.3 2.8 %collective-permute-done.28 = bf16[256,2176]{1,0:T(8,128)(2,1)S(1)} collective-permute-done((bf16[256,2176]{1,0:T(8,128)(2,1)S(1)}, bf16[256,2176]{1,0:T(8,128)(2,1)S(1)}, u32[]{:S(2)}, u32[]{:S(2)}) %collective-permute-start.28) | collective-permute-done | bytes 1114144 | tf_op jit(solution)/shard_map/ppermute | solution.py:534
  188.0 2.7 %collective-permute-start.30 = (bf16[128,2176]{1,0:T(8,128)(2,1)S(1)}, bf16[128,2176]{1,0:T(8,128)(2,1)S(1)}, u32[]{:S(2)}, u32[]{:S(2)}) collective-permute-start(bf16[128,2176]{1,0:T(8,128)(2,1)S(1)} %get-tuple-element.109), channel_id=1, source_target_pairs={{0,6},{1,7},{2,0},{3,1},{4,2},{5,3},{6,4},{7,5},{8,14},{9,15},{10,... | collective-permute-start | bytes 1671176 | tf_op jit(solution)/shard_map/ppermute | solution.py:529
  190.8 12.6 %collective-permute-done.29.top_before = bf16[128,2176]{1,0:T(8,128)(2,1)S(1)} collective-permute-done((bf16[128,2176]{1,0:T(8,128)(2,1)S(1)}, bf16[128,2176]{1,0:T(8,128)(2,1)S(1)}, u32[]{:S(2)}, u32[]{:S(2)}) %collective-permute-start.29) | collective-permute-done | bytes 557088 | tf_op jit(solution)/shard_map/ppermute | solution.py:524
  203.4 1.5 settle.1
  204.9 3.8 %all-to-all-start.3 = ((bf16[16,16,2176]{2,1,0:T(8,128)(2,1)}), bf16[16,16,2176]{2,1,0:T(8,128)(2,1)S(1)}, u32[]{:S(2)}, u32[]{:S(2)}) async-start(bf16[16,16,2176]{2,1,0:T(8,128)(2,1)} %bitcast.29), calls=%async_computation.3 | async-start | bytes 2228224 | tf_op jit(solution)/shard_map/all_to_all | solution.py:681
  208.9 18.0 %all-to-all-done.3 = bf16[16,16,2176]{2,1,0:T(8,128)(2,1)S(1)} async-done(((bf16[16,16,2176]{2,1,0:T(8,128)(2,1)}), bf16[16,16,2176]{2,1,0:T(8,128)(2,1)S(1)}, u32[]{:S(2)}, u32[]{:S(2)}) %all-to-all-start.3) | async-done | bytes 1114144 | tf_op jit(solution)/shard_map/all_to_all | solution.py:681
  226.9 1.7 combine.1
  228.6 1.3 copy.56
  (137 shorter events, 24.1 us)
Async XLA Ops:
  1.6 36.6 %copy-start.3 = (bf16[2,512,128]{2,1,0:T(8,128)(2,1)}, bf16[2,512,128]{2,1,0:T(8,128)(2,1)S(1)}, u32[]{:S(2)}) copy-start(bf16[2,512,128]{2,1,0:T(8,128)(2,1)S(1)} %get-tuple-element.125.reads) | copy-start | bytes 786436
  1.6 12.9 %copy-start.34 = (f32[8]{0:T(128)S(1)}, f32[8]{0:T(128)}, u32[]{:S(2)}) copy-start(f32[8]{0:T(128)} %param.23) | copy-start | bytes 100
  6.5 9.6 %copy-start.19 = (f32[2,512,128]{2,1,0:T(8,128)}, f32[2,512,128]{2,1,0:T(8,128)S(1)}, u32[]{:S(2)}) copy-start(f32[2,512,128]{2,1,0:T(8,128)S(1)} %get-tuple-element.57.first) | copy-start | bytes 1572868
  6.5 16.8 %all-to-all-start = ((bf16[16,72,128]{2,1,0:T(8,128)(2,1)}), bf16[16,72,128]{2,1,0:T(8,128)(2,1)S(1)}, u32[]{:S(2)}, u32[]{:S(2)}) async-start(bf16[16,72,128]{2,1,0:T(8,128)(2,1)} %get-tuple-element.59), calls=%async_computation | async-start | bytes 589824 | tf_op jit(solution)/shard_map/all_to_all | solution.py:630
  16.0 22.2 %copy-start.1 = (bf16[512,2,512]{2,0,1:T(8,128)(2,1)}, bf16[512,2,512]{2,0,1:T(8,128)(2,1)S(1)}, u32[]{:S(2)}) copy-start(bf16[512,2,512]{2,0,1:T(8,128)(2,1)S(1)} %copy.54) | copy-start | bytes 3145732
  25.8 12.4 %all-to-all-start.1 = ((bf16[16,64,128]{2,1,0:T(8,128)(2,1)}), bf16[16,64,128]{2,1,0:T(8,128)(2,1)S(1)}, u32[]{:S(2)}, u32[]{:S(2)}) async-start(bf16[16,64,128]{2,1,0:T(8,128)(2,1)} %scan.1), calls=%async_computation.1 | async-start | bytes 524288 | tf_op jit(solution)/shard_map/all_to_all | solution.py:636
  30.7 7.5 %copy-start.14 = (f32[512]{0:T(512)S(1)}, f32[512]{0:T(512)}, u32[]{:S(2)}) copy-start(f32[512]{0:T(512)} %param.24) | copy-start | bytes 6148
  30.7 7.5 %copy-start.22 = (f32[1,512,8]{2,1,0:T(8,128)S(1)}, f32[1,512,8]{2,1,0:T(8,128)}, u32[]{:S(2)}) copy-start(f32[1,512,8]{2,1,0:T(8,128)} %copy-done.21) | copy-start | bytes 49156
  45.2 8.3 %collective-permute-start = (bf16[4,64,2048]{2,1,0:T(8,128)(2,1)}, bf16[4,64,2048]{2,1,0:T(8,128)(2,1)S(1)}, u32[]{:S(2)}, u32[]{:S(2)}) collective-permute-start(bf16[4,64,2048]{2,1,0:T(8,128)(2,1)} %get-tuple-element.65), channel_id=1, source_target_pairs={{0,1},{1,0},{2,3},{3,2},{4,5},{5,4},{6,7},{7,6},{8,9},{9,8},{10,11... | collective-permute-start | bytes 3145736 | tf_op jit(solution)/shard_map/ppermute | solution.py:534
  51.7 5.7 %collective-permute-start.1 = (bf16[4,64,2048]{2,1,0:T(8,128)(2,1)}, bf16[4,64,2048]{2,1,0:T(8,128)(2,1)}, u32[]{:S(2)}, u32[]{:S(2)}) collective-permute-start(bf16[4,64,2048]{2,1,0:T(8,128)(2,1)} %get-tuple-element.69), channel_id=1, source_target_pairs={{0,1},{1,0},{2,3},{3,2},{4,5},{5,4},{6,7},{7,6},{8,9},{9,8},{10,11... | collective-permute-start | bytes 3145736 | tf_op jit(solution)/shard_map/ppermute | solution.py:534
  54.4 23.7 %collective-permute-start.2 = (bf16[64,2048]{1,0:T(8,128)(2,1)}, bf16[64,2048]{1,0:T(8,128)(2,1)S(1)}, u32[]{:S(2)}, u32[]{:S(2)}) collective-permute-start(bf16[64,2048]{1,0:T(8,128)(2,1)} %get-tuple-element.118), channel_id=1, source_target_pairs={{0,6},{1,7},{2,0},{3,1},{4,2},{5,3},{6,4},{7,5},{8,14},{9,15},{10,... | collective-permute-start | bytes 786440 | tf_op jit(solution)/shard_map/ppermute | solution.py:529
  57.4 10.4 %collective-permute-start.3 = (bf16[64,2048]{1,0:T(8,128)(2,1)S(1)}, bf16[64,2048]{1,0:T(8,128)(2,1)S(1)}, u32[]{:S(2)}, u32[]{:S(2)}) collective-permute-start(bf16[64,2048]{1,0:T(8,128)(2,1)S(1)} %get-tuple-element.117), channel_id=1, source_target_pairs={{0,2},{1,3},{2,4},{3,5},{4,6},{5,7},{6,0},{7,1},{8,10},{9,11},{10,... | collective-permute-start | bytes 786440 | tf_op jit(solution)/shard_map/ppermute | solution.py:524
  59.3 15.3 %copy-start.26 = (bf16[64,2,2048]{2,1,0:T(2,128)(2,1)S(1)}, bf16[64,2,2048]{2,1,0:T(2,128)(2,1)}, u32[]{:S(2)}) copy-start(bf16[64,2,2048]{2,1,0:T(2,128)(2,1)} %param.26) | copy-start | bytes 1572868
  59.3 15.2 %slice-start = ((s32[16,3]{0,1:T(4,128)}), s32[16,2]{0,1:T(2,128)S(1)}, s32[]{:S(2)}) async-start(s32[16,3]{0,1:T(4,128)} %copy-done.32), calls=%async_computation.4 | async-start | bytes 2048 | tf_op jit(solution)/shard_map/slice.1
  59.3 18.8 %collective-permute-start.5 = (bf16[64,2048]{1,0:T(8,128)(2,1)}, bf16[64,2048]{1,0:T(8,128)(2,1)}, u32[]{:S(2)}, u32[]{:S(2)}) collective-permute-start(bf16[64,2048]{1,0:T(8,128)(2,1)} %get-tuple-element.116), channel_id=1, source_target_pairs={{0,2},{1,3},{2,4},{3,5},{4,6},{5,7},{6,0},{7,1},{8,10},{9,11},{10,... | collective-permute-start | bytes 786440 | tf_op jit(solution)/shard_map/ppermute | solution.py:524
  59.9 9.1 %collective-permute-start.6 = (bf16[64,2048]{1,0:T(8,128)(2,1)S(1)}, bf16[64,2048]{1,0:T(8,128)(2,1)S(1)}, u32[]{:S(2)}, u32[]{:S(2)}) collective-permute-start(bf16[64,2048]{1,0:T(8,128)(2,1)S(1)} %get-tuple-element.115), channel_id=1, source_target_pairs={{0,6},{1,7},{2,0},{3,1},{4,2},{5,3},{6,4},{7,5},{8,14},{9,15},{10,... | collective-permute-start | bytes 786440 | tf_op jit(solution)/shard_map/ppermute | solution.py:529
  68.6 11.1 %copy-start.5 = (f32[2048]{0:T(1024)S(1)}, f32[2048]{0:T(1024)}, u32[]{:S(2)}) copy-start(f32[2048]{0:T(1024)} %param.27) | copy-start | bytes 24580
  68.6 9.5 %collective-permute-start.4 = (bf16[64,2048]{1,0:T(8,128)(2,1)}, bf16[64,2048]{1,0:T(8,128)(2,1)}, u32[]{:S(2)}, u32[]{:S(2)}) collective-permute-start(bf16[64,2048]{1,0:T(8,128)(2,1)} %fusion.1), channel_id=1, source_target_pairs={{0,2},{1,3},{2,4},{3,5},{4,6},{5,7},{6,0},{7,1},{8,10},{9,11},{10,... | collective-permute-start | bytes 786440 | tf_op jit(solution)/shard_map/ppermute | solution.py:524
  70.8 9.0 %collective-permute-start.7 = (bf16[64,2048]{1,0:T(8,128)(2,1)}, bf16[64,2048]{1,0:T(8,128)(2,1)}, u32[]{:S(2)}, u32[]{:S(2)}) collective-permute-start(bf16[64,2048]{1,0:T(8,128)(2,1)} %fusion), channel_id=1, source_target_pairs={{0,6},{1,7},{2,0},{3,1},{4,2},{5,3},{6,4},{7,5},{8,14},{9,15},{10,... | collective-permute-start | bytes 786440 | tf_op jit(solution)/shard_map/ppermute | solution.py:529
  80.8 26.3 %copy-start.7 = (bf16[1,2048,896]{2,1,0:T(8,128)(2,1)S(1)}, bf16[1,2048,896]{2,1,0:T(8,128)(2,1)}, u32[]{:S(2)}) copy-start(bf16[1,2048,896]{2,1,0:T(8,128)(2,1)} %param.29) | copy-start | bytes 11010052
  83.0 20.1 %copy-start.11 = (f32[128,2048]{1,0:T(8,128)}, f32[128,2048]{1,0:T(8,128)S(1)}, u32[]{:S(2)}) copy-start(f32[128,2048]{1,0:T(8,128)S(1)} %get-tuple-element.108.hidden) | copy-start | bytes 3145732
  83.0 24.1 %copy-start.6 = (bf16[1,2048,896]{2,1,0:T(8,128)(2,1)S(1)}, bf16[1,2048,896]{2,1,0:T(8,128)(2,1)}, u32[]{:S(2)}) copy-start(bf16[1,2048,896]{2,1,0:T(8,128)(2,1)} %param.28) | copy-start | bytes 11010052
  103.2 3.9 %collective-permute-start.10 = (bf16[256,2176]{1,0:T(8,128)(2,1)S(1)}, bf16[256,2176]{1,0:T(8,128)(2,1)S(1)}, u32[]{:S(2)}, u32[]{:S(2)}) collective-permute-start(bf16[256,2176]{1,0:T(8,128)(2,1)S(1)} %bitcast.79), channel_id=1, source_target_pairs={{0,1},{1,0},{2,3},{3,2},{4,5},{5,4},{6,7},{7,6},{8,9},{9,8},{10,11... | collective-permute-start | bytes 3342344 | tf_op jit(solution)/shard_map/ppermute | solution.py:534
  103.3 17.1 %collective-permute-start.8 = (bf16[128,2176]{1,0:T(8,128)(2,1)S(1)}, bf16[128,2176]{1,0:T(8,128)(2,1)S(1)}, u32[]{:S(2)}, u32[]{:S(2)}) collective-permute-start(bf16[128,2176]{1,0:T(8,128)(2,1)S(1)} %bitcast.109), channel_id=1, source_target_pairs={{0,2},{1,3},{2,4},{3,5},{4,6},{5,7},{6,0},{7,1},{8,10},{9,11},{10,... | collective-permute-start | bytes 1671176 | tf_op jit(solution)/shard_map/ppermute | solution.py:524
  103.3 17.0 %collective-permute-start.9 = (bf16[128,2176]{1,0:T(8,128)(2,1)S(1)}, bf16[128,2176]{1,0:T(8,128)(2,1)S(1)}, u32[]{:S(2)}, u32[]{:S(2)}) collective-permute-start(bf16[128,2176]{1,0:T(8,128)(2,1)S(1)} %bitcast.107), channel_id=1, source_target_pairs={{0,6},{1,7},{2,0},{3,1},{4,2},{5,3},{6,4},{7,5},{8,14},{9,15},{10,... | collective-permute-start | bytes 1671176 | tf_op jit(solution)/shard_map/ppermute | solution.py:529
  120.3 3.8 %collective-permute-start.14 = (bf16[128,2176]{1,0:T(8,128)(2,1)S(1)}, bf16[128,2176]{1,0:T(8,128)(2,1)S(1)}, u32[]{:S(2)}, u32[]{:S(2)}) collective-permute-start(bf16[128,2176]{1,0:T(8,128)(2,1)S(1)} %collective-permute-done.8.refs_0_), channel_id=1, source_target_pairs={{0,1},{1,0},{2,3},{3,2},{4,5},{5,4},{6,7},{7,6},{8,9},{9,8},{10,11... | collective-permute-start | bytes 1671176 | tf_op jit(solution)/shard_map/ppermute | solution.py:534
  120.3 3.8 %collective-permute-start.15 = (bf16[128,2176]{1,0:T(8,128)(2,1)S(1)}, bf16[128,2176]{1,0:T(8,128)(2,1)S(1)}, u32[]{:S(2)}, u32[]{:S(2)}) collective-permute-start(bf16[128,2176]{1,0:T(8,128)(2,1)S(1)} %collective-permute-done.9.refs_1_), channel_id=1, source_target_pairs={{0,1},{1,0},{2,3},{3,2},{4,5},{5,4},{6,7},{7,6},{8,9},{9,8},{10,11... | collective-permute-start | bytes 1671176 | tf_op jit(solution)/shard_map/ppermute | solution.py:534
  120.8 16.3 %collective-permute-start.13 = (bf16[256,2176]{1,0:T(8,128)(2,1)S(1)}, bf16[256,2176]{1,0:T(8,128)(2,1)S(1)}, u32[]{:S(2)}, u32[]{:S(2)}) collective-permute-start(bf16[256,2176]{1,0:T(8,128)(2,1)S(1)} %get-tuple-element.76), channel_id=1, source_target_pairs={{0,1},{1,0},{2,3},{3,2},{4,5},{5,4},{6,7},{7,6},{8,9},{9,8},{10,11... | collective-permute-start | bytes 3342344 | tf_op jit(solution)/shard_map/ppermute | solution.py:534
  120.8 16.3 %collective-permute-start.11 = (bf16[128,2176]{1,0:T(8,128)(2,1)S(1)}, bf16[128,2176]{1,0:T(8,128)(2,1)S(1)}, u32[]{:S(2)}, u32[]{:S(2)}) collective-permute-start(bf16[128,2176]{1,0:T(8,128)(2,1)S(1)} %collective-permute-done.8.refs_0_), channel_id=1, source_target_pairs={{0,2},{1,3},{2,4},{3,5},{4,6},{5,7},{6,0},{7,1},{8,10},{9,11},{10,... | collective-permute-start | bytes 1671176 | tf_op jit(solution)/shard_map/ppermute | solution.py:524
  122.0 15.2 %collective-permute-start.12 = (bf16[128,2176]{1,0:T(8,128)(2,1)S(1)}, bf16[128,2176]{1,0:T(8,128)(2,1)S(1)}, u32[]{:S(2)}, u32[]{:S(2)}) collective-permute-start(bf16[128,2176]{1,0:T(8,128)(2,1)S(1)} %collective-permute-done.9.refs_1_), channel_id=1, source_target_pairs={{0,6},{1,7},{2,0},{3,1},{4,2},{5,3},{6,4},{7,5},{8,14},{9,15},{10,... | collective-permute-start | bytes 1671176 | tf_op jit(solution)/shard_map/ppermute | solution.py:529
  137.2 3.5 %collective-permute-start.18 = (bf16[256,2176]{1,0:T(8,128)(2,1)S(1)}, bf16[256,2176]{1,0:T(8,128)(2,1)S(1)}, u32[]{:S(2)}, u32[]{:S(2)}) collective-permute-start(bf16[256,2176]{1,0:T(8,128)(2,1)S(1)} %get-tuple-element.83), channel_id=1, source_target_pairs={{0,1},{1,0},{2,3},{3,2},{4,5},{5,4},{6,7},{7,6},{8,9},{9,8},{10,11... | collective-permute-start | bytes 3342344 | tf_op jit(solution)/shard_map/ppermute | solution.py:534
  137.2 15.5 %collective-permute-start.16 = (bf16[128,2176]{1,0:T(8,128)(2,1)S(1)}, bf16[128,2176]{1,0:T(8,128)(2,1)S(1)}, u32[]{:S(2)}, u32[]{:S(2)}) collective-permute-start(bf16[128,2176]{1,0:T(8,128)(2,1)S(1)} %bitcast.110), channel_id=1, source_target_pairs={{0,6},{1,7},{2,0},{3,1},{4,2},{5,3},{6,4},{7,5},{8,14},{9,15},{10,... | collective-permute-start | bytes 1671176 | tf_op jit(solution)/shard_map/ppermute | solution.py:529
  140.1 16.0 %collective-permute-start.17 = (bf16[128,2176]{1,0:T(8,128)(2,1)S(1)}, bf16[128,2176]{1,0:T(8,128)(2,1)S(1)}, u32[]{:S(2)}, u32[]{:S(2)}) collective-permute-start(bf16[128,2176]{1,0:T(8,128)(2,1)S(1)} %bitcast.108), channel_id=1, source_target_pairs={{0,2},{1,3},{2,4},{3,5},{4,6},{5,7},{6,0},{7,1},{8,10},{9,11},{10,... | collective-permute-start | bytes 1671176 | tf_op jit(solution)/shard_map/ppermute | solution.py:524
  140.1 2.0 collective-permute-start.19
  140.4 2.5 %collective-permute-start.20 = (bf16[128,2176]{1,0:T(8,128)(2,1)S(1)}, bf16[128,2176]{1,0:T(8,128)(2,1)S(1)}, u32[]{:S(2)}, u32[]{:S(2)}) collective-permute-start(bf16[128,2176]{1,0:T(8,128)(2,1)S(1)} %collective-permute-done.12.refs_1_), channel_id=1, source_target_pairs={{0,1},{1,0},{2,3},{3,2},{4,5},{5,4},{6,7},{7,6},{8,9},{9,8},{10,11... | collective-permute-start | bytes 1671176 | tf_op jit(solution)/shard_map/ppermute | solution.py:534
  156.1 2.8 %collective-permute-start.21 = (bf16[256,2176]{1,0:T(8,128)(2,1)S(1)}, bf16[256,2176]{1,0:T(8,128)(2,1)S(1)}, u32[]{:S(2)}, u32[]{:S(2)}) collective-permute-start(bf16[256,2176]{1,0:T(8,128)(2,1)S(1)} %get-tuple-element.91), channel_id=1, source_target_pairs={{0,1},{1,0},{2,3},{3,2},{4,5},{5,4},{6,7},{7,6},{8,9},{9,8},{10,11... | collective-permute-start | bytes 3342344 | tf_op jit(solution)/shard_map/ppermute | solution.py:534
  156.1 15.4 %collective-permute-start.24 = (bf16[128,2176]{1,0:T(8,128)(2,1)S(1)}, bf16[128,2176]{1,0:T(8,128)(2,1)S(1)}, u32[]{:S(2)}, u32[]{:S(2)}) collective-permute-start(bf16[128,2176]{1,0:T(8,128)(2,1)S(1)} %get-tuple-element.96), channel_id=1, source_target_pairs={{0,6},{1,7},{2,0},{3,1},{4,2},{5,3},{6,4},{7,5},{8,14},{9,15},{10,... | collective-permute-start | bytes 1671176 | tf_op jit(solution)/shard_map/ppermute | solution.py:529
  156.4 16.7 %collective-permute-start.25 = (bf16[128,2176]{1,0:T(8,128)(2,1)S(1)}, bf16[128,2176]{1,0:T(8,128)(2,1)S(1)}, u32[]{:S(2)}, u32[]{:S(2)}) collective-permute-start(bf16[128,2176]{1,0:T(8,128)(2,1)S(1)} %get-tuple-element.97), channel_id=1, source_target_pairs={{0,2},{1,3},{2,4},{3,5},{4,6},{5,7},{6,0},{7,1},{8,10},{9,11},{10,... | collective-permute-start | bytes 1671176 | tf_op jit(solution)/shard_map/ppermute | solution.py:524
  158.1 2.0 collective-permute-start.26
  158.1 4.3 %collective-permute-start.27 = (bf16[128,2176]{1,0:T(8,128)(2,1)S(1)}, bf16[128,2176]{1,0:T(8,128)(2,1)S(1)}, u32[]{:S(2)}, u32[]{:S(2)}) collective-permute-start(bf16[128,2176]{1,0:T(8,128)(2,1)S(1)} %collective-permute-done.17.refs_1_), channel_id=1, source_target_pairs={{0,1},{1,0},{2,3},{3,2},{4,5},{5,4},{6,7},{7,6},{8,9},{9,8},{10,11... | collective-permute-start | bytes 1671176 | tf_op jit(solution)/shard_map/ppermute | solution.py:534
  159.1 25.2 %collective-permute-start.22 = (bf16[128,2176]{1,0:T(8,128)(2,1)S(1)}, bf16[128,2176]{1,0:T(8,128)(2,1)S(1)}, u32[]{:S(2)}, u32[]{:S(2)}) collective-permute-start(bf16[128,2176]{1,0:T(8,128)(2,1)S(1)} %get-tuple-element.94), channel_id=1, source_target_pairs={{0,2},{1,3},{2,4},{3,5},{4,6},{5,7},{6,0},{7,1},{8,10},{9,11},{10,... | collective-permute-start | bytes 1671176 | tf_op jit(solution)/shard_map/ppermute | solution.py:524
  160.1 24.2 %collective-permute-start.23 = (bf16[128,2176]{1,0:T(8,128)(2,1)S(1)}, bf16[128,2176]{1,0:T(8,128)(2,1)S(1)}, u32[]{:S(2)}, u32[]{:S(2)}) collective-permute-start(bf16[128,2176]{1,0:T(8,128)(2,1)S(1)} %get-tuple-element.95), channel_id=1, source_target_pairs={{0,6},{1,7},{2,0},{3,1},{4,2},{5,3},{6,4},{7,5},{8,14},{9,15},{10,... | collective-permute-start | bytes 1671176 | tf_op jit(solution)/shard_map/ppermute | solution.py:529
  184.3 2.8 %collective-permute-start.28 = (bf16[256,2176]{1,0:T(8,128)(2,1)S(1)}, bf16[256,2176]{1,0:T(8,128)(2,1)S(1)}, u32[]{:S(2)}, u32[]{:S(2)}) collective-permute-start(bf16[256,2176]{1,0:T(8,128)(2,1)S(1)} %get-tuple-element.104), channel_id=1, source_target_pairs={{0,1},{1,0},{2,3},{3,2},{4,5},{5,4},{6,7},{7,6},{8,9},{9,8},{10,11... | collective-permute-start | bytes 3342344 | tf_op jit(solution)/shard_map/ppermute | solution.py:534
  187.4 15.9 %collective-permute-start.29 = (bf16[128,2176]{1,0:T(8,128)(2,1)S(1)}, bf16[128,2176]{1,0:T(8,128)(2,1)S(1)}, u32[]{:S(2)}, u32[]{:S(2)}) collective-permute-start(bf16[128,2176]{1,0:T(8,128)(2,1)S(1)} %get-tuple-element.110), channel_id=1, source_target_pairs={{0,2},{1,3},{2,4},{3,5},{4,6},{5,7},{6,0},{7,1},{8,10},{9,11},{10,... | collective-permute-start | bytes 1671176 | tf_op jit(solution)/shard_map/ppermute | solution.py:524
  188.0 15.3 %collective-permute-start.30 = (bf16[128,2176]{1,0:T(8,128)(2,1)S(1)}, bf16[128,2176]{1,0:T(8,128)(2,1)S(1)}, u32[]{:S(2)}, u32[]{:S(2)}) collective-permute-start(bf16[128,2176]{1,0:T(8,128)(2,1)S(1)} %get-tuple-element.109), channel_id=1, source_target_pairs={{0,6},{1,7},{2,0},{3,1},{4,2},{5,3},{6,4},{7,5},{8,14},{9,15},{10,... | collective-permute-start | bytes 1671176 | tf_op jit(solution)/shard_map/ppermute | solution.py:529
  204.9 21.9 %copy-start.12 = (f32[128,2048]{1,0:T(8,128)S(1)}, f32[128,2048]{1,0:T(8,128)}, u32[]{:S(2)}) copy-start(f32[128,2048]{1,0:T(8,128)} %copy-done.11) | copy-start | bytes 3145732
  204.9 21.9 %copy-start.13 = (f32[4,2048]{1,0:T(4,128)S(1)}, f32[4,2048]{1,0:T(4,128)}, u32[]{:S(2)}) copy-start(f32[4,2048]{1,0:T(4,128)} %directions.1) | copy-start | bytes 98308
  204.9 21.9 %all-to-all-start.3 = ((bf16[16,16,2176]{2,1,0:T(8,128)(2,1)}), bf16[16,16,2176]{2,1,0:T(8,128)(2,1)S(1)}, u32[]{:S(2)}, u32[]{:S(2)}) async-start(bf16[16,16,2176]{2,1,0:T(8,128)(2,1)} %bitcast.29), calls=%async_computation.3 | async-start | bytes 2228224 | tf_op jit(solution)/shard_map/all_to_all | solution.py:681
  (22 other events, 46.4 us)

commit v4 on v3

--- a/solution.py
+++ b/solution.py
@@ -65,69 +65,62 @@
     )
 
 
-def contrib_kernel(decay, step, inputs, writes, parcel, first, total, running):
-    block = pl.program_id(1)
-    heads = decay.shape[1]
-    cum_row = running_sums(decay[0])
-    end_row = jnp.broadcast_to(cum_row[:, BLOCK - 1 :], (heads, STATE))
-    to_end_row = jnp.exp(cum_row[:, BLOCK - 1 :] - cum_row) * step[0]
-    to_end = jnp.transpose(to_end_row)
-    scaled = (inputs[0].astype(F32) * spread_heads(to_end, heads)).astype(BF16)
-    contrib = lax.dot_general(
-        scaled, writes[0], (((0,), (0,)), ((), ())), preferred_element_type=F32
-    )
-
-    @pl.when(block == 0)
-    def _():
-        first[0] = contrib
-        running[...] = contrib
-        total[...] = end_row
-
-    @pl.when(block > 0)
-    def _():
-        running[...] = over_rows(jnp.exp(end_row)) * running[...] + contrib
-        total[...] = total[...] + end_row
-
-    @pl.when(block == pl.num_programs(1) - 1)
-    def _():
-        carried = jnp.exp(total[...])
-        high, rest = two_parts(carried)
-        middle, low = two_parts(carried - high.astype(F32))
-        row = lax.broadcasted_iota(jnp.int32, (heads, 8, STATE), 1)
-        wide = lambda part: jnp.broadcast_to(part.astype(F32)[:, None, :], (heads, 8, STATE))
-        extra = jnp.where(
-            row == 0,
-            wide(high),
-            jnp.where(row == 1, wide(middle), jnp.where(row == 2, wide(low), 0.0)),
+def contrib_kernel(decay, step, inputs, writes, parcel, first):
+    heads, length = decay.shape[1], decay.shape[2]
+    running = total = None
+    for start in range(0, length, BLOCK):
+        span = slice(start, start + BLOCK)
+        cum_row = running_sums(decay[0, :, span])
+        end = cum_row[:, BLOCK - 1 :]
+        to_end = jnp.transpose(jnp.exp(end - cum_row) * step[0, :, span])
+        scaled = (inputs[0, span, :].astype(F32) * spread_heads(to_end, heads)).astype(BF16)
+        contrib = lax.dot_general(
+            scaled, writes[0, span, :], (((0,), (0,)), ((), ())), preferred_element_type=F32
         )
-        parcel[:, :HEAD_DIM, :] = running[...].reshape(heads, HEAD_DIM, STATE).astype(BF16)
-        parcel[:, HEAD_DIM:, :] = extra.astype(BF16)
+        end_row = jnp.broadcast_to(end, (heads, STATE))
+        if start == 0:
+            first[0] = contrib
+            running, total = contrib, end_row
+        else:
+            running = over_rows(jnp.exp(end_row)) * running + contrib
+            total = total + end_row
+    carried = jnp.exp(total)
+    high, rest = two_parts(carried)
+    middle, low = two_parts(carried - high.astype(F32))
+    row = lax.broadcasted_iota(jnp.int32, (heads, 8, STATE), 1)
+    wide = lambda part: jnp.broadcast_to(part.astype(F32)[:, None, :], (heads, 8, STATE))
+    extra = jnp.where(
+        row == 0,
+        wide(high),
+        jnp.where(row == 1, wide(middle), jnp.where(row == 2, wide(low), 0.0)),
+    )
+    parcel[:, :HEAD_DIM, :] = running.reshape(heads, HEAD_DIM, STATE).astype(BF16)
+    parcel[:, HEAD_DIM:, :] = extra.astype(BF16)
 
 
 def contrib_call(decays, steps, inputs, writes):
     seqs, heads, length = decays.shape
     width = inputs.shape[2]
-    blocks = length // BLOCK
+    assert length == 2 * BLOCK
     return pl.pallas_call(
         contrib_kernel,
-        grid=(seqs, blocks),
+        grid=(seqs,),
         in_specs=[
-            pl.BlockSpec((1, heads, BLOCK), lambda b, c: (b, 0, c)),
-            pl.BlockSpec((1, heads, BLOCK), lambda b, c: (b, 0, c)),
-            pl.BlockSpec((1, BLOCK, width), lambda b, c: (b, c, 0)),
-            pl.BlockSpec((1, BLOCK, STATE), lambda b, c: (b, c, 0)),
+            pl.BlockSpec((1, heads, length), lambda b: (b, 0, 0)),
+            pl.BlockSpec((1, heads, length), lambda b: (b, 0, 0)),
+            pl.BlockSpec((1, length, width), lambda b: (b, 0, 0)),
+            pl.BlockSpec((1, length, STATE), lambda b: (b, 0, 0)),
         ],
         out_specs=[
-            pl.BlockSpec((heads, HEAD_DIM + 8, STATE), lambda b, c: (b, 0, 0)),
-            pl.BlockSpec((1, width, STATE), lambda b, c: (b, 0, 0)),
+            pl.BlockSpec((heads, HEAD_DIM + 8, STATE), lambda b: (b, 0, 0)),
+            pl.BlockSpec((1, width, STATE), lambda b: (b, 0, 0)),
         ],
         out_shape=[
             jax.ShapeDtypeStruct((seqs * heads, HEAD_DIM + 8, STATE), BF16),
             jax.ShapeDtypeStruct((seqs, width, STATE), F32),
         ],
-        scratch_shapes=[pltpu.VMEM((heads, STATE), F32), pltpu.VMEM((width, STATE), F32)],
         compiler_params=pltpu.CompilerParams(
-            dimension_semantics=("arbitrary", "arbitrary"), vmem_limit_bytes=16 * 2**20
+            dimension_semantics=("arbitrary",), vmem_limit_bytes=16 * 2**20
         ),
         cost_estimate=pl.CostEstimate(flops=10**9, bytes_accessed=2 * 2**20, transcendentals=8192),
         name="contrib",
@@ -287,7 +280,7 @@
             pl.BlockSpec((1, BLOCK, width), lambda c: (0, c, 0)),
             pl.BlockSpec((1, BLOCK, width), lambda c: (which, c, 0)),
             pl.BlockSpec((1, width), lambda c: (0, 0)),
-            pl.BlockSpec((width, D), lambda c: (0, 0)),
+            pl.BlockSpec(memory_space=pltpu.VMEM),
         ],
         out_specs=[anywhere, anywhere],
         out_shape=[jax.ShapeDtypeStruct((columns // 2, keep, D), BF16)] * 2,
@@ -390,7 +383,9 @@
         norm = jnp.sum(direction * direction, axis=1, keepdims=True) + 1e-06
         along = jnp.sum(combined * direction, axis=1, keepdims=True) / norm
         combined = combined - along * direction
-    out[...] = combined.astype(BF16)
+    half = rows // 2
+    out[:, 0, :] = combined[:half].astype(BF16)
+    out[:, 1, :] = combined[half:].astype(BF16)
 
 
 def combine_call(returned, places, gates, hidden, directions):
@@ -398,7 +393,7 @@
     count = returned.shape[0]
     return pl.pallas_call(
         combine_kernel,
-        out_shape=jax.ShapeDtypeStruct((rows, D), BF16),
+        out_shape=jax.ShapeDtypeStruct((rows // 2, 2, D), BF16),
         scratch_shapes=[
             pltpu.VMEM((count, 128), F32),
             pltpu.VMEM((count + count // FOLD, D), BF16),
@@ -688,7 +683,7 @@
         hidden_state,
         directions,
     )
-    return swap(combined.reshape(seqs, length_dev // columns, D))
+    return combined
 
 
 def solution(mesh):

time: 231 us -> 229 us (level)
  transfers between devices with their start and end apart: 34 -> 34, of which waited for: 19 -> 19; matrix products, arithmetic and copies ran while one was open for 5% -> 5% of each run, Pallas kernels for 18% -> 19%
where the time goes in v4:
time: 229 us; the launch traced here: 228 us
  waiting for transfers between devices  76 us (33%)
  Pallas kernels  58.6 us (26%)
  starting transfers between devices  45.8 us (20%)
  blocking collectives  20.1 us (9%)
  local copies, waits for them, and re-layouts  19.7 us (9%)
  other arithmetic  7.79 us (3%)
    ppermute x9, waiting for transfers between devices, from_before(): lax.ppermute(values, 'exp', [(i, (i + 2) % size) for i in range(size)])  41.3 us
    pallas_call x4, Pallas kernels, expert_call(): pl.pallas_call(functools.partial(expert_kernel, counts), in_specs=[anywhe...  33.8 us
    ppermute x9, starting transfers between devices, from_after(): lax.ppermute(values, 'exp', [(i, (i - 2) % size) for i in range(size)])  23.6 us
    all_to_all x1, blocking collectives, on_device(): lax.all_to_all(packed.reshape(experts, FOLD, D + 128), 'seq', split_axis=...  20.1 us
    all_to_all x1, waiting for transfers between devices, on_device(): lax.all_to_all(summed.reshape(experts, FOLD, D + 128), 'seq', split_axis=...  18 us
    unnamed x72, local copies, waits for them, and re-layouts  16.1 us
    pallas_call x2, Pallas kernels, mixer_call(): pl.pallas_call(mixer_kernel, grid=(blocks,), in_specs=[pl.BlockSpec(memor...  8.35 us
    all_to_all x1, starting transfers between devices, on_device(): lax.all_to_all(parcel, 'seq', split_axis=0, concat_axis=0, tiled=True)  7.97 us
  transfers between devices with their start and end apart: 34, of which 19 were waited for; matrix products, arithmetic and copies ran while one was open for 5% of the time, Pallas kernels for 19%

profile of v4, /device:TPU:0, one launch (start us, length us, event | category | flops | bytes accessed | tf_op | source)
XLA Modules:
  0.0 228.4 jit_solution(13561073550858684008)
XLA Ops:
  0.0 1.4 copy.52
  1.6 3.8 %contrib.1 = (bf16[16,72,128]{2,1,0:T(8,128)(2,1)}, f32[2,512,128]{2,1,0:T(8,128)S(1)}) custom-call(f32[2,8,512]{2,1,0:T(8,128)S(1)} %get-tuple-element.124.decay, f32[2,8,512]{2,1,0:T(8,128)S(1)} %get-tuple-element.123.step, bf16[2,512,512]{2,1,0:T(8,128)(2,1)S(1)} %bitcast.82, bf16[2,512,128]{2,1,0:T(8,128)(2,1)S(1)} %get-tuple-element.126.writes), custom_call_target="tpu_custom_call" | custom-call | flops 1000000000 | bytes 2097152 | tf_op jit(solution)/shard_map/contrib/pallas_call | solution.py:105
  5.4 8.0 %all-to-all-start = ((bf16[16,72,128]{2,1,0:T(8,128)(2,1)}), bf16[16,72,128]{2,1,0:T(8,128)(2,1)S(1)}, u32[]{:S(2)}, u32[]{:S(2)}) async-start(bf16[16,72,128]{2,1,0:T(8,128)(2,1)} %get-tuple-element.59), calls=%async_computation | async-start | bytes 589824 | tf_op jit(solution)/shard_map/all_to_all | solution.py:625
  13.5 1.4 copy.51
  14.9 2.3 %within.2 = (f32[1,512,512]{2,1,0:T(8,128)S(1)}, f32[1,512,8]{2,1,0:T(8,128)S(1)}) custom-call(f32[2,8,512]{2,1,0:T(8,128)S(1)} %get-tuple-element.124.decay, f32[2,8,512]{2,1,0:T(8,128)S(1)} %get-tuple-element.123.step, bf16[2,512,512]{2,1,0:T(8,128)(2,1)S(1)} %bitcast.83, bf16[2,512,128]{2,1,0:T(8,128)(2,1)S(1)} %get-tuple-element.126.writes, ...), custom_call_target="tpu_custom_call" | custom-call | flops 3000000000 | bytes 2097152 | tf_op jit(solution)/shard_map/within/pallas_call | solution.py:173
  18.9 3.3 %all-to-all-done.parcels = bf16[16,72,128]{2,1,0:T(8,128)(2,1)S(1)} async-done(((bf16[16,72,128]{2,1,0:T(8,128)(2,1)}), bf16[16,72,128]{2,1,0:T(8,128)(2,1)S(1)}, u32[]{:S(2)}, u32[]{:S(2)}) %all-to-all-start) | async-done | bytes 294944 | tf_op jit(solution)/shard_map/all_to_all | solution.py:625
  22.9 1.7 scan.1
  24.6 3.9 %all-to-all-start.1 = ((bf16[16,64,128]{2,1,0:T(8,128)(2,1)}), bf16[16,64,128]{2,1,0:T(8,128)(2,1)S(1)}, u32[]{:S(2)}, u32[]{:S(2)}) async-start(bf16[16,64,128]{2,1,0:T(8,128)(2,1)} %scan.1), calls=%async_computation.1 | async-start | bytes 524288 | tf_op jit(solution)/shard_map/all_to_all | solution.py:631
  29.6 2.3 within.3
  33.6 3.5 %all-to-all-done.1.entering = bf16[16,64,128]{2,1,0:T(8,128)(2,1)S(1)} async-done(((bf16[16,64,128]{2,1,0:T(8,128)(2,1)}), bf16[16,64,128]{2,1,0:T(8,128)(2,1)S(1)}, u32[]{:S(2)}, u32[]{:S(2)}) %all-to-all-start.1) | async-done | bytes 262176 | tf_op jit(solution)/shard_map/all_to_all | solution.py:631
  37.1 1.6 copy-done.9
  38.7 1.2 copy-done.16
  39.9 4.2 %mixer.2 = (bf16[4,64,2048]{2,1,0:T(8,128)(2,1)S(1)}, bf16[4,64,2048]{2,1,0:T(8,128)(2,1)}) custom-call(s32[1]{0:T(128)} %bitcast.8.place, f32[1,512,8]{2,1,0:T(8,128)S(1)} %copy-done.22, bf16[2,512,128]{2,1,0:T(8,128)(2,1)S(1)} %get-tuple-element.125.reads, bf16[16,64,128]{2,1,0:T(8,128)(2,1)S(1)} %all-to-all-done.1.entering, ...), custom_call_target="tpu_custom_call" | custom-call | flops 2000000000 | bytes 6291456 | tf_op jit(solution)/shard_map/mixer/pallas_call | solution.py:272
  44.3 1.2 copy-done.2
  46.4 4.2 %mixer.3 = (bf16[4,64,2048]{2,1,0:T(8,128)(2,1)S(1)}, bf16[4,64,2048]{2,1,0:T(8,128)(2,1)}) custom-call(s32[1]{0:T(128)} %bitcast.8.place, f32[1,512,8]{2,1,0:T(8,128)S(1)} %copy-done.24, bf16[2,512,128]{2,1,0:T(8,128)(2,1)S(1)} %copy-done.4, bf16[16,64,128]{2,1,0:T(8,128)(2,1)S(1)} %all-to-all-done.1.entering, f32[1,512,512]{2,1,0:T(8,128)S(1)} %copy-done.18, ...), custom_call_target="tpu_custom_call" | custom-call | flops 2000000000 | bytes 6291456 | tf_op jit(solution)/shard_map/mixer/pallas_call | solution.py:272
  53.2 3.0 %collective-permute-start.2 = (bf16[64,2048]{1,0:T(8,128)(2,1)}, bf16[64,2048]{1,0:T(8,128)(2,1)S(1)}, u32[]{:S(2)}, u32[]{:S(2)}) collective-permute-start(bf16[64,2048]{1,0:T(8,128)(2,1)} %get-tuple-element.118), channel_id=1, source_target_pairs={{0,6},{1,7},{2,0},{3,1},{4,2},{5,3},{6,4},{7,5},{8,14},{9,15},{10,... | collective-permute-start | bytes 786440 | tf_op jit(solution)/shard_map/ppermute | solution.py:524
  56.3 1.9 fusion.5
  58.8 2.8 %collective-permute-start.6 = (bf16[64,2048]{1,0:T(8,128)(2,1)S(1)}, bf16[64,2048]{1,0:T(8,128)(2,1)S(1)}, u32[]{:S(2)}, u32[]{:S(2)}) collective-permute-start(bf16[64,2048]{1,0:T(8,128)(2,1)S(1)} %get-tuple-element.115), channel_id=1, source_target_pairs={{0,6},{1,7},{2,0},{3,1},{4,2},{5,3},{6,4},{7,5},{8,14},{9,15},{10,... | collective-permute-start | bytes 786440 | tf_op jit(solution)/shard_map/ppermute | solution.py:524
  61.5 5.2 %collective-permute-done.3 = bf16[64,2048]{1,0:T(8,128)(2,1)S(1)} collective-permute-done((bf16[64,2048]{1,0:T(8,128)(2,1)S(1)}, bf16[64,2048]{1,0:T(8,128)(2,1)S(1)}, u32[]{:S(2)}, u32[]{:S(2)}) %collective-permute-start.3) | collective-permute-done | bytes 262176 | tf_op jit(solution)/shard_map/ppermute | solution.py:519
  67.9 1.7 fusion
  69.6 3.7 %collective-permute-start.7 = (bf16[64,2048]{1,0:T(8,128)(2,1)}, bf16[64,2048]{1,0:T(8,128)(2,1)}, u32[]{:S(2)}, u32[]{:S(2)}) collective-permute-start(bf16[64,2048]{1,0:T(8,128)(2,1)} %fusion), channel_id=1, source_target_pairs={{0,6},{1,7},{2,0},{3,1},{4,2},{5,3},{6,4},{7,5},{8,14},{9,15},{10,... | collective-permute-start | bytes 786440 | tf_op jit(solution)/shard_map/ppermute | solution.py:524
  77.0 1.6 collective-permute-done.7.refs_3_
  79.7 2.3 dispatch.1
  81.9 20.1 %all_to_all.20 = bf16[16,16,2176]{2,1,0:T(8,128)(2,1)S(1)} all-to-all(bf16[16,16,2176]{2,1,0:T(8,128)(2,1)S(1)} %bitcast.79), channel_id=1, replica_groups=mesh['seq'=16,'exp'=8] {'seq'}, dimensions={0} | all-to-all | bytes 2228224 | tf_op jit(solution)/shard_map/all_to_all | solution.py:672
  102.2 3.8 %collective-permute-start.9 = (bf16[128,2176]{1,0:T(8,128)(2,1)S(1)}, bf16[128,2176]{1,0:T(8,128)(2,1)S(1)}, u32[]{:S(2)}, u32[]{:S(2)}) collective-permute-start(bf16[128,2176]{1,0:T(8,128)(2,1)S(1)} %bitcast.102), channel_id=1, source_target_pairs={{0,6},{1,7},{2,0},{3,1},{4,2},{5,3},{6,4},{7,5},{8,14},{9,15},{10,... | collective-permute-start | bytes 1671176 | tf_op jit(solution)/shard_map/ppermute | solution.py:524
  106.0 2.0 copy-done.8
  108.0 8.4 %expert.4 = (bf16[256,2176]{1,0:T(8,128)(2,1)S(1)}, bf16[256,2176]{1,0:T(8,128)(2,1)S(1)}) custom-call(bf16[256,2176]{1,0:T(8,128)(2,1)S(1)} %bitcast.76, bf16[256,2176]{1,0:T(8,128)(2,1)S(1)} %collective-permute-done.10.refs_1_, bf16[2048,896]{1,0:T(8,128)(2,1)S(1)} %bitcast.88, bf16[2048,896]{1,0:T(8,128)(2,1)S(1)} %bitcast.92, bf16[896,2048]{1,0:T(8,128)(2,1)S(1)} %bitcast.96), custom_call_target="tpu_custom_call" | custom-call | flops 5989466112 | bytes 15466496 | tf_op jit(solution)/shard_map/expert/pallas_call | solution.py:473
  116.5 2.7 %collective-permute-done.8.refs_0_ = bf16[128,2176]{1,0:T(8,128)(2,1)S(1)} collective-permute-done((bf16[128,2176]{1,0:T(8,128)(2,1)S(1)}, bf16[128,2176]{1,0:T(8,128)(2,1)S(1)}, u32[]{:S(2)}, u32[]{:S(2)}) %collective-permute-start.8) | collective-permute-done | bytes 557088 | tf_op jit(solution)/shard_map/ppermute | solution.py:519
  120.9 2.1 collective-permute-start.12
  123.0 8.5 %expert.5 = (bf16[256,2176]{1,0:T(8,128)(2,1)S(1)}, bf16[256,2176]{1,0:T(8,128)(2,1)S(1)}) custom-call(bf16[128,2176]{1,0:T(8,128)(2,1)S(1)} %collective-permute-done.8.refs_0_, bf16[128,2176]{1,0:T(8,128)(2,1)S(1)} %collective-permute-done.9.refs_1_, bf16[128,2176]{1,0:T(8,128)(2,1)S(1)} %collective-permute-done.14.refs_2_, ...), custom_call_target="tpu_custom_call" | custom-call | flops 5989466112 | bytes 15466496 | tf_op jit(solution)/shard_map/expert/pallas_call | solution.py:473
  131.4 4.6 %collective-permute-done.11.refs_0_ = bf16[128,2176]{1,0:T(8,128)(2,1)S(1)} collective-permute-done((bf16[128,2176]{1,0:T(8,128)(2,1)S(1)}, bf16[128,2176]{1,0:T(8,128)(2,1)S(1)}, u32[]{:S(2)}, u32[]{:S(2)}) %collective-permute-start.11) | collective-permute-done | bytes 557088 | tf_op jit(solution)/shard_map/ppermute | solution.py:519
  136.1 2.9 %collective-permute-start.16 = (bf16[128,2176]{1,0:T(8,128)(2,1)S(1)}, bf16[128,2176]{1,0:T(8,128)(2,1)S(1)}, u32[]{:S(2)}, u32[]{:S(2)}) collective-permute-start(bf16[128,2176]{1,0:T(8,128)(2,1)S(1)} %bitcast.105), channel_id=1, source_target_pairs={{0,6},{1,7},{2,0},{3,1},{4,2},{5,3},{6,4},{7,5},{8,14},{9,15},{10,... | collective-permute-start | bytes 1671176 | tf_op jit(solution)/shard_map/ppermute | solution.py:524
  139.8 1.2 collective-permute-done.19.refs_2_
  141.8 8.4 %expert.6 = (bf16[256,2176]{1,0:T(8,128)(2,1)S(1)}, bf16[256,2176]{1,0:T(8,128)(2,1)S(1)}) custom-call(bf16[128,2176]{1,0:T(8,128)(2,1)S(1)} %collective-permute-done.11.refs_0_, bf16[128,2176]{1,0:T(8,128)(2,1)S(1)} %collective-permute-done.12.refs_1_, bf16[128,2176]{1,0:T(8,128)(2,1)S(1)} %collective-permute-done.19.refs_2_, ...), custom_call_target="tpu_custom_call" | custom-call | flops 5989466112 | bytes 15466496 | tf_op jit(solution)/shard_map/expert/pallas_call | solution.py:473
  150.2 1.3 collective-permute-done.16.refs_0_
  151.6 3.4 %collective-permute-done.17.refs_1_ = bf16[128,2176]{1,0:T(8,128)(2,1)S(1)} collective-permute-done((bf16[128,2176]{1,0:T(8,128)(2,1)S(1)}, bf16[128,2176]{1,0:T(8,128)(2,1)S(1)}, u32[]{:S(2)}, u32[]{:S(2)}) %collective-permute-start.17) | collective-permute-done | bytes 557088 | tf_op jit(solution)/shard_map/ppermute | solution.py:519
  155.3 1.7 collective-permute-start.25
  159.0 2.3 %collective-permute-start.23 = (bf16[128,2176]{1,0:T(8,128)(2,1)S(1)}, bf16[128,2176]{1,0:T(8,128)(2,1)S(1)}, u32[]{:S(2)}, u32[]{:S(2)}) collective-permute-start(bf16[128,2176]{1,0:T(8,128)(2,1)S(1)} %get-tuple-element.95), channel_id=1, source_target_pairs={{0,6},{1,7},{2,0},{3,1},{4,2},{5,3},{6,4},{7,5},{8,14},{9,15},{10,... | collective-permute-start | bytes 1671176 | tf_op jit(solution)/shard_map/ppermute | solution.py:524
  161.3 8.4 %expert.7 = (bf16[256,2176]{1,0:T(8,128)(2,1)S(1)}, bf16[256,2176]{1,0:T(8,128)(2,1)S(1)}) custom-call(bf16[128,2176]{1,0:T(8,128)(2,1)S(1)} %collective-permute-done.16.refs_0_, bf16[128,2176]{1,0:T(8,128)(2,1)S(1)} %collective-permute-done.17.refs_1_, bf16[128,2176]{1,0:T(8,128)(2,1)S(1)} %collective-permute-done.26.refs_2_, ...), custom_call_target="tpu_custom_call" | custom-call | flops 5989466112 | bytes 15466496 | tf_op jit(solution)/shard_map/expert/pallas_call | solution.py:473
  170.4 1.5 collective-permute-done.25.bottom_before
  171.9 11.2 %collective-permute-done.22 = bf16[128,2176]{1,0:T(8,128)(2,1)S(1)} collective-permute-done((bf16[128,2176]{1,0:T(8,128)(2,1)S(1)}, bf16[128,2176]{1,0:T(8,128)(2,1)S(1)}, u32[]{:S(2)}, u32[]{:S(2)}) %collective-permute-start.22) | collective-permute-done | bytes 557088 | tf_op jit(solution)/shard_map/ppermute | solution.py:519
  183.2 2.8 %collective-permute-done.28 = bf16[256,2176]{1,0:T(8,128)(2,1)S(1)} collective-permute-done((bf16[256,2176]{1,0:T(8,128)(2,1)S(1)}, bf16[256,2176]{1,0:T(8,128)(2,1)S(1)}, u32[]{:S(2)}, u32[]{:S(2)}) %collective-permute-start.28) | collective-permute-done | bytes 1114144 | tf_op jit(solution)/shard_map/ppermute | solution.py:529
  186.9 2.7 %collective-permute-start.30 = (bf16[128,2176]{1,0:T(8,128)(2,1)S(1)}, bf16[128,2176]{1,0:T(8,128)(2,1)S(1)}, u32[]{:S(2)}, u32[]{:S(2)}) collective-permute-start(bf16[128,2176]{1,0:T(8,128)(2,1)S(1)} %get-tuple-element.109), channel_id=1, source_target_pairs={{0,6},{1,7},{2,0},{3,1},{4,2},{5,3},{6,4},{7,5},{8,14},{9,15},{10,... | collective-permute-start | bytes 1671176 | tf_op jit(solution)/shard_map/ppermute | solution.py:524
  189.6 12.6 %collective-permute-done.29.top_before = bf16[128,2176]{1,0:T(8,128)(2,1)S(1)} collective-permute-done((bf16[128,2176]{1,0:T(8,128)(2,1)S(1)}, bf16[128,2176]{1,0:T(8,128)(2,1)S(1)}, u32[]{:S(2)}, u32[]{:S(2)}) %collective-permute-start.29) | collective-permute-done | bytes 557088 | tf_op jit(solution)/shard_map/ppermute | solution.py:519
  202.3 1.5 settle.1
  203.8 3.8 %all-to-all-start.3 = ((bf16[16,16,2176]{2,1,0:T(8,128)(2,1)}), bf16[16,16,2176]{2,1,0:T(8,128)(2,1)S(1)}, u32[]{:S(2)}, u32[]{:S(2)}) async-start(bf16[16,16,2176]{2,1,0:T(8,128)(2,1)} %bitcast.29), calls=%async_computation.3 | async-start | bytes 2228224 | tf_op jit(solution)/shard_map/all_to_all | solution.py:676
  207.8 18.0 %all-to-all-done.3 = bf16[16,16,2176]{2,1,0:T(8,128)(2,1)S(1)} async-done(((bf16[16,16,2176]{2,1,0:T(8,128)(2,1)}), bf16[16,16,2176]{2,1,0:T(8,128)(2,1)S(1)}, u32[]{:S(2)}, u32[]{:S(2)}) %all-to-all-start.3) | async-done | bytes 1114144 | tf_op jit(solution)/shard_map/all_to_all | solution.py:676
  225.8 2.6 %combine.1 = bf16[64,2,2048]{2,1,0:T(2,128)(2,1)} custom-call(bf16[256,2176]{1,0:T(8,128)(2,1)S(1)} %bitcast.78, s32[128,2]{1,0:T(8,128)S(1)} %bitcast_select_fusion.places, f32[128,2]{1,0:T(8,128)S(1)} %bitcast.86, f32[128,2048]{1,0:T(8,128)S(1)} %copy-done.12, f32[4,2048]{1,0:T(4,128)S(1)} %copy-done.13), custom_call_target="tpu_custom_call" | custom-call | flops 1000000000 | bytes 4194304 | tf_op jit(solution)/shard_map/combine/pallas_call | solution.py:394
  (136 shorter events, 22.9 us)
Async XLA Ops:
  1.6 35.5 %copy-start.3 = (bf16[2,512,128]{2,1,0:T(8,128)(2,1)}, bf16[2,512,128]{2,1,0:T(8,128)(2,1)S(1)}, u32[]{:S(2)}) copy-start(bf16[2,512,128]{2,1,0:T(8,128)(2,1)S(1)} %get-tuple-element.125.reads) | copy-start | bytes 786436
  1.6 11.8 %copy-start.34 = (f32[8]{0:T(128)S(1)}, f32[8]{0:T(128)}, u32[]{:S(2)}) copy-start(f32[8]{0:T(128)} %param.23) | copy-start | bytes 100
  5.4 9.6 %copy-start.19 = (f32[2,512,128]{2,1,0:T(8,128)}, f32[2,512,128]{2,1,0:T(8,128)S(1)}, u32[]{:S(2)}) copy-start(f32[2,512,128]{2,1,0:T(8,128)S(1)} %get-tuple-element.57.first) | copy-start | bytes 1572868
  5.4 16.8 %all-to-all-start = ((bf16[16,72,128]{2,1,0:T(8,128)(2,1)}), bf16[16,72,128]{2,1,0:T(8,128)(2,1)S(1)}, u32[]{:S(2)}, u32[]{:S(2)}) async-start(bf16[16,72,128]{2,1,0:T(8,128)(2,1)} %get-tuple-element.59), calls=%async_computation | async-start | bytes 589824 | tf_op jit(solution)/shard_map/all_to_all | solution.py:625
  14.9 22.2 %copy-start.1 = (bf16[512,2,512]{2,0,1:T(8,128)(2,1)}, bf16[512,2,512]{2,0,1:T(8,128)(2,1)S(1)}, u32[]{:S(2)}) copy-start(bf16[512,2,512]{2,0,1:T(8,128)(2,1)S(1)} %copy.51) | copy-start | bytes 3145732
  24.6 12.4 %all-to-all-start.1 = ((bf16[16,64,128]{2,1,0:T(8,128)(2,1)}), bf16[16,64,128]{2,1,0:T(8,128)(2,1)S(1)}, u32[]{:S(2)}, u32[]{:S(2)}) async-start(bf16[16,64,128]{2,1,0:T(8,128)(2,1)} %scan.1), calls=%async_computation.1 | async-start | bytes 524288 | tf_op jit(solution)/shard_map/all_to_all | solution.py:631
  29.6 7.5 %copy-start.14 = (f32[512]{0:T(512)S(1)}, f32[512]{0:T(512)}, u32[]{:S(2)}) copy-start(f32[512]{0:T(512)} %param.24) | copy-start | bytes 6148
  29.6 7.5 %copy-start.22 = (f32[1,512,8]{2,1,0:T(8,128)S(1)}, f32[1,512,8]{2,1,0:T(8,128)}, u32[]{:S(2)}) copy-start(f32[1,512,8]{2,1,0:T(8,128)} %copy-done.21) | copy-start | bytes 49156
  44.1 8.2 %collective-permute-start = (bf16[4,64,2048]{2,1,0:T(8,128)(2,1)}, bf16[4,64,2048]{2,1,0:T(8,128)(2,1)S(1)}, u32[]{:S(2)}, u32[]{:S(2)}) collective-permute-start(bf16[4,64,2048]{2,1,0:T(8,128)(2,1)} %get-tuple-element.65), channel_id=1, source_target_pairs={{0,1},{1,0},{2,3},{3,2},{4,5},{5,4},{6,7},{7,6},{8,9},{9,8},{10,11... | collective-permute-start | bytes 3145736 | tf_op jit(solution)/shard_map/ppermute | solution.py:529
  50.6 5.7 %collective-permute-start.1 = (bf16[4,64,2048]{2,1,0:T(8,128)(2,1)}, bf16[4,64,2048]{2,1,0:T(8,128)(2,1)}, u32[]{:S(2)}, u32[]{:S(2)}) collective-permute-start(bf16[4,64,2048]{2,1,0:T(8,128)(2,1)} %get-tuple-element.69), channel_id=1, source_target_pairs={{0,1},{1,0},{2,3},{3,2},{4,5},{5,4},{6,7},{7,6},{8,9},{9,8},{10,11... | collective-permute-start | bytes 3145736 | tf_op jit(solution)/shard_map/ppermute | solution.py:529
  53.2 23.7 %collective-permute-start.2 = (bf16[64,2048]{1,0:T(8,128)(2,1)}, bf16[64,2048]{1,0:T(8,128)(2,1)S(1)}, u32[]{:S(2)}, u32[]{:S(2)}) collective-permute-start(bf16[64,2048]{1,0:T(8,128)(2,1)} %get-tuple-element.118), channel_id=1, source_target_pairs={{0,6},{1,7},{2,0},{3,1},{4,2},{5,3},{6,4},{7,5},{8,14},{9,15},{10,... | collective-permute-start | bytes 786440 | tf_op jit(solution)/shard_map/ppermute | solution.py:524
  56.3 10.4 %collective-permute-start.3 = (bf16[64,2048]{1,0:T(8,128)(2,1)S(1)}, bf16[64,2048]{1,0:T(8,128)(2,1)S(1)}, u32[]{:S(2)}, u32[]{:S(2)}) collective-permute-start(bf16[64,2048]{1,0:T(8,128)(2,1)S(1)} %get-tuple-element.117), channel_id=1, source_target_pairs={{0,2},{1,3},{2,4},{3,5},{4,6},{5,7},{6,0},{7,1},{8,10},{9,11},{10,... | collective-permute-start | bytes 786440 | tf_op jit(solution)/shard_map/ppermute | solution.py:519
  58.1 15.3 %copy-start.26 = (bf16[64,2,2048]{2,1,0:T(2,128)(2,1)S(1)}, bf16[64,2,2048]{2,1,0:T(2,128)(2,1)}, u32[]{:S(2)}) copy-start(bf16[64,2,2048]{2,1,0:T(2,128)(2,1)} %param.26) | copy-start | bytes 1572868
  58.1 15.2 %slice-start = ((s32[16,3]{0,1:T(4,128)}), s32[16,2]{0,1:T(2,128)S(1)}, s32[]{:S(2)}) async-start(s32[16,3]{0,1:T(4,128)} %copy-done.32), calls=%async_computation.4 | async-start | bytes 2048 | tf_op jit(solution)/shard_map/slice.1
  58.1 18.8 %collective-permute-start.5 = (bf16[64,2048]{1,0:T(8,128)(2,1)}, bf16[64,2048]{1,0:T(8,128)(2,1)}, u32[]{:S(2)}, u32[]{:S(2)}) collective-permute-start(bf16[64,2048]{1,0:T(8,128)(2,1)} %get-tuple-element.116), channel_id=1, source_target_pairs={{0,2},{1,3},{2,4},{3,5},{4,6},{5,7},{6,0},{7,1},{8,10},{9,11},{10,... | collective-permute-start | bytes 786440 | tf_op jit(solution)/shard_map/ppermute | solution.py:519
  58.8 9.1 %collective-permute-start.6 = (bf16[64,2048]{1,0:T(8,128)(2,1)S(1)}, bf16[64,2048]{1,0:T(8,128)(2,1)S(1)}, u32[]{:S(2)}, u32[]{:S(2)}) collective-permute-start(bf16[64,2048]{1,0:T(8,128)(2,1)S(1)} %get-tuple-element.115), channel_id=1, source_target_pairs={{0,6},{1,7},{2,0},{3,1},{4,2},{5,3},{6,4},{7,5},{8,14},{9,15},{10,... | collective-permute-start | bytes 786440 | tf_op jit(solution)/shard_map/ppermute | solution.py:524
  67.5 11.1 %copy-start.5 = (f32[2048]{0:T(1024)S(1)}, f32[2048]{0:T(1024)}, u32[]{:S(2)}) copy-start(f32[2048]{0:T(1024)} %param.27) | copy-start | bytes 24580
  67.5 9.5 %collective-permute-start.4 = (bf16[64,2048]{1,0:T(8,128)(2,1)}, bf16[64,2048]{1,0:T(8,128)(2,1)}, u32[]{:S(2)}, u32[]{:S(2)}) collective-permute-start(bf16[64,2048]{1,0:T(8,128)(2,1)} %fusion.1), channel_id=1, source_target_pairs={{0,2},{1,3},{2,4},{3,5},{4,6},{5,7},{6,0},{7,1},{8,10},{9,11},{10,... | collective-permute-start | bytes 786440 | tf_op jit(solution)/shard_map/ppermute | solution.py:519
  69.6 9.0 %collective-permute-start.7 = (bf16[64,2048]{1,0:T(8,128)(2,1)}, bf16[64,2048]{1,0:T(8,128)(2,1)}, u32[]{:S(2)}, u32[]{:S(2)}) collective-permute-start(bf16[64,2048]{1,0:T(8,128)(2,1)} %fusion), channel_id=1, source_target_pairs={{0,6},{1,7},{2,0},{3,1},{4,2},{5,3},{6,4},{7,5},{8,14},{9,15},{10,... | collective-permute-start | bytes 786440 | tf_op jit(solution)/shard_map/ppermute | solution.py:524
  79.6 26.3 %copy-start.7 = (bf16[1,2048,896]{2,1,0:T(8,128)(2,1)S(1)}, bf16[1,2048,896]{2,1,0:T(8,128)(2,1)}, u32[]{:S(2)}) copy-start(bf16[1,2048,896]{2,1,0:T(8,128)(2,1)} %param.29) | copy-start | bytes 11010052
  81.9 20.1 %copy-start.11 = (f32[128,2048]{1,0:T(8,128)}, f32[128,2048]{1,0:T(8,128)S(1)}, u32[]{:S(2)}) copy-start(f32[128,2048]{1,0:T(8,128)S(1)} %get-tuple-element.108.hidden) | copy-start | bytes 3145732
  81.9 24.1 %copy-start.6 = (bf16[1,2048,896]{2,1,0:T(8,128)(2,1)S(1)}, bf16[1,2048,896]{2,1,0:T(8,128)(2,1)}, u32[]{:S(2)}) copy-start(bf16[1,2048,896]{2,1,0:T(8,128)(2,1)} %param.28) | copy-start | bytes 11010052
  102.1 3.9 %collective-permute-start.10 = (bf16[256,2176]{1,0:T(8,128)(2,1)S(1)}, bf16[256,2176]{1,0:T(8,128)(2,1)S(1)}, u32[]{:S(2)}, u32[]{:S(2)}) collective-permute-start(bf16[256,2176]{1,0:T(8,128)(2,1)S(1)} %bitcast.75), channel_id=1, source_target_pairs={{0,1},{1,0},{2,3},{3,2},{4,5},{5,4},{6,7},{7,6},{8,9},{9,8},{10,11... | collective-permute-start | bytes 3342344 | tf_op jit(solution)/shard_map/ppermute | solution.py:529
  102.1 17.1 %collective-permute-start.8 = (bf16[128,2176]{1,0:T(8,128)(2,1)S(1)}, bf16[128,2176]{1,0:T(8,128)(2,1)S(1)}, u32[]{:S(2)}, u32[]{:S(2)}) collective-permute-start(bf16[128,2176]{1,0:T(8,128)(2,1)S(1)} %bitcast.104), channel_id=1, source_target_pairs={{0,2},{1,3},{2,4},{3,5},{4,6},{5,7},{6,0},{7,1},{8,10},{9,11},{10,... | collective-permute-start | bytes 1671176 | tf_op jit(solution)/shard_map/ppermute | solution.py:519
  102.2 17.0 %collective-permute-start.9 = (bf16[128,2176]{1,0:T(8,128)(2,1)S(1)}, bf16[128,2176]{1,0:T(8,128)(2,1)S(1)}, u32[]{:S(2)}, u32[]{:S(2)}) collective-permute-start(bf16[128,2176]{1,0:T(8,128)(2,1)S(1)} %bitcast.102), channel_id=1, source_target_pairs={{0,6},{1,7},{2,0},{3,1},{4,2},{5,3},{6,4},{7,5},{8,14},{9,15},{10,... | collective-permute-start | bytes 1671176 | tf_op jit(solution)/shard_map/ppermute | solution.py:524
  119.2 3.8 %collective-permute-start.14 = (bf16[128,2176]{1,0:T(8,128)(2,1)S(1)}, bf16[128,2176]{1,0:T(8,128)(2,1)S(1)}, u32[]{:S(2)}, u32[]{:S(2)}) collective-permute-start(bf16[128,2176]{1,0:T(8,128)(2,1)S(1)} %collective-permute-done.8.refs_0_), channel_id=1, source_target_pairs={{0,1},{1,0},{2,3},{3,2},{4,5},{5,4},{6,7},{7,6},{8,9},{9,8},{10,11... | collective-permute-start | bytes 1671176 | tf_op jit(solution)/shard_map/ppermute | solution.py:529
  119.2 3.8 %collective-permute-start.15 = (bf16[128,2176]{1,0:T(8,128)(2,1)S(1)}, bf16[128,2176]{1,0:T(8,128)(2,1)S(1)}, u32[]{:S(2)}, u32[]{:S(2)}) collective-permute-start(bf16[128,2176]{1,0:T(8,128)(2,1)S(1)} %collective-permute-done.9.refs_1_), channel_id=1, source_target_pairs={{0,1},{1,0},{2,3},{3,2},{4,5},{5,4},{6,7},{7,6},{8,9},{9,8},{10,11... | collective-permute-start | bytes 1671176 | tf_op jit(solution)/shard_map/ppermute | solution.py:529
  119.7 16.3 %collective-permute-start.13 = (bf16[256,2176]{1,0:T(8,128)(2,1)S(1)}, bf16[256,2176]{1,0:T(8,128)(2,1)S(1)}, u32[]{:S(2)}, u32[]{:S(2)}) collective-permute-start(bf16[256,2176]{1,0:T(8,128)(2,1)S(1)} %get-tuple-element.76), channel_id=1, source_target_pairs={{0,1},{1,0},{2,3},{3,2},{4,5},{5,4},{6,7},{7,6},{8,9},{9,8},{10,11... | collective-permute-start | bytes 3342344 | tf_op jit(solution)/shard_map/ppermute | solution.py:529
  119.7 16.3 %collective-permute-start.11 = (bf16[128,2176]{1,0:T(8,128)(2,1)S(1)}, bf16[128,2176]{1,0:T(8,128)(2,1)S(1)}, u32[]{:S(2)}, u32[]{:S(2)}) collective-permute-start(bf16[128,2176]{1,0:T(8,128)(2,1)S(1)} %collective-permute-done.8.refs_0_), channel_id=1, source_target_pairs={{0,2},{1,3},{2,4},{3,5},{4,6},{5,7},{6,0},{7,1},{8,10},{9,11},{10,... | collective-permute-start | bytes 1671176 | tf_op jit(solution)/shard_map/ppermute | solution.py:519
  120.9 15.2 %collective-permute-start.12 = (bf16[128,2176]{1,0:T(8,128)(2,1)S(1)}, bf16[128,2176]{1,0:T(8,128)(2,1)S(1)}, u32[]{:S(2)}, u32[]{:S(2)}) collective-permute-start(bf16[128,2176]{1,0:T(8,128)(2,1)S(1)} %collective-permute-done.9.refs_1_), channel_id=1, source_target_pairs={{0,6},{1,7},{2,0},{3,1},{4,2},{5,3},{6,4},{7,5},{8,14},{9,15},{10,... | collective-permute-start | bytes 1671176 | tf_op jit(solution)/shard_map/ppermute | solution.py:524
  136.1 3.5 %collective-permute-start.18 = (bf16[256,2176]{1,0:T(8,128)(2,1)S(1)}, bf16[256,2176]{1,0:T(8,128)(2,1)S(1)}, u32[]{:S(2)}, u32[]{:S(2)}) collective-permute-start(bf16[256,2176]{1,0:T(8,128)(2,1)S(1)} %get-tuple-element.83), channel_id=1, source_target_pairs={{0,1},{1,0},{2,3},{3,2},{4,5},{5,4},{6,7},{7,6},{8,9},{9,8},{10,11... | collective-permute-start | bytes 3342344 | tf_op jit(solution)/shard_map/ppermute | solution.py:529
  136.1 15.5 %collective-permute-start.16 = (bf16[128,2176]{1,0:T(8,128)(2,1)S(1)}, bf16[128,2176]{1,0:T(8,128)(2,1)S(1)}, u32[]{:S(2)}, u32[]{:S(2)}) collective-permute-start(bf16[128,2176]{1,0:T(8,128)(2,1)S(1)} %bitcast.105), channel_id=1, source_target_pairs={{0,6},{1,7},{2,0},{3,1},{4,2},{5,3},{6,4},{7,5},{8,14},{9,15},{10,... | collective-permute-start | bytes 1671176 | tf_op jit(solution)/shard_map/ppermute | solution.py:524
  139.0 16.0 %collective-permute-start.17 = (bf16[128,2176]{1,0:T(8,128)(2,1)S(1)}, bf16[128,2176]{1,0:T(8,128)(2,1)S(1)}, u32[]{:S(2)}, u32[]{:S(2)}) collective-permute-start(bf16[128,2176]{1,0:T(8,128)(2,1)S(1)} %bitcast.103), channel_id=1, source_target_pairs={{0,2},{1,3},{2,4},{3,5},{4,6},{5,7},{6,0},{7,1},{8,10},{9,11},{10,... | collective-permute-start | bytes 1671176 | tf_op jit(solution)/shard_map/ppermute | solution.py:519
  139.0 2.0 collective-permute-start.19
  139.2 2.5 %collective-permute-start.20 = (bf16[128,2176]{1,0:T(8,128)(2,1)S(1)}, bf16[128,2176]{1,0:T(8,128)(2,1)S(1)}, u32[]{:S(2)}, u32[]{:S(2)}) collective-permute-start(bf16[128,2176]{1,0:T(8,128)(2,1)S(1)} %collective-permute-done.12.refs_1_), channel_id=1, source_target_pairs={{0,1},{1,0},{2,3},{3,2},{4,5},{5,4},{6,7},{7,6},{8,9},{9,8},{10,11... | collective-permute-start | bytes 1671176 | tf_op jit(solution)/shard_map/ppermute | solution.py:529
  155.0 2.8 %collective-permute-start.21 = (bf16[256,2176]{1,0:T(8,128)(2,1)S(1)}, bf16[256,2176]{1,0:T(8,128)(2,1)S(1)}, u32[]{:S(2)}, u32[]{:S(2)}) collective-permute-start(bf16[256,2176]{1,0:T(8,128)(2,1)S(1)} %get-tuple-element.91), channel_id=1, source_target_pairs={{0,1},{1,0},{2,3},{3,2},{4,5},{5,4},{6,7},{7,6},{8,9},{9,8},{10,11... | collective-permute-start | bytes 3342344 | tf_op jit(solution)/shard_map/ppermute | solution.py:529
  155.0 15.4 %collective-permute-start.24 = (bf16[128,2176]{1,0:T(8,128)(2,1)S(1)}, bf16[128,2176]{1,0:T(8,128)(2,1)S(1)}, u32[]{:S(2)}, u32[]{:S(2)}) collective-permute-start(bf16[128,2176]{1,0:T(8,128)(2,1)S(1)} %get-tuple-element.96), channel_id=1, source_target_pairs={{0,6},{1,7},{2,0},{3,1},{4,2},{5,3},{6,4},{7,5},{8,14},{9,15},{10,... | collective-permute-start | bytes 1671176 | tf_op jit(solution)/shard_map/ppermute | solution.py:524
  155.3 16.7 %collective-permute-start.25 = (bf16[128,2176]{1,0:T(8,128)(2,1)S(1)}, bf16[128,2176]{1,0:T(8,128)(2,1)S(1)}, u32[]{:S(2)}, u32[]{:S(2)}) collective-permute-start(bf16[128,2176]{1,0:T(8,128)(2,1)S(1)} %get-tuple-element.97), channel_id=1, source_target_pairs={{0,2},{1,3},{2,4},{3,5},{4,6},{5,7},{6,0},{7,1},{8,10},{9,11},{10,... | collective-permute-start | bytes 1671176 | tf_op jit(solution)/shard_map/ppermute | solution.py:519
  157.0 2.0 collective-permute-start.26
  157.0 4.3 %collective-permute-start.27 = (bf16[128,2176]{1,0:T(8,128)(2,1)S(1)}, bf16[128,2176]{1,0:T(8,128)(2,1)S(1)}, u32[]{:S(2)}, u32[]{:S(2)}) collective-permute-start(bf16[128,2176]{1,0:T(8,128)(2,1)S(1)} %collective-permute-done.17.refs_1_), channel_id=1, source_target_pairs={{0,1},{1,0},{2,3},{3,2},{4,5},{5,4},{6,7},{7,6},{8,9},{9,8},{10,11... | collective-permute-start | bytes 1671176 | tf_op jit(solution)/shard_map/ppermute | solution.py:529
  158.0 25.2 %collective-permute-start.22 = (bf16[128,2176]{1,0:T(8,128)(2,1)S(1)}, bf16[128,2176]{1,0:T(8,128)(2,1)S(1)}, u32[]{:S(2)}, u32[]{:S(2)}) collective-permute-start(bf16[128,2176]{1,0:T(8,128)(2,1)S(1)} %get-tuple-element.94), channel_id=1, source_target_pairs={{0,2},{1,3},{2,4},{3,5},{4,6},{5,7},{6,0},{7,1},{8,10},{9,11},{10,... | collective-permute-start | bytes 1671176 | tf_op jit(solution)/shard_map/ppermute | solution.py:519
  159.0 24.2 %collective-permute-start.23 = (bf16[128,2176]{1,0:T(8,128)(2,1)S(1)}, bf16[128,2176]{1,0:T(8,128)(2,1)S(1)}, u32[]{:S(2)}, u32[]{:S(2)}) collective-permute-start(bf16[128,2176]{1,0:T(8,128)(2,1)S(1)} %get-tuple-element.95), channel_id=1, source_target_pairs={{0,6},{1,7},{2,0},{3,1},{4,2},{5,3},{6,4},{7,5},{8,14},{9,15},{10,... | collective-permute-start | bytes 1671176 | tf_op jit(solution)/shard_map/ppermute | solution.py:524
  183.2 2.8 %collective-permute-start.28 = (bf16[256,2176]{1,0:T(8,128)(2,1)S(1)}, bf16[256,2176]{1,0:T(8,128)(2,1)S(1)}, u32[]{:S(2)}, u32[]{:S(2)}) collective-permute-start(bf16[256,2176]{1,0:T(8,128)(2,1)S(1)} %get-tuple-element.104), channel_id=1, source_target_pairs={{0,1},{1,0},{2,3},{3,2},{4,5},{5,4},{6,7},{7,6},{8,9},{9,8},{10,11... | collective-permute-start | bytes 3342344 | tf_op jit(solution)/shard_map/ppermute | solution.py:529
  186.3 15.9 %collective-permute-start.29 = (bf16[128,2176]{1,0:T(8,128)(2,1)S(1)}, bf16[128,2176]{1,0:T(8,128)(2,1)S(1)}, u32[]{:S(2)}, u32[]{:S(2)}) collective-permute-start(bf16[128,2176]{1,0:T(8,128)(2,1)S(1)} %get-tuple-element.110), channel_id=1, source_target_pairs={{0,2},{1,3},{2,4},{3,5},{4,6},{5,7},{6,0},{7,1},{8,10},{9,11},{10,... | collective-permute-start | bytes 1671176 | tf_op jit(solution)/shard_map/ppermute | solution.py:519
  186.9 15.3 %collective-permute-start.30 = (bf16[128,2176]{1,0:T(8,128)(2,1)S(1)}, bf16[128,2176]{1,0:T(8,128)(2,1)S(1)}, u32[]{:S(2)}, u32[]{:S(2)}) collective-permute-start(bf16[128,2176]{1,0:T(8,128)(2,1)S(1)} %get-tuple-element.109), channel_id=1, source_target_pairs={{0,6},{1,7},{2,0},{3,1},{4,2},{5,3},{6,4},{7,5},{8,14},{9,15},{10,... | collective-permute-start | bytes 1671176 | tf_op jit(solution)/shard_map/ppermute | solution.py:524
  203.8 21.9 %copy-start.12 = (f32[128,2048]{1,0:T(8,128)S(1)}, f32[128,2048]{1,0:T(8,128)}, u32[]{:S(2)}) copy-start(f32[128,2048]{1,0:T(8,128)} %copy-done.11) | copy-start | bytes 3145732
  203.8 21.9 %copy-start.13 = (f32[4,2048]{1,0:T(4,128)S(1)}, f32[4,2048]{1,0:T(4,128)}, u32[]{:S(2)}) copy-start(f32[4,2048]{1,0:T(4,128)} %directions.1) | copy-start | bytes 98308
  203.8 21.9 %all-to-all-start.3 = ((bf16[16,16,2176]{2,1,0:T(8,128)(2,1)}), bf16[16,16,2176]{2,1,0:T(8,128)(2,1)S(1)}, u32[]{:S(2)}, u32[]{:S(2)}) async-start(bf16[16,16,2176]{2,1,0:T(8,128)(2,1)} %bitcast.29), calls=%async_computation.3 | async-start | bytes 2228224 | tf_op jit(solution)/shard_map/all_to_all | solution.py:676
  (22 other events, 46.4 us)

commit v5 on v4

--- a/solution.py
+++ b/solution.py
@@ -235,8 +235,13 @@
     gated = ssd_out * (gates / (1.0 + jnp.exp(-gates)))
     factor = lax.rsqrt(jnp.mean(gated * gated, axis=-1, keepdims=True) + 1e-05)
     normed = (gated * factor * gain[...]).astype(BF16)
-    product = jnp.dot(normed, weight[...], preferred_element_type=F32).astype(BF16)
-    held[block] = product.reshape(held.shape[1], keep, D)
+
+    @pl.loop(0, D // 512)
+    def _(index):
+        span = pl.ds(pl.multiple_of(index * 512, 512), 512)
+        product = jnp.dot(normed, weight[:, span], preferred_element_type=F32).astype(BF16)
+        held[block, :, :, span] = product.reshape(held.shape[1], keep, 512)
+
     pieces = held.shape[1]
     chip, core = lax.div(place[0], 2), lax.rem(place[0], 2)
 
@@ -564,16 +569,14 @@
     got = from_sibling(passed)
     others = from_sibling(far_top), from_sibling(far_bottom)
     near_top, near_bottom = add_up(kept[:half], got[:half]), add_up(kept[half:], got[half:])
-    near_top, near_bottom, far_top, far_bottom = after(
-        (near_top, near_bottom, far_top, far_bottom)
-    )
+    kept_top, kept_bottom = call((far_top, far_bottom))
+    others = after(others, near_top, near_bottom, kept_top)
     top_after = from_after(near_top)
     bottom_before = from_before(near_bottom)
-    kept, passed = call((far_top, far_bottom, *others))
-    after_top, before_bottom, kept, passed = after((after_top, before_bottom, kept, passed))
+    passed_top, passed_bottom = call(others)
     late = from_sibling(after_top), from_sibling(before_bottom)
-    got = from_sibling(passed)
-    far_top, far_bottom = add_up(kept[:half], got[:half]), add_up(kept[half:], got[half:])
+    far_top = add_up(kept_top, from_sibling(passed_top))
+    far_bottom = add_up(kept_bottom, from_sibling(passed_bottom))
     far_top, far_bottom, after_top, before_bottom = after(
         (far_top, far_bottom, after_top, before_bottom)
     )

time: 229 us -> 230 us (level)
    ppermute x13 -> x14, waiting for transfers between devices: 5.83 us -> 4.6 us  [from_sibling(): return lax.ppermute(values, 'exp', [(i, i ^ 1) for i in range(size)])]
    pallas_call x4 -> x5, Pallas kernels: 33.8 us -> 34.9 us  [expert_call(): pl.pallas_call(functools.partial(expert_kernel, counts), in_specs=[anywhe...]
    convert_element_type x7 -> x8, other arithmetic: 6.18 us -> 6.2 us  [add_up(): return total.astype(BF16)]
  transfers between devices with their start and end apart: 34 -> 35, of which waited for: 19 -> 15; matrix products, arithmetic and copies ran while one was open for 5% -> 5% of each run, Pallas kernels for 19% -> 19%
where the time goes in v5:
time: 230 us; the launch traced here: 229 us
  waiting for transfers between devices  74.1 us (32%)
  Pallas kernels  60.4 us (26%)
  starting transfers between devices  46.6 us (20%)
  blocking collectives  20.1 us (9%)
  local copies, waits for them, and re-layouts  19.7 us (9%)
  other arithmetic  7.81 us (3%)
    ppermute x9, waiting for transfers between devices, from_before(): lax.ppermute(values, 'exp', [(i, (i + 2) % size) for i in range(size)])  40.9 us
    pallas_call x5, Pallas kernels, expert_call(): pl.pallas_call(functools.partial(expert_kernel, counts), in_specs=[anywhe...  34.9 us
    ppermute x9, starting transfers between devices, from_after(): lax.ppermute(values, 'exp', [(i, (i - 2) % size) for i in range(size)])  25 us
    all_to_all x1, blocking collectives, on_device(): lax.all_to_all(packed.reshape(experts, FOLD, D + 128), 'seq', split_axis=...  20.1 us
    all_to_all x1, waiting for transfers between devices, on_device(): lax.all_to_all(summed.reshape(experts, FOLD, D + 128), 'seq', split_axis=...  18 us
    unnamed x72, local copies, waits for them, and re-layouts  16.1 us
    pallas_call x2, Pallas kernels, mixer_call(): pl.pallas_call(mixer_kernel, grid=(blocks,), in_specs=[pl.BlockSpec(memor...  8.96 us
    all_to_all x1, starting transfers between devices, on_device(): lax.all_to_all(parcel, 'seq', split_axis=0, concat_axis=0, tiled=True)  7.97 us
  transfers between devices with their start and end apart: 35, of which 15 were waited for; matrix products, arithmetic and copies ran while one was open for 5% of the time, Pallas kernels for 19%

profile of v5, /device:TPU:0, one launch (start us, length us, event | category | flops | bytes accessed | tf_op | source)
XLA Modules:
  0.0 229.2 jit_solution(9587364893607582700)
XLA Ops:
  0.0 1.4 copy.52
  1.6 3.8 %contrib.1 = (bf16[16,72,128]{2,1,0:T(8,128)(2,1)}, f32[2,512,128]{2,1,0:T(8,128)S(1)}) custom-call(f32[2,8,512]{2,1,0:T(8,128)S(1)} %get-tuple-element.114.decay, f32[2,8,512]{2,1,0:T(8,128)S(1)} %get-tuple-element.113.step, bf16[2,512,512]{2,1,0:T(8,128)(2,1)S(1)} %bitcast.97, bf16[2,512,128]{2,1,0:T(8,128)(2,1)S(1)} %get-tuple-element.116.writes), custom_call_target="tpu_custom_call" | custom-call | flops 1000000000 | bytes 2097152 | tf_op jit(solution)/shard_map/contrib/pallas_call | solution.py:105
  5.4 8.0 %all-to-all-start = ((bf16[16,72,128]{2,1,0:T(8,128)(2,1)}), bf16[16,72,128]{2,1,0:T(8,128)(2,1)S(1)}, u32[]{:S(2)}, u32[]{:S(2)}) async-start(bf16[16,72,128]{2,1,0:T(8,128)(2,1)} %get-tuple-element.55), calls=%async_computation | async-start | bytes 589824 | tf_op jit(solution)/shard_map/all_to_all | solution.py:628
  13.5 1.4 copy.51
  14.9 2.3 %within.2 = (f32[1,512,512]{2,1,0:T(8,128)S(1)}, f32[1,512,8]{2,1,0:T(8,128)S(1)}) custom-call(f32[2,8,512]{2,1,0:T(8,128)S(1)} %get-tuple-element.114.decay, f32[2,8,512]{2,1,0:T(8,128)S(1)} %get-tuple-element.113.step, bf16[2,512,512]{2,1,0:T(8,128)(2,1)S(1)} %bitcast.98, bf16[2,512,128]{2,1,0:T(8,128)(2,1)S(1)} %get-tuple-element.116.writes, ...), custom_call_target="tpu_custom_call" | custom-call | flops 3000000000 | bytes 2097152 | tf_op jit(solution)/shard_map/within/pallas_call | solution.py:173
  18.9 3.3 %all-to-all-done.parcels = bf16[16,72,128]{2,1,0:T(8,128)(2,1)S(1)} async-done(((bf16[16,72,128]{2,1,0:T(8,128)(2,1)}), bf16[16,72,128]{2,1,0:T(8,128)(2,1)S(1)}, u32[]{:S(2)}, u32[]{:S(2)}) %all-to-all-start) | async-done | bytes 294944 | tf_op jit(solution)/shard_map/all_to_all | solution.py:628
  22.9 1.7 scan.1
  24.6 3.9 %all-to-all-start.1 = ((bf16[16,64,128]{2,1,0:T(8,128)(2,1)}), bf16[16,64,128]{2,1,0:T(8,128)(2,1)S(1)}, u32[]{:S(2)}, u32[]{:S(2)}) async-start(bf16[16,64,128]{2,1,0:T(8,128)(2,1)} %scan.1), calls=%async_computation.1 | async-start | bytes 524288 | tf_op jit(solution)/shard_map/all_to_all | solution.py:634
  29.6 2.3 within.3
  33.6 3.5 %all-to-all-done.1.entering = bf16[16,64,128]{2,1,0:T(8,128)(2,1)S(1)} async-done(((bf16[16,64,128]{2,1,0:T(8,128)(2,1)}), bf16[16,64,128]{2,1,0:T(8,128)(2,1)S(1)}, u32[]{:S(2)}, u32[]{:S(2)}) %all-to-all-start.1) | async-done | bytes 262176 | tf_op jit(solution)/shard_map/all_to_all | solution.py:634
  37.1 1.6 copy-done.9
  38.7 1.2 copy-done.16
  39.9 4.5 %mixer.2 = (bf16[4,64,2048]{2,1,0:T(8,128)(2,1)S(1)}, bf16[4,64,2048]{2,1,0:T(8,128)(2,1)}) custom-call(s32[1]{0:T(128)} %bitcast.8.place, f32[1,512,8]{2,1,0:T(8,128)S(1)} %copy-done.22, bf16[2,512,128]{2,1,0:T(8,128)(2,1)S(1)} %get-tuple-element.115.reads, bf16[16,64,128]{2,1,0:T(8,128)(2,1)S(1)} %all-to-all-done.1.entering, ...), custom_call_target="tpu_custom_call" | custom-call | flops 2000000000 | bytes 6291456 | tf_op jit(solution)/shard_map/mixer/pallas_call | solution.py:277
  46.7 4.5 %mixer.3 = (bf16[4,64,2048]{2,1,0:T(8,128)(2,1)S(1)}, bf16[4,64,2048]{2,1,0:T(8,128)(2,1)}) custom-call(s32[1]{0:T(128)} %bitcast.8.place, f32[1,512,8]{2,1,0:T(8,128)S(1)} %copy-done.24, bf16[2,512,128]{2,1,0:T(8,128)(2,1)S(1)} %copy-done.7, bf16[16,64,128]{2,1,0:T(8,128)(2,1)S(1)} %all-to-all-done.1.entering, f32[1,512,512]{2,1,0:T(8,128)S(1)} %copy-done.18, ...), custom_call_target="tpu_custom_call" | custom-call | flops 2000000000 | bytes 6291456 | tf_op jit(solution)/shard_map/mixer/pallas_call | solution.py:277
  53.8 3.1 %collective-permute-start.2 = (bf16[64,2048]{1,0:T(8,128)(2,1)}, bf16[64,2048]{1,0:T(8,128)(2,1)S(1)}, u32[]{:S(2)}, u32[]{:S(2)}) collective-permute-start(bf16[64,2048]{1,0:T(8,128)(2,1)} %get-tuple-element.108), channel_id=1, source_target_pairs={{0,6},{1,7},{2,0},{3,1},{4,2},{5,3},{6,4},{7,5},{8,14},{9,15},{10,... | collective-permute-start | bytes 786440 | tf_op jit(solution)/shard_map/ppermute | solution.py:529
  56.9 1.9 fusion.5
  59.4 2.8 %collective-permute-start.6 = (bf16[64,2048]{1,0:T(8,128)(2,1)S(1)}, bf16[64,2048]{1,0:T(8,128)(2,1)S(1)}, u32[]{:S(2)}, u32[]{:S(2)}) collective-permute-start(bf16[64,2048]{1,0:T(8,128)(2,1)S(1)} %get-tuple-element.105), channel_id=1, source_target_pairs={{0,6},{1,7},{2,0},{3,1},{4,2},{5,3},{6,4},{7,5},{8,14},{9,15},{10,... | collective-permute-start | bytes 786440 | tf_op jit(solution)/shard_map/ppermute | solution.py:529
  62.2 5.1 %collective-permute-done.3 = bf16[64,2048]{1,0:T(8,128)(2,1)S(1)} collective-permute-done((bf16[64,2048]{1,0:T(8,128)(2,1)S(1)}, bf16[64,2048]{1,0:T(8,128)(2,1)S(1)}, u32[]{:S(2)}, u32[]{:S(2)}) %collective-permute-start.3) | collective-permute-done | bytes 262176 | tf_op jit(solution)/shard_map/ppermute | solution.py:524
  68.5 1.8 fusion
  70.3 3.7 %collective-permute-start.7 = (bf16[64,2048]{1,0:T(8,128)(2,1)}, bf16[64,2048]{1,0:T(8,128)(2,1)}, u32[]{:S(2)}, u32[]{:S(2)}) collective-permute-start(bf16[64,2048]{1,0:T(8,128)(2,1)} %fusion), channel_id=1, source_target_pairs={{0,6},{1,7},{2,0},{3,1},{4,2},{5,3},{6,4},{7,5},{8,14},{9,15},{10,... | collective-permute-start | bytes 786440 | tf_op jit(solution)/shard_map/ppermute | solution.py:529
  77.6 1.6 collective-permute-done.7.refs_3_
  80.3 2.3 dispatch.1
  82.5 20.1 %all_to_all.20 = bf16[16,16,2176]{2,1,0:T(8,128)(2,1)S(1)} all-to-all(bf16[16,16,2176]{2,1,0:T(8,128)(2,1)S(1)} %bitcast.94), channel_id=1, replica_groups=mesh['seq'=16,'exp'=8] {'seq'}, dimensions={0} | all-to-all | bytes 2228224 | tf_op jit(solution)/shard_map/all_to_all | solution.py:675
  103.0 3.8 %collective-permute-start.9 = (bf16[128,2176]{1,0:T(8,128)(2,1)S(1)}, bf16[128,2176]{1,0:T(8,128)(2,1)S(1)}, u32[]{:S(2)}, u32[]{:S(2)}) collective-permute-start(bf16[128,2176]{1,0:T(8,128)(2,1)S(1)} %bitcast.105), channel_id=1, source_target_pairs={{0,6},{1,7},{2,0},{3,1},{4,2},{5,3},{6,4},{7,5},{8,14},{9,15},{10,... | collective-permute-start | bytes 1671176 | tf_op jit(solution)/shard_map/ppermute | solution.py:529
  106.8 2.0 copy-done.2
  108.8 8.4 %expert.5 = (bf16[256,2176]{1,0:T(8,128)(2,1)S(1)}, bf16[256,2176]{1,0:T(8,128)(2,1)S(1)}) custom-call(bf16[256,2176]{1,0:T(8,128)(2,1)S(1)} %bitcast.91, bf16[256,2176]{1,0:T(8,128)(2,1)S(1)} %collective-permute-done.10.refs_1_, bf16[2048,896]{1,0:T(8,128)(2,1)S(1)} %bitcast.75, bf16[2048,896]{1,0:T(8,128)(2,1)S(1)} %bitcast.80, bf16[896,2048]{1,0:T(8,128)(2,1)S(1)} %bitcast.85), custom_call_target="tpu_custom_call" | custom-call | flops 5989466112 | bytes 15466496 | tf_op jit(solution)/shard_map/expert/pallas_call | solution.py:478
  117.3 2.7 %collective-permute-done.8.refs_0_ = bf16[128,2176]{1,0:T(8,128)(2,1)S(1)} collective-permute-done((bf16[128,2176]{1,0:T(8,128)(2,1)S(1)}, bf16[128,2176]{1,0:T(8,128)(2,1)S(1)}, u32[]{:S(2)}, u32[]{:S(2)}) %collective-permute-start.8) | collective-permute-done | bytes 557088 | tf_op jit(solution)/shard_map/ppermute | solution.py:524
  121.6 2.1 collective-permute-start.12
  123.8 8.4 %expert.6 = (bf16[256,2176]{1,0:T(8,128)(2,1)S(1)}, bf16[256,2176]{1,0:T(8,128)(2,1)S(1)}) custom-call(bf16[128,2176]{1,0:T(8,128)(2,1)S(1)} %collective-permute-done.8.refs_0_, bf16[128,2176]{1,0:T(8,128)(2,1)S(1)} %collective-permute-done.9.refs_1_, bf16[128,2176]{1,0:T(8,128)(2,1)S(1)} %collective-permute-done.14.refs_2_, ...), custom_call_target="tpu_custom_call" | custom-call | flops 5989466112 | bytes 15466496 | tf_op jit(solution)/shard_map/expert/pallas_call | solution.py:478
  132.2 4.6 %collective-permute-done.11.refs_0_ = bf16[128,2176]{1,0:T(8,128)(2,1)S(1)} collective-permute-done((bf16[128,2176]{1,0:T(8,128)(2,1)S(1)}, bf16[128,2176]{1,0:T(8,128)(2,1)S(1)}, u32[]{:S(2)}, u32[]{:S(2)}) %collective-permute-start.11) | collective-permute-done | bytes 557088 | tf_op jit(solution)/shard_map/ppermute | solution.py:524
  136.9 2.9 %collective-permute-start.21 = (bf16[128,2176]{1,0:T(8,128)(2,1)S(1)}, bf16[128,2176]{1,0:T(8,128)(2,1)S(1)}, u32[]{:S(2)}, u32[]{:S(2)}) collective-permute-start(bf16[128,2176]{1,0:T(8,128)(2,1)S(1)} %bitcast.108), channel_id=1, source_target_pairs={{0,6},{1,7},{2,0},{3,1},{4,2},{5,3},{6,4},{7,5},{8,14},{9,15},{10,... | collective-permute-start | bytes 1671176 | tf_op jit(solution)/shard_map/ppermute | solution.py:529
  140.3 4.8 %expert.7 = (bf16[128,2176]{1,0:T(8,128)(2,1)S(1)}, bf16[128,2176]{1,0:T(8,128)(2,1)S(1)}) custom-call(bf16[128,2176]{1,0:T(8,128)(2,1)S(1)} %collective-permute-done.11.refs_0_, bf16[128,2176]{1,0:T(8,128)(2,1)S(1)} %collective-permute-done.12.refs_1_, bf16[2048,896]{1,0:T(8,128)(2,1)S(1)} %bitcast.77, bf16[2048,896]{1,0:T(8,128)(2,1)S(1)} %bitcast.82, ...), custom_call_target="tpu_custom_call" | custom-call | flops 2994733056 | bytes 13238272 | tf_op jit(solution)/shard_map/expert/pallas_call | solution.py:478
  145.4 4.8 %expert.8 = (bf16[128,2176]{1,0:T(8,128)(2,1)S(1)}, bf16[128,2176]{1,0:T(8,128)(2,1)S(1)}) custom-call(bf16[128,2176]{1,0:T(8,128)(2,1)S(1)} %collective-permute-done.16.refs_0_, bf16[128,2176]{1,0:T(8,128)(2,1)S(1)} %collective-permute-done.17.refs_1_, bf16[2048,896]{1,0:T(8,128)(2,1)S(1)} %bitcast.78, bf16[2048,896]{1,0:T(8,128)(2,1)S(1)} %bitcast.83, ...), custom_call_target="tpu_custom_call" | custom-call | flops 2994733056 | bytes 13238272 | tf_op jit(solution)/shard_map/expert/pallas_call | solution.py:478
  150.5 1.8 collective-permute-done.21.refs_0_
  152.4 3.4 %collective-permute-done.22.refs_1_ = bf16[128,2176]{1,0:T(8,128)(2,1)S(1)} collective-permute-done((bf16[128,2176]{1,0:T(8,128)(2,1)S(1)}, bf16[128,2176]{1,0:T(8,128)(2,1)S(1)}, u32[]{:S(2)}, u32[]{:S(2)}) %collective-permute-start.22) | collective-permute-done | bytes 557088 | tf_op jit(solution)/shard_map/ppermute | solution.py:524
  156.6 1.2 collective-permute-start.26
  157.9 1.8 collective-permute-done.20
  160.0 3.2 %collective-permute-start.24 = (bf16[128,2176]{1,0:T(8,128)(2,1)S(1)}, bf16[128,2176]{1,0:T(8,128)(2,1)S(1)}, u32[]{:S(2)}, u32[]{:S(2)}) collective-permute-start(bf16[128,2176]{1,0:T(8,128)(2,1)S(1)} %add_convert_fusion.2), channel_id=1, source_target_pairs={{0,6},{1,7},{2,0},{3,1},{4,2},{5,3},{6,4},{7,5},{8,14},{9,15},{10,... | collective-permute-start | bytes 1671176 | tf_op jit(solution)/shard_map/ppermute | solution.py:529
  163.2 8.4 %expert.9 = (bf16[256,2176]{1,0:T(8,128)(2,1)S(1)}, bf16[256,2176]{1,0:T(8,128)(2,1)S(1)}) custom-call(bf16[128,2176]{1,0:T(8,128)(2,1)S(1)} %collective-permute-done.21.refs_0_, bf16[128,2176]{1,0:T(8,128)(2,1)S(1)} %collective-permute-done.22.refs_1_, bf16[128,2176]{1,0:T(8,128)(2,1)S(1)} %collective-permute-done.27.refs_2_, ...), custom_call_target="tpu_custom_call" | custom-call | flops 5989466112 | bytes 15466496 | tf_op jit(solution)/shard_map/expert/pallas_call | solution.py:478
  171.7 1.6 collective-permute-done.26.bottom_before
  173.3 10.7 %collective-permute-done.23 = bf16[128,2176]{1,0:T(8,128)(2,1)S(1)} collective-permute-done((bf16[128,2176]{1,0:T(8,128)(2,1)S(1)}, bf16[128,2176]{1,0:T(8,128)(2,1)S(1)}, u32[]{:S(2)}, u32[]{:S(2)}) %collective-permute-start.23) | collective-permute-done | bytes 557088 | tf_op jit(solution)/shard_map/ppermute | solution.py:524
  184.0 2.8 %collective-permute-done.29 = bf16[256,2176]{1,0:T(8,128)(2,1)S(1)} collective-permute-done((bf16[256,2176]{1,0:T(8,128)(2,1)S(1)}, bf16[256,2176]{1,0:T(8,128)(2,1)S(1)}, u32[]{:S(2)}, u32[]{:S(2)}) %collective-permute-start.29) | collective-permute-done | bytes 1114144 | tf_op jit(solution)/shard_map/ppermute | solution.py:534
  187.7 2.7 %collective-permute-start.31 = (bf16[128,2176]{1,0:T(8,128)(2,1)S(1)}, bf16[128,2176]{1,0:T(8,128)(2,1)S(1)}, u32[]{:S(2)}, u32[]{:S(2)}) collective-permute-start(bf16[128,2176]{1,0:T(8,128)(2,1)S(1)} %get-tuple-element.101), channel_id=1, source_target_pairs={{0,6},{1,7},{2,0},{3,1},{4,2},{5,3},{6,4},{7,5},{8,14},{9,15},{10,... | collective-permute-start | bytes 1671176 | tf_op jit(solution)/shard_map/ppermute | solution.py:529
  190.4 12.6 %collective-permute-done.30.top_before = bf16[128,2176]{1,0:T(8,128)(2,1)S(1)} collective-permute-done((bf16[128,2176]{1,0:T(8,128)(2,1)S(1)}, bf16[128,2176]{1,0:T(8,128)(2,1)S(1)}, u32[]{:S(2)}, u32[]{:S(2)}) %collective-permute-start.30) | collective-permute-done | bytes 557088 | tf_op jit(solution)/shard_map/ppermute | solution.py:524
  203.1 1.5 settle.1
  204.6 3.8 %all-to-all-start.3 = ((bf16[16,16,2176]{2,1,0:T(8,128)(2,1)}), bf16[16,16,2176]{2,1,0:T(8,128)(2,1)S(1)}, u32[]{:S(2)}, u32[]{:S(2)}) async-start(bf16[16,16,2176]{2,1,0:T(8,128)(2,1)} %bitcast.29), calls=%async_computation.3 | async-start | bytes 2228224 | tf_op jit(solution)/shard_map/all_to_all | solution.py:679
  208.6 18.0 %all-to-all-done.3 = bf16[16,16,2176]{2,1,0:T(8,128)(2,1)S(1)} async-done(((bf16[16,16,2176]{2,1,0:T(8,128)(2,1)}), bf16[16,16,2176]{2,1,0:T(8,128)(2,1)S(1)}, u32[]{:S(2)}, u32[]{:S(2)}) %all-to-all-start.3) | async-done | bytes 1114144 | tf_op jit(solution)/shard_map/all_to_all | solution.py:679
  226.6 2.6 %combine.1 = bf16[64,2,2048]{2,1,0:T(2,128)(2,1)} custom-call(bf16[256,2176]{1,0:T(8,128)(2,1)S(1)} %bitcast.93, s32[128,2]{1,0:T(8,128)S(1)} %bitcast_select_fusion.places, f32[128,2]{1,0:T(8,128)S(1)} %bitcast.101, f32[128,2048]{1,0:T(8,128)S(1)} %copy-done.12, f32[4,2048]{1,0:T(4,128)S(1)} %copy-done.13), custom_call_target="tpu_custom_call" | custom-call | flops 1000000000 | bytes 4194304 | tf_op jit(solution)/shard_map/combine/pallas_call | solution.py:399
  (140 shorter events, 22.1 us)
Async XLA Ops:
  1.6 35.5 %copy-start.6 = (bf16[2,512,128]{2,1,0:T(8,128)(2,1)}, bf16[2,512,128]{2,1,0:T(8,128)(2,1)S(1)}, u32[]{:S(2)}) copy-start(bf16[2,512,128]{2,1,0:T(8,128)(2,1)S(1)} %get-tuple-element.115.reads) | copy-start | bytes 786436
  1.6 11.8 %copy-start.34 = (f32[8]{0:T(128)S(1)}, f32[8]{0:T(128)}, u32[]{:S(2)}) copy-start(f32[8]{0:T(128)} %param.23) | copy-start | bytes 100
  5.4 9.6 %copy-start.19 = (f32[2,512,128]{2,1,0:T(8,128)}, f32[2,512,128]{2,1,0:T(8,128)S(1)}, u32[]{:S(2)}) copy-start(f32[2,512,128]{2,1,0:T(8,128)S(1)} %get-tuple-element.53.first) | copy-start | bytes 1572868
  5.4 16.8 %all-to-all-start = ((bf16[16,72,128]{2,1,0:T(8,128)(2,1)}), bf16[16,72,128]{2,1,0:T(8,128)(2,1)S(1)}, u32[]{:S(2)}, u32[]{:S(2)}) async-start(bf16[16,72,128]{2,1,0:T(8,128)(2,1)} %get-tuple-element.55), calls=%async_computation | async-start | bytes 589824 | tf_op jit(solution)/shard_map/all_to_all | solution.py:628
  14.9 22.2 %copy-start.4 = (bf16[512,2,512]{2,0,1:T(8,128)(2,1)}, bf16[512,2,512]{2,0,1:T(8,128)(2,1)S(1)}, u32[]{:S(2)}) copy-start(bf16[512,2,512]{2,0,1:T(8,128)(2,1)S(1)} %copy.51) | copy-start | bytes 3145732
  24.6 12.5 %all-to-all-start.1 = ((bf16[16,64,128]{2,1,0:T(8,128)(2,1)}), bf16[16,64,128]{2,1,0:T(8,128)(2,1)S(1)}, u32[]{:S(2)}, u32[]{:S(2)}) async-start(bf16[16,64,128]{2,1,0:T(8,128)(2,1)} %scan.1), calls=%async_computation.1 | async-start | bytes 524288 | tf_op jit(solution)/shard_map/all_to_all | solution.py:634
  29.6 7.5 %copy-start.22 = (f32[1,512,8]{2,1,0:T(8,128)S(1)}, f32[1,512,8]{2,1,0:T(8,128)}, u32[]{:S(2)}) copy-start(f32[1,512,8]{2,1,0:T(8,128)} %copy-done.21) | copy-start | bytes 49156
  44.4 8.5 %collective-permute-start = (bf16[4,64,2048]{2,1,0:T(8,128)(2,1)}, bf16[4,64,2048]{2,1,0:T(8,128)(2,1)S(1)}, u32[]{:S(2)}, u32[]{:S(2)}) collective-permute-start(bf16[4,64,2048]{2,1,0:T(8,128)(2,1)} %get-tuple-element.61), channel_id=1, source_target_pairs={{0,1},{1,0},{2,3},{3,2},{4,5},{5,4},{6,7},{7,6},{8,9},{9,8},{10,11... | collective-permute-start | bytes 3145736 | tf_op jit(solution)/shard_map/ppermute | solution.py:534
  51.2 5.7 %collective-permute-start.1 = (bf16[4,64,2048]{2,1,0:T(8,128)(2,1)}, bf16[4,64,2048]{2,1,0:T(8,128)(2,1)}, u32[]{:S(2)}, u32[]{:S(2)}) collective-permute-start(bf16[4,64,2048]{2,1,0:T(8,128)(2,1)} %get-tuple-element.65), channel_id=1, source_target_pairs={{0,1},{1,0},{2,3},{3,2},{4,5},{5,4},{6,7},{7,6},{8,9},{9,8},{10,11... | collective-permute-start | bytes 3145736 | tf_op jit(solution)/shard_map/ppermute | solution.py:534
  53.8 23.7 %collective-permute-start.2 = (bf16[64,2048]{1,0:T(8,128)(2,1)}, bf16[64,2048]{1,0:T(8,128)(2,1)S(1)}, u32[]{:S(2)}, u32[]{:S(2)}) collective-permute-start(bf16[64,2048]{1,0:T(8,128)(2,1)} %get-tuple-element.108), channel_id=1, source_target_pairs={{0,6},{1,7},{2,0},{3,1},{4,2},{5,3},{6,4},{7,5},{8,14},{9,15},{10,... | collective-permute-start | bytes 786440 | tf_op jit(solution)/shard_map/ppermute | solution.py:529
  56.9 10.4 %collective-permute-start.3 = (bf16[64,2048]{1,0:T(8,128)(2,1)S(1)}, bf16[64,2048]{1,0:T(8,128)(2,1)S(1)}, u32[]{:S(2)}, u32[]{:S(2)}) collective-permute-start(bf16[64,2048]{1,0:T(8,128)(2,1)S(1)} %get-tuple-element.107), channel_id=1, source_target_pairs={{0,2},{1,3},{2,4},{3,5},{4,6},{5,7},{6,0},{7,1},{8,10},{9,11},{10,... | collective-permute-start | bytes 786440 | tf_op jit(solution)/shard_map/ppermute | solution.py:524
  58.8 15.3 %copy-start.26 = (bf16[64,2,2048]{2,1,0:T(2,128)(2,1)S(1)}, bf16[64,2,2048]{2,1,0:T(2,128)(2,1)}, u32[]{:S(2)}) copy-start(bf16[64,2,2048]{2,1,0:T(2,128)(2,1)} %param.26) | copy-start | bytes 1572868
  58.8 15.2 %slice-start = ((s32[16,3]{0,1:T(4,128)}), s32[16,2]{0,1:T(2,128)S(1)}, s32[]{:S(2)}) async-start(s32[16,3]{0,1:T(4,128)} %copy-done.32), calls=%async_computation.4 | async-start | bytes 2048 | tf_op jit(solution)/shard_map/slice.1
  58.8 18.8 %collective-permute-start.5 = (bf16[64,2048]{1,0:T(8,128)(2,1)}, bf16[64,2048]{1,0:T(8,128)(2,1)}, u32[]{:S(2)}, u32[]{:S(2)}) collective-permute-start(bf16[64,2048]{1,0:T(8,128)(2,1)} %get-tuple-element.106), channel_id=1, source_target_pairs={{0,2},{1,3},{2,4},{3,5},{4,6},{5,7},{6,0},{7,1},{8,10},{9,11},{10,... | collective-permute-start | bytes 786440 | tf_op jit(solution)/shard_map/ppermute | solution.py:524
  59.4 9.1 %collective-permute-start.6 = (bf16[64,2048]{1,0:T(8,128)(2,1)S(1)}, bf16[64,2048]{1,0:T(8,128)(2,1)S(1)}, u32[]{:S(2)}, u32[]{:S(2)}) collective-permute-start(bf16[64,2048]{1,0:T(8,128)(2,1)S(1)} %get-tuple-element.105), channel_id=1, source_target_pairs={{0,6},{1,7},{2,0},{3,1},{4,2},{5,3},{6,4},{7,5},{8,14},{9,15},{10,... | collective-permute-start | bytes 786440 | tf_op jit(solution)/shard_map/ppermute | solution.py:529
  68.1 11.1 %copy-start.8 = (f32[2048]{0:T(1024)S(1)}, f32[2048]{0:T(1024)}, u32[]{:S(2)}) copy-start(f32[2048]{0:T(1024)} %param.27) | copy-start | bytes 24580
  68.1 9.5 %collective-permute-start.4 = (bf16[64,2048]{1,0:T(8,128)(2,1)}, bf16[64,2048]{1,0:T(8,128)(2,1)}, u32[]{:S(2)}, u32[]{:S(2)}) collective-permute-start(bf16[64,2048]{1,0:T(8,128)(2,1)} %fusion.1), channel_id=1, source_target_pairs={{0,2},{1,3},{2,4},{3,5},{4,6},{5,7},{6,0},{7,1},{8,10},{9,11},{10,... | collective-permute-start | bytes 786440 | tf_op jit(solution)/shard_map/ppermute | solution.py:524
  70.3 9.0 %collective-permute-start.7 = (bf16[64,2048]{1,0:T(8,128)(2,1)}, bf16[64,2048]{1,0:T(8,128)(2,1)}, u32[]{:S(2)}, u32[]{:S(2)}) collective-permute-start(bf16[64,2048]{1,0:T(8,128)(2,1)} %fusion), channel_id=1, source_target_pairs={{0,6},{1,7},{2,0},{3,1},{4,2},{5,3},{6,4},{7,5},{8,14},{9,15},{10,... | collective-permute-start | bytes 786440 | tf_op jit(solution)/shard_map/ppermute | solution.py:529
  80.3 26.5 %copy-start.1 = (bf16[1,2048,896]{2,1,0:T(8,128)(2,1)S(1)}, bf16[1,2048,896]{2,1,0:T(8,128)(2,1)}, u32[]{:S(2)}) copy-start(bf16[1,2048,896]{2,1,0:T(8,128)(2,1)} %param.29) | copy-start | bytes 11010052
  82.5 20.1 %copy-start.11 = (f32[128,2048]{1,0:T(8,128)}, f32[128,2048]{1,0:T(8,128)S(1)}, u32[]{:S(2)}) copy-start(f32[128,2048]{1,0:T(8,128)S(1)} %get-tuple-element.100.hidden) | copy-start | bytes 3145732
  82.5 24.3 %copy-start = (bf16[1,2048,896]{2,1,0:T(8,128)(2,1)S(1)}, bf16[1,2048,896]{2,1,0:T(8,128)(2,1)}, u32[]{:S(2)}) copy-start(bf16[1,2048,896]{2,1,0:T(8,128)(2,1)} %param.28) | copy-start | bytes 11010052
  102.7 4.1 %collective-permute-start.10 = (bf16[256,2176]{1,0:T(8,128)(2,1)S(1)}, bf16[256,2176]{1,0:T(8,128)(2,1)S(1)}, u32[]{:S(2)}, u32[]{:S(2)}) collective-permute-start(bf16[256,2176]{1,0:T(8,128)(2,1)S(1)} %bitcast.90), channel_id=1, source_target_pairs={{0,1},{1,0},{2,3},{3,2},{4,5},{5,4},{6,7},{7,6},{8,9},{9,8},{10,11... | collective-permute-start | bytes 3342344 | tf_op jit(solution)/shard_map/ppermute | solution.py:534
  102.8 17.2 %collective-permute-start.8 = (bf16[128,2176]{1,0:T(8,128)(2,1)S(1)}, bf16[128,2176]{1,0:T(8,128)(2,1)S(1)}, u32[]{:S(2)}, u32[]{:S(2)}) collective-permute-start(bf16[128,2176]{1,0:T(8,128)(2,1)S(1)} %bitcast.107), channel_id=1, source_target_pairs={{0,2},{1,3},{2,4},{3,5},{4,6},{5,7},{6,0},{7,1},{8,10},{9,11},{10,... | collective-permute-start | bytes 1671176 | tf_op jit(solution)/shard_map/ppermute | solution.py:524
  103.0 17.0 %collective-permute-start.9 = (bf16[128,2176]{1,0:T(8,128)(2,1)S(1)}, bf16[128,2176]{1,0:T(8,128)(2,1)S(1)}, u32[]{:S(2)}, u32[]{:S(2)}) collective-permute-start(bf16[128,2176]{1,0:T(8,128)(2,1)S(1)} %bitcast.105), channel_id=1, source_target_pairs={{0,6},{1,7},{2,0},{3,1},{4,2},{5,3},{6,4},{7,5},{8,14},{9,15},{10,... | collective-permute-start | bytes 1671176 | tf_op jit(solution)/shard_map/ppermute | solution.py:529
  120.0 3.8 %collective-permute-start.14 = (bf16[128,2176]{1,0:T(8,128)(2,1)S(1)}, bf16[128,2176]{1,0:T(8,128)(2,1)S(1)}, u32[]{:S(2)}, u32[]{:S(2)}) collective-permute-start(bf16[128,2176]{1,0:T(8,128)(2,1)S(1)} %collective-permute-done.8.refs_0_), channel_id=1, source_target_pairs={{0,1},{1,0},{2,3},{3,2},{4,5},{5,4},{6,7},{7,6},{8,9},{9,8},{10,11... | collective-permute-start | bytes 1671176 | tf_op jit(solution)/shard_map/ppermute | solution.py:534
  120.0 3.8 %collective-permute-start.15 = (bf16[128,2176]{1,0:T(8,128)(2,1)S(1)}, bf16[128,2176]{1,0:T(8,128)(2,1)S(1)}, u32[]{:S(2)}, u32[]{:S(2)}) collective-permute-start(bf16[128,2176]{1,0:T(8,128)(2,1)S(1)} %collective-permute-done.9.refs_1_), channel_id=1, source_target_pairs={{0,1},{1,0},{2,3},{3,2},{4,5},{5,4},{6,7},{7,6},{8,9},{9,8},{10,11... | collective-permute-start | bytes 1671176 | tf_op jit(solution)/shard_map/ppermute | solution.py:534
  120.5 16.3 %collective-permute-start.13 = (bf16[256,2176]{1,0:T(8,128)(2,1)S(1)}, bf16[256,2176]{1,0:T(8,128)(2,1)S(1)}, u32[]{:S(2)}, u32[]{:S(2)}) collective-permute-start(bf16[256,2176]{1,0:T(8,128)(2,1)S(1)} %get-tuple-element.72), channel_id=1, source_target_pairs={{0,1},{1,0},{2,3},{3,2},{4,5},{5,4},{6,7},{7,6},{8,9},{9,8},{10,11... | collective-permute-start | bytes 3342344 | tf_op jit(solution)/shard_map/ppermute | solution.py:534
  120.5 16.3 %collective-permute-start.11 = (bf16[128,2176]{1,0:T(8,128)(2,1)S(1)}, bf16[128,2176]{1,0:T(8,128)(2,1)S(1)}, u32[]{:S(2)}, u32[]{:S(2)}) collective-permute-start(bf16[128,2176]{1,0:T(8,128)(2,1)S(1)} %collective-permute-done.8.refs_0_), channel_id=1, source_target_pairs={{0,2},{1,3},{2,4},{3,5},{4,6},{5,7},{6,0},{7,1},{8,10},{9,11},{10,... | collective-permute-start | bytes 1671176 | tf_op jit(solution)/shard_map/ppermute | solution.py:524
  121.6 15.2 %collective-permute-start.12 = (bf16[128,2176]{1,0:T(8,128)(2,1)S(1)}, bf16[128,2176]{1,0:T(8,128)(2,1)S(1)}, u32[]{:S(2)}, u32[]{:S(2)}) collective-permute-start(bf16[128,2176]{1,0:T(8,128)(2,1)S(1)} %collective-permute-done.9.refs_1_), channel_id=1, source_target_pairs={{0,6},{1,7},{2,0},{3,1},{4,2},{5,3},{6,4},{7,5},{8,14},{9,15},{10,... | collective-permute-start | bytes 1671176 | tf_op jit(solution)/shard_map/ppermute | solution.py:529
  136.8 8.3 %collective-permute-start.18 = (bf16[256,2176]{1,0:T(8,128)(2,1)S(1)}, bf16[256,2176]{1,0:T(8,128)(2,1)S(1)}, u32[]{:S(2)}, u32[]{:S(2)}) collective-permute-start(bf16[256,2176]{1,0:T(8,128)(2,1)S(1)} %get-tuple-element.80), channel_id=1, source_target_pairs={{0,1},{1,0},{2,3},{3,2},{4,5},{5,4},{6,7},{7,6},{8,9},{9,8},{10,11... | collective-permute-start | bytes 3342344 | tf_op jit(solution)/shard_map/ppermute | solution.py:534
  136.9 15.5 %collective-permute-start.21 = (bf16[128,2176]{1,0:T(8,128)(2,1)S(1)}, bf16[128,2176]{1,0:T(8,128)(2,1)S(1)}, u32[]{:S(2)}, u32[]{:S(2)}) collective-permute-start(bf16[128,2176]{1,0:T(8,128)(2,1)S(1)} %bitcast.108), channel_id=1, source_target_pairs={{0,6},{1,7},{2,0},{3,1},{4,2},{5,3},{6,4},{7,5},{8,14},{9,15},{10,... | collective-permute-start | bytes 1671176 | tf_op jit(solution)/shard_map/ppermute | solution.py:529
  139.8 16.0 %collective-permute-start.22 = (bf16[128,2176]{1,0:T(8,128)(2,1)S(1)}, bf16[128,2176]{1,0:T(8,128)(2,1)S(1)}, u32[]{:S(2)}, u32[]{:S(2)}) collective-permute-start(bf16[128,2176]{1,0:T(8,128)(2,1)S(1)} %bitcast.106), channel_id=1, source_target_pairs={{0,2},{1,3},{2,4},{3,5},{4,6},{5,7},{6,0},{7,1},{8,10},{9,11},{10,... | collective-permute-start | bytes 1671176 | tf_op jit(solution)/shard_map/ppermute | solution.py:524
  139.8 5.6 %collective-permute-start.16 = (bf16[128,2176]{1,0:T(8,128)(2,1)S(1)}, bf16[128,2176]{1,0:T(8,128)(2,1)S(1)}, u32[]{:S(2)}, u32[]{:S(2)}) collective-permute-start(bf16[128,2176]{1,0:T(8,128)(2,1)S(1)} %collective-permute-done.11.refs_0_), channel_id=1, source_target_pairs={{0,1},{1,0},{2,3},{3,2},{4,5},{5,4},{6,7},{7,6},{8,9},{9,8},{10,11... | collective-permute-start | bytes 1671176 | tf_op jit(solution)/shard_map/ppermute | solution.py:534
  140.0 5.4 %collective-permute-start.17 = (bf16[128,2176]{1,0:T(8,128)(2,1)S(1)}, bf16[128,2176]{1,0:T(8,128)(2,1)S(1)}, u32[]{:S(2)}, u32[]{:S(2)}) collective-permute-start(bf16[128,2176]{1,0:T(8,128)(2,1)S(1)} %collective-permute-done.12.refs_1_), channel_id=1, source_target_pairs={{0,1},{1,0},{2,3},{3,2},{4,5},{5,4},{6,7},{7,6},{8,9},{9,8},{10,11... | collective-permute-start | bytes 1671176 | tf_op jit(solution)/shard_map/ppermute | solution.py:534
  150.2 7.6 %collective-permute-start.19 = (bf16[128,2176]{1,0:T(8,128)(2,1)S(1)}, bf16[128,2176]{1,0:T(8,128)(2,1)S(1)}, u32[]{:S(2)}, u32[]{:S(2)}) collective-permute-start(bf16[128,2176]{1,0:T(8,128)(2,1)S(1)} %get-tuple-element.83), channel_id=1, source_target_pairs={{0,1},{1,0},{2,3},{3,2},{4,5},{5,4},{6,7},{7,6},{8,9},{9,8},{10,11... | collective-permute-start | bytes 1671176 | tf_op jit(solution)/shard_map/ppermute | solution.py:534
  152.4 7.6 %collective-permute-start.27 = (bf16[128,2176]{1,0:T(8,128)(2,1)S(1)}, bf16[128,2176]{1,0:T(8,128)(2,1)S(1)}, u32[]{:S(2)}, u32[]{:S(2)}) collective-permute-start(bf16[128,2176]{1,0:T(8,128)(2,1)S(1)} %collective-permute-done.21.refs_0_), channel_id=1, source_target_pairs={{0,1},{1,0},{2,3},{3,2},{4,5},{5,4},{6,7},{7,6},{8,9},{9,8},{10,11... | collective-permute-start | bytes 1671176 | tf_op jit(solution)/shard_map/ppermute | solution.py:534
  155.8 7.4 %collective-permute-start.28 = (bf16[128,2176]{1,0:T(8,128)(2,1)S(1)}, bf16[128,2176]{1,0:T(8,128)(2,1)S(1)}, u32[]{:S(2)}, u32[]{:S(2)}) collective-permute-start(bf16[128,2176]{1,0:T(8,128)(2,1)S(1)} %collective-permute-done.22.refs_1_), channel_id=1, source_target_pairs={{0,1},{1,0},{2,3},{3,2},{4,5},{5,4},{6,7},{7,6},{8,9},{9,8},{10,11... | collective-permute-start | bytes 1671176 | tf_op jit(solution)/shard_map/ppermute | solution.py:534
  155.8 15.9 %collective-permute-start.25 = (bf16[128,2176]{1,0:T(8,128)(2,1)S(1)}, bf16[128,2176]{1,0:T(8,128)(2,1)S(1)}, u32[]{:S(2)}, u32[]{:S(2)}) collective-permute-start(bf16[128,2176]{1,0:T(8,128)(2,1)S(1)} %get-tuple-element.104), channel_id=1, source_target_pairs={{0,6},{1,7},{2,0},{3,1},{4,2},{5,3},{6,4},{7,5},{8,14},{9,15},{10,... | collective-permute-start | bytes 1671176 | tf_op jit(solution)/shard_map/ppermute | solution.py:529
  156.6 16.7 %collective-permute-start.26 = (bf16[128,2176]{1,0:T(8,128)(2,1)S(1)}, bf16[128,2176]{1,0:T(8,128)(2,1)S(1)}, u32[]{:S(2)}, u32[]{:S(2)}) collective-permute-start(bf16[128,2176]{1,0:T(8,128)(2,1)S(1)} %get-tuple-element.103), channel_id=1, source_target_pairs={{0,2},{1,3},{2,4},{3,5},{4,6},{5,7},{6,0},{7,1},{8,10},{9,11},{10,... | collective-permute-start | bytes 1671176 | tf_op jit(solution)/shard_map/ppermute | solution.py:524
  157.8 2.0 collective-permute-start.20
  159.9 24.1 %collective-permute-start.23 = (bf16[128,2176]{1,0:T(8,128)(2,1)S(1)}, bf16[128,2176]{1,0:T(8,128)(2,1)S(1)}, u32[]{:S(2)}, u32[]{:S(2)}) collective-permute-start(bf16[128,2176]{1,0:T(8,128)(2,1)S(1)} %add_convert_fusion.3), channel_id=1, source_target_pairs={{0,2},{1,3},{2,4},{3,5},{4,6},{5,7},{6,0},{7,1},{8,10},{9,11},{10,... | collective-permute-start | bytes 1671176 | tf_op jit(solution)/shard_map/ppermute | solution.py:524
  160.0 24.0 %collective-permute-start.24 = (bf16[128,2176]{1,0:T(8,128)(2,1)S(1)}, bf16[128,2176]{1,0:T(8,128)(2,1)S(1)}, u32[]{:S(2)}, u32[]{:S(2)}) collective-permute-start(bf16[128,2176]{1,0:T(8,128)(2,1)S(1)} %add_convert_fusion.2), channel_id=1, source_target_pairs={{0,6},{1,7},{2,0},{3,1},{4,2},{5,3},{6,4},{7,5},{8,14},{9,15},{10,... | collective-permute-start | bytes 1671176 | tf_op jit(solution)/shard_map/ppermute | solution.py:529
  184.0 2.8 %collective-permute-start.29 = (bf16[256,2176]{1,0:T(8,128)(2,1)S(1)}, bf16[256,2176]{1,0:T(8,128)(2,1)S(1)}, u32[]{:S(2)}, u32[]{:S(2)}) collective-permute-start(bf16[256,2176]{1,0:T(8,128)(2,1)S(1)} %get-tuple-element.96), channel_id=1, source_target_pairs={{0,1},{1,0},{2,3},{3,2},{4,5},{5,4},{6,7},{7,6},{8,9},{9,8},{10,11... | collective-permute-start | bytes 3342344 | tf_op jit(solution)/shard_map/ppermute | solution.py:534
  187.1 15.9 %collective-permute-start.30 = (bf16[128,2176]{1,0:T(8,128)(2,1)S(1)}, bf16[128,2176]{1,0:T(8,128)(2,1)S(1)}, u32[]{:S(2)}, u32[]{:S(2)}) collective-permute-start(bf16[128,2176]{1,0:T(8,128)(2,1)S(1)} %get-tuple-element.102), channel_id=1, source_target_pairs={{0,2},{1,3},{2,4},{3,5},{4,6},{5,7},{6,0},{7,1},{8,10},{9,11},{10,... | collective-permute-start | bytes 1671176 | tf_op jit(solution)/shard_map/ppermute | solution.py:524
  187.7 15.4 %collective-permute-start.31 = (bf16[128,2176]{1,0:T(8,128)(2,1)S(1)}, bf16[128,2176]{1,0:T(8,128)(2,1)S(1)}, u32[]{:S(2)}, u32[]{:S(2)}) collective-permute-start(bf16[128,2176]{1,0:T(8,128)(2,1)S(1)} %get-tuple-element.101), channel_id=1, source_target_pairs={{0,6},{1,7},{2,0},{3,1},{4,2},{5,3},{6,4},{7,5},{8,14},{9,15},{10,... | collective-permute-start | bytes 1671176 | tf_op jit(solution)/shard_map/ppermute | solution.py:529
  204.6 21.9 %copy-start.12 = (f32[128,2048]{1,0:T(8,128)S(1)}, f32[128,2048]{1,0:T(8,128)}, u32[]{:S(2)}) copy-start(f32[128,2048]{1,0:T(8,128)} %copy-done.11) | copy-start | bytes 3145732
  204.6 21.9 %copy-start.13 = (f32[4,2048]{1,0:T(4,128)S(1)}, f32[4,2048]{1,0:T(4,128)}, u32[]{:S(2)}) copy-start(f32[4,2048]{1,0:T(4,128)} %directions.1) | copy-start | bytes 98308
  204.6 21.9 %all-to-all-start.3 = ((bf16[16,16,2176]{2,1,0:T(8,128)(2,1)}), bf16[16,16,2176]{2,1,0:T(8,128)(2,1)S(1)}, u32[]{:S(2)}, u32[]{:S(2)}) async-start(bf16[16,16,2176]{2,1,0:T(8,128)(2,1)} %bitcast.29), calls=%async_computation.3 | async-start | bytes 2228224 | tf_op jit(solution)/shard_map/all_to_all | solution.py:679
  (23 other events, 55.1 us)

commit v6 on v4

--- a/solution.py
+++ b/solution.py
@@ -318,7 +318,7 @@
     for index, (own, got) in enumerate(((own_top, got_top), (own_bottom, got_bottom))):
         span = pl.ds(index * half, half)
         hidden[span, :] = (
-            residual[span, :].astype(F32)
+            residual[:, index, :].astype(F32)
             + (own[0].astype(F32) + got[0].astype(F32))
             + others[2 * index][...].astype(F32)
             + others[2 * index + 1][...].astype(F32)
@@ -337,7 +337,7 @@
 
 
 def dispatch_call(residual, gain, places, owns, others, experts):
-    rows, half = residual.shape[0], residual.shape[0] // 2
+    rows, half = 2 * residual.shape[0], residual.shape[0]
     count = experts * FOLD
     whole = lambda shape: pl.BlockSpec(shape, lambda i: (0,) * len(shape))
     return pl.pallas_call(
@@ -662,7 +662,7 @@
         ranked < FOLD, picks * FOLD + ranked, experts * FOLD + picks
     ).reshape(rows_keep, 2)
     hidden_state, packed = dispatch_call(
-        swap(resid).reshape(rows_keep, D),
+        resid,
         moe_gain[None, :],
         places.T,
         (kept, got, kept_late, got_late),

time: 229 us -> 230 us (level)
    unnamed x72 -> x70, local copies, waits for them, and re-layouts: 16.1 us -> 16.1 us
  transfers between devices with their start and end apart: 34 -> 34, of which waited for: 19 -> 20; matrix products, arithmetic and copies ran while one was open for 5% -> 5% of each run, Pallas kernels for 19% -> 19%
where the time goes in v6:
time: 230 us; the launch traced here: 229 us
  waiting for transfers between devices  77 us (33%)
  Pallas kernels  58.9 us (26%)
  starting transfers between devices  45.7 us (20%)
  blocking collectives  20.1 us (9%)
  local copies, waits for them, and re-layouts  18.8 us (8%)
  other arithmetic  7.79 us (3%)
    ppermute x9, waiting for transfers between devices, from_before(): lax.ppermute(values, 'exp', [(i, (i + 2) % size) for i in range(size)])  42.2 us
    pallas_call x4, Pallas kernels, expert_call(): pl.pallas_call(functools.partial(expert_kernel, counts), in_specs=[anywhe...  33.8 us
    ppermute x9, starting transfers between devices, from_after(): lax.ppermute(values, 'exp', [(i, (i - 2) % size) for i in range(size)])  23.7 us
    all_to_all x1, blocking collectives, on_device(): lax.all_to_all(packed.reshape(experts, FOLD, D + 128), 'seq', split_axis=...  20.1 us
    all_to_all x1, waiting for transfers between devices, on_device(): lax.all_to_all(summed.reshape(experts, FOLD, D + 128), 'seq', split_axis=...  18 us
    unnamed x70, local copies, waits for them, and re-layouts  16.1 us
    pallas_call x2, Pallas kernels, mixer_call(): pl.pallas_call(mixer_kernel, grid=(blocks,), in_specs=[pl.BlockSpec(memor...  8.36 us
    all_to_all x1, starting transfers between devices, on_device(): lax.all_to_all(parcel, 'seq', split_axis=0, concat_axis=0, tiled=True)  7.97 us
  transfers between devices with their start and end apart: 34, of which 20 were waited for; matrix products, arithmetic and copies ran while one was open for 5% of the time, Pallas kernels for 19%

profile of v6, /device:TPU:0, one launch (start us, length us, event | category | flops | bytes accessed | tf_op | source)
XLA Modules:
  0.0 228.8 jit_solution(8303746150573541915)
XLA Ops:
  0.0 1.4 copy.50
  1.6 3.8 %contrib.1 = (bf16[16,72,128]{2,1,0:T(8,128)(2,1)}, f32[2,512,128]{2,1,0:T(8,128)S(1)}) custom-call(f32[2,8,512]{2,1,0:T(8,128)S(1)} %get-tuple-element.124.decay, f32[2,8,512]{2,1,0:T(8,128)S(1)} %get-tuple-element.123.step, bf16[2,512,512]{2,1,0:T(8,128)(2,1)S(1)} %bitcast.79, bf16[2,512,128]{2,1,0:T(8,128)(2,1)S(1)} %get-tuple-element.126.writes), custom_call_target="tpu_custom_call" | custom-call | flops 1000000000 | bytes 2097152 | tf_op jit(solution)/shard_map/contrib/pallas_call | solution.py:105
  5.4 8.0 %all-to-all-start = ((bf16[16,72,128]{2,1,0:T(8,128)(2,1)}), bf16[16,72,128]{2,1,0:T(8,128)(2,1)S(1)}, u32[]{:S(2)}, u32[]{:S(2)}) async-start(bf16[16,72,128]{2,1,0:T(8,128)(2,1)} %get-tuple-element.59), calls=%async_computation | async-start | bytes 589824 | tf_op jit(solution)/shard_map/all_to_all | solution.py:625
  13.5 1.4 copy.49
  14.9 2.3 %within.2 = (f32[1,512,512]{2,1,0:T(8,128)S(1)}, f32[1,512,8]{2,1,0:T(8,128)S(1)}) custom-call(f32[2,8,512]{2,1,0:T(8,128)S(1)} %get-tuple-element.124.decay, f32[2,8,512]{2,1,0:T(8,128)S(1)} %get-tuple-element.123.step, bf16[2,512,512]{2,1,0:T(8,128)(2,1)S(1)} %bitcast.80, bf16[2,512,128]{2,1,0:T(8,128)(2,1)S(1)} %get-tuple-element.126.writes, ...), custom_call_target="tpu_custom_call" | custom-call | flops 3000000000 | bytes 2097152 | tf_op jit(solution)/shard_map/within/pallas_call | solution.py:173
  18.9 3.3 %all-to-all-done.parcels = bf16[16,72,128]{2,1,0:T(8,128)(2,1)S(1)} async-done(((bf16[16,72,128]{2,1,0:T(8,128)(2,1)}), bf16[16,72,128]{2,1,0:T(8,128)(2,1)S(1)}, u32[]{:S(2)}, u32[]{:S(2)}) %all-to-all-start) | async-done | bytes 294944 | tf_op jit(solution)/shard_map/all_to_all | solution.py:625
  22.9 1.7 scan.1
  24.7 3.9 %all-to-all-start.1 = ((bf16[16,64,128]{2,1,0:T(8,128)(2,1)}), bf16[16,64,128]{2,1,0:T(8,128)(2,1)S(1)}, u32[]{:S(2)}, u32[]{:S(2)}) async-start(bf16[16,64,128]{2,1,0:T(8,128)(2,1)} %scan.1), calls=%async_computation.1 | async-start | bytes 524288 | tf_op jit(solution)/shard_map/all_to_all | solution.py:631
  29.7 2.3 within.3
  33.7 3.5 %all-to-all-done.1.entering = bf16[16,64,128]{2,1,0:T(8,128)(2,1)S(1)} async-done(((bf16[16,64,128]{2,1,0:T(8,128)(2,1)}), bf16[16,64,128]{2,1,0:T(8,128)(2,1)S(1)}, u32[]{:S(2)}, u32[]{:S(2)}) %all-to-all-start.1) | async-done | bytes 262176 | tf_op jit(solution)/shard_map/all_to_all | solution.py:631
  37.2 1.6 copy-done.9
  38.7 1.2 copy-done.16
  40.0 4.2 %mixer.2 = (bf16[4,64,2048]{2,1,0:T(8,128)(2,1)S(1)}, bf16[4,64,2048]{2,1,0:T(8,128)(2,1)}) custom-call(s32[1]{0:T(128)} %bitcast.6.place, f32[1,512,8]{2,1,0:T(8,128)S(1)} %copy-done.22, bf16[2,512,128]{2,1,0:T(8,128)(2,1)S(1)} %get-tuple-element.125.reads, bf16[16,64,128]{2,1,0:T(8,128)(2,1)S(1)} %all-to-all-done.1.entering, ...), custom_call_target="tpu_custom_call" | custom-call | flops 2000000000 | bytes 6291456 | tf_op jit(solution)/shard_map/mixer/pallas_call | solution.py:272
  44.3 1.2 copy-done.1
  46.5 4.2 %mixer.3 = (bf16[4,64,2048]{2,1,0:T(8,128)(2,1)S(1)}, bf16[4,64,2048]{2,1,0:T(8,128)(2,1)}) custom-call(s32[1]{0:T(128)} %bitcast.6.place, f32[1,512,8]{2,1,0:T(8,128)S(1)} %copy-done.24, bf16[2,512,128]{2,1,0:T(8,128)(2,1)S(1)} %copy-done.4, bf16[16,64,128]{2,1,0:T(8,128)(2,1)S(1)} %all-to-all-done.1.entering, f32[1,512,512]{2,1,0:T(8,128)S(1)} %copy-done.18, ...), custom_call_target="tpu_custom_call" | custom-call | flops 2000000000 | bytes 6291456 | tf_op jit(solution)/shard_map/mixer/pallas_call | solution.py:272
  53.2 3.1 %collective-permute-start.2 = (bf16[64,2048]{1,0:T(8,128)(2,1)}, bf16[64,2048]{1,0:T(8,128)(2,1)S(1)}, u32[]{:S(2)}, u32[]{:S(2)}) collective-permute-start(bf16[64,2048]{1,0:T(8,128)(2,1)} %get-tuple-element.118), channel_id=1, source_target_pairs={{0,6},{1,7},{2,0},{3,1},{4,2},{5,3},{6,4},{7,5},{8,14},{9,15},{10,... | collective-permute-start | bytes 786440 | tf_op jit(solution)/shard_map/ppermute | solution.py:524
  56.3 1.9 fusion.5
  58.7 2.8 %collective-permute-start.6 = (bf16[64,2048]{1,0:T(8,128)(2,1)S(1)}, bf16[64,2048]{1,0:T(8,128)(2,1)S(1)}, u32[]{:S(2)}, u32[]{:S(2)}) collective-permute-start(bf16[64,2048]{1,0:T(8,128)(2,1)S(1)} %get-tuple-element.115), channel_id=1, source_target_pairs={{0,6},{1,7},{2,0},{3,1},{4,2},{5,3},{6,4},{7,5},{8,14},{9,15},{10,... | collective-permute-start | bytes 786440 | tf_op jit(solution)/shard_map/ppermute | solution.py:524
  61.5 5.2 %collective-permute-done.3 = bf16[64,2048]{1,0:T(8,128)(2,1)S(1)} collective-permute-done((bf16[64,2048]{1,0:T(8,128)(2,1)S(1)}, bf16[64,2048]{1,0:T(8,128)(2,1)S(1)}, u32[]{:S(2)}, u32[]{:S(2)}) %collective-permute-start.3) | collective-permute-done | bytes 262176 | tf_op jit(solution)/shard_map/ppermute | solution.py:519
  67.9 1.7 fusion
  69.7 3.7 %collective-permute-start.7 = (bf16[64,2048]{1,0:T(8,128)(2,1)}, bf16[64,2048]{1,0:T(8,128)(2,1)}, u32[]{:S(2)}, u32[]{:S(2)}) collective-permute-start(bf16[64,2048]{1,0:T(8,128)(2,1)} %fusion), channel_id=1, source_target_pairs={{0,6},{1,7},{2,0},{3,1},{4,2},{5,3},{6,4},{7,5},{8,14},{9,15},{10,... | collective-permute-start | bytes 786440 | tf_op jit(solution)/shard_map/ppermute | solution.py:524
  76.9 1.8 collective-permute-done.7.refs_3_
  79.7 2.6 %dispatch.1 = (f32[128,2048]{1,0:T(8,128)S(1)}, bf16[256,2176]{1,0:T(8,128)(2,1)S(1)}) custom-call(bf16[64,2,2048]{2,1,0:T(2,128)(2,1)S(1)} %copy-done.2, f32[1,2048]{1,0:T(1,128)S(1)} %bitcast.84, s32[2,128]{1,0:T(2,128)S(1)} %copy.39.places, bf16[4,64,2048]{2,1,0:T(8,128)(2,1)S(1)} %get-tuple-element.64.own_top, ...), custom_call_target="tpu_custom_call" | custom-call | flops 200000000 | bytes 5242880 | tf_op jit(solution)/shard_map/dispatch/pallas_call | solution.py:343
  82.3 20.1 %all_to_all.20 = bf16[16,16,2176]{2,1,0:T(8,128)(2,1)S(1)} all-to-all(bf16[16,16,2176]{2,1,0:T(8,128)(2,1)S(1)} %bitcast.76), channel_id=1, replica_groups=mesh['seq'=16,'exp'=8] {'seq'}, dimensions={0} | all-to-all | bytes 2228224 | tf_op jit(solution)/shard_map/all_to_all | solution.py:672
  102.6 3.8 %collective-permute-start.9 = (bf16[128,2176]{1,0:T(8,128)(2,1)S(1)}, bf16[128,2176]{1,0:T(8,128)(2,1)S(1)}, u32[]{:S(2)}, u32[]{:S(2)}) collective-permute-start(bf16[128,2176]{1,0:T(8,128)(2,1)S(1)} %bitcast.99), channel_id=1, source_target_pairs={{0,6},{1,7},{2,0},{3,1},{4,2},{5,3},{6,4},{7,5},{8,14},{9,15},{10,... | collective-permute-start | bytes 1671176 | tf_op jit(solution)/shard_map/ppermute | solution.py:524
  106.4 2.0 copy-done.8
  108.4 8.4 %expert.4 = (bf16[256,2176]{1,0:T(8,128)(2,1)S(1)}, bf16[256,2176]{1,0:T(8,128)(2,1)S(1)}) custom-call(bf16[256,2176]{1,0:T(8,128)(2,1)S(1)} %bitcast.74, bf16[256,2176]{1,0:T(8,128)(2,1)S(1)} %collective-permute-done.10.refs_1_, bf16[2048,896]{1,0:T(8,128)(2,1)S(1)} %bitcast.85, bf16[2048,896]{1,0:T(8,128)(2,1)S(1)} %bitcast.89, bf16[896,2048]{1,0:T(8,128)(2,1)S(1)} %bitcast.93), custom_call_target="tpu_custom_call" | custom-call | flops 5989466112 | bytes 15466496 | tf_op jit(solution)/shard_map/expert/pallas_call | solution.py:473
  116.8 2.7 %collective-permute-done.8.refs_0_ = bf16[128,2176]{1,0:T(8,128)(2,1)S(1)} collective-permute-done((bf16[128,2176]{1,0:T(8,128)(2,1)S(1)}, bf16[128,2176]{1,0:T(8,128)(2,1)S(1)}, u32[]{:S(2)}, u32[]{:S(2)}) %collective-permute-start.8) | collective-permute-done | bytes 557088 | tf_op jit(solution)/shard_map/ppermute | solution.py:519
  121.2 2.1 collective-permute-start.12
  123.3 8.4 %expert.5 = (bf16[256,2176]{1,0:T(8,128)(2,1)S(1)}, bf16[256,2176]{1,0:T(8,128)(2,1)S(1)}) custom-call(bf16[128,2176]{1,0:T(8,128)(2,1)S(1)} %collective-permute-done.8.refs_0_, bf16[128,2176]{1,0:T(8,128)(2,1)S(1)} %collective-permute-done.9.refs_1_, bf16[128,2176]{1,0:T(8,128)(2,1)S(1)} %collective-permute-done.14.refs_2_, ...), custom_call_target="tpu_custom_call" | custom-call | flops 5989466112 | bytes 15466496 | tf_op jit(solution)/shard_map/expert/pallas_call | solution.py:473
  131.8 4.6 %collective-permute-done.11.refs_0_ = bf16[128,2176]{1,0:T(8,128)(2,1)S(1)} collective-permute-done((bf16[128,2176]{1,0:T(8,128)(2,1)S(1)}, bf16[128,2176]{1,0:T(8,128)(2,1)S(1)}, u32[]{:S(2)}, u32[]{:S(2)}) %collective-permute-start.11) | collective-permute-done | bytes 557088 | tf_op jit(solution)/shard_map/ppermute | solution.py:519
  136.4 2.9 %collective-permute-start.16 = (bf16[128,2176]{1,0:T(8,128)(2,1)S(1)}, bf16[128,2176]{1,0:T(8,128)(2,1)S(1)}, u32[]{:S(2)}, u32[]{:S(2)}) collective-permute-start(bf16[128,2176]{1,0:T(8,128)(2,1)S(1)} %bitcast.102), channel_id=1, source_target_pairs={{0,6},{1,7},{2,0},{3,1},{4,2},{5,3},{6,4},{7,5},{8,14},{9,15},{10,... | collective-permute-start | bytes 1671176 | tf_op jit(solution)/shard_map/ppermute | solution.py:524
  140.2 1.2 collective-permute-done.19.refs_2_
  142.1 8.4 %expert.6 = (bf16[256,2176]{1,0:T(8,128)(2,1)S(1)}, bf16[256,2176]{1,0:T(8,128)(2,1)S(1)}) custom-call(bf16[128,2176]{1,0:T(8,128)(2,1)S(1)} %collective-permute-done.11.refs_0_, bf16[128,2176]{1,0:T(8,128)(2,1)S(1)} %collective-permute-done.12.refs_1_, bf16[128,2176]{1,0:T(8,128)(2,1)S(1)} %collective-permute-done.19.refs_2_, ...), custom_call_target="tpu_custom_call" | custom-call | flops 5989466112 | bytes 15466496 | tf_op jit(solution)/shard_map/expert/pallas_call | solution.py:473
  150.6 1.3 collective-permute-done.16.refs_0_
  151.9 3.4 %collective-permute-done.17.refs_1_ = bf16[128,2176]{1,0:T(8,128)(2,1)S(1)} collective-permute-done((bf16[128,2176]{1,0:T(8,128)(2,1)S(1)}, bf16[128,2176]{1,0:T(8,128)(2,1)S(1)}, u32[]{:S(2)}, u32[]{:S(2)}) %collective-permute-start.17) | collective-permute-done | bytes 557088 | tf_op jit(solution)/shard_map/ppermute | solution.py:519
  155.6 1.7 collective-permute-start.25
  159.3 2.3 %collective-permute-start.23 = (bf16[128,2176]{1,0:T(8,128)(2,1)S(1)}, bf16[128,2176]{1,0:T(8,128)(2,1)S(1)}, u32[]{:S(2)}, u32[]{:S(2)}) collective-permute-start(bf16[128,2176]{1,0:T(8,128)(2,1)S(1)} %get-tuple-element.95), channel_id=1, source_target_pairs={{0,6},{1,7},{2,0},{3,1},{4,2},{5,3},{6,4},{7,5},{8,14},{9,15},{10,... | collective-permute-start | bytes 1671176 | tf_op jit(solution)/shard_map/ppermute | solution.py:524
  161.7 8.4 %expert.7 = (bf16[256,2176]{1,0:T(8,128)(2,1)S(1)}, bf16[256,2176]{1,0:T(8,128)(2,1)S(1)}) custom-call(bf16[128,2176]{1,0:T(8,128)(2,1)S(1)} %collective-permute-done.16.refs_0_, bf16[128,2176]{1,0:T(8,128)(2,1)S(1)} %collective-permute-done.17.refs_1_, bf16[128,2176]{1,0:T(8,128)(2,1)S(1)} %collective-permute-done.26.refs_2_, ...), custom_call_target="tpu_custom_call" | custom-call | flops 5989466112 | bytes 15466496 | tf_op jit(solution)/shard_map/expert/pallas_call | solution.py:473
  170.8 1.5 collective-permute-done.25.bottom_before
  172.3 11.2 %collective-permute-done.22 = bf16[128,2176]{1,0:T(8,128)(2,1)S(1)} collective-permute-done((bf16[128,2176]{1,0:T(8,128)(2,1)S(1)}, bf16[128,2176]{1,0:T(8,128)(2,1)S(1)}, u32[]{:S(2)}, u32[]{:S(2)}) %collective-permute-start.22) | collective-permute-done | bytes 557088 | tf_op jit(solution)/shard_map/ppermute | solution.py:519
  183.5 2.8 %collective-permute-done.28 = bf16[256,2176]{1,0:T(8,128)(2,1)S(1)} collective-permute-done((bf16[256,2176]{1,0:T(8,128)(2,1)S(1)}, bf16[256,2176]{1,0:T(8,128)(2,1)S(1)}, u32[]{:S(2)}, u32[]{:S(2)}) %collective-permute-start.28) | collective-permute-done | bytes 1114144 | tf_op jit(solution)/shard_map/ppermute | solution.py:529
  187.3 2.7 %collective-permute-start.30 = (bf16[128,2176]{1,0:T(8,128)(2,1)S(1)}, bf16[128,2176]{1,0:T(8,128)(2,1)S(1)}, u32[]{:S(2)}, u32[]{:S(2)}) collective-permute-start(bf16[128,2176]{1,0:T(8,128)(2,1)S(1)} %get-tuple-element.109), channel_id=1, source_target_pairs={{0,6},{1,7},{2,0},{3,1},{4,2},{5,3},{6,4},{7,5},{8,14},{9,15},{10,... | collective-permute-start | bytes 1671176 | tf_op jit(solution)/shard_map/ppermute | solution.py:524
  190.0 12.6 %collective-permute-done.29.top_before = bf16[128,2176]{1,0:T(8,128)(2,1)S(1)} collective-permute-done((bf16[128,2176]{1,0:T(8,128)(2,1)S(1)}, bf16[128,2176]{1,0:T(8,128)(2,1)S(1)}, u32[]{:S(2)}, u32[]{:S(2)}) %collective-permute-start.29) | collective-permute-done | bytes 557088 | tf_op jit(solution)/shard_map/ppermute | solution.py:519
  202.6 1.5 settle.1
  204.2 3.8 %all-to-all-start.3 = ((bf16[16,16,2176]{2,1,0:T(8,128)(2,1)}), bf16[16,16,2176]{2,1,0:T(8,128)(2,1)S(1)}, u32[]{:S(2)}, u32[]{:S(2)}) async-start(bf16[16,16,2176]{2,1,0:T(8,128)(2,1)} %bitcast.27), calls=%async_computation.3 | async-start | bytes 2228224 | tf_op jit(solution)/shard_map/all_to_all | solution.py:676
  208.1 18.0 %all-to-all-done.3 = bf16[16,16,2176]{2,1,0:T(8,128)(2,1)S(1)} async-done(((bf16[16,16,2176]{2,1,0:T(8,128)(2,1)}), bf16[16,16,2176]{2,1,0:T(8,128)(2,1)S(1)}, u32[]{:S(2)}, u32[]{:S(2)}) %all-to-all-start.3) | async-done | bytes 1114144 | tf_op jit(solution)/shard_map/all_to_all | solution.py:676
  226.1 2.6 %combine.1 = bf16[64,2,2048]{2,1,0:T(2,128)(2,1)} custom-call(bf16[256,2176]{1,0:T(8,128)(2,1)S(1)} %bitcast.75, s32[128,2]{1,0:T(8,128)S(1)} %bitcast_select_fusion.places, f32[128,2]{1,0:T(8,128)S(1)} %bitcast.83, f32[128,2048]{1,0:T(8,128)S(1)} %copy-done.12, f32[4,2048]{1,0:T(4,128)S(1)} %copy-done.13), custom_call_target="tpu_custom_call" | custom-call | flops 1000000000 | bytes 4194304 | tf_op jit(solution)/shard_map/combine/pallas_call | solution.py:394
  (133 shorter events, 22.7 us)
Async XLA Ops:
  1.6 35.5 %copy-start.3 = (bf16[2,512,128]{2,1,0:T(8,128)(2,1)}, bf16[2,512,128]{2,1,0:T(8,128)(2,1)S(1)}, u32[]{:S(2)}) copy-start(bf16[2,512,128]{2,1,0:T(8,128)(2,1)S(1)} %get-tuple-element.125.reads) | copy-start | bytes 786436
  1.6 11.8 %copy-start.33 = (f32[8]{0:T(128)S(1)}, f32[8]{0:T(128)}, u32[]{:S(2)}) copy-start(f32[8]{0:T(128)} %param.23) | copy-start | bytes 100
  5.4 9.6 %copy-start.19 = (f32[2,512,128]{2,1,0:T(8,128)}, f32[2,512,128]{2,1,0:T(8,128)S(1)}, u32[]{:S(2)}) copy-start(f32[2,512,128]{2,1,0:T(8,128)S(1)} %get-tuple-element.57.first) | copy-start | bytes 1572868
  5.4 16.8 %all-to-all-start = ((bf16[16,72,128]{2,1,0:T(8,128)(2,1)}), bf16[16,72,128]{2,1,0:T(8,128)(2,1)S(1)}, u32[]{:S(2)}, u32[]{:S(2)}) async-start(bf16[16,72,128]{2,1,0:T(8,128)(2,1)} %get-tuple-element.59), calls=%async_computation | async-start | bytes 589824 | tf_op jit(solution)/shard_map/all_to_all | solution.py:625
  14.9 22.2 %copy-start = (bf16[512,2,512]{2,0,1:T(8,128)(2,1)}, bf16[512,2,512]{2,0,1:T(8,128)(2,1)S(1)}, u32[]{:S(2)}) copy-start(bf16[512,2,512]{2,0,1:T(8,128)(2,1)S(1)} %copy.49) | copy-start | bytes 3145732
  24.7 12.5 %all-to-all-start.1 = ((bf16[16,64,128]{2,1,0:T(8,128)(2,1)}), bf16[16,64,128]{2,1,0:T(8,128)(2,1)S(1)}, u32[]{:S(2)}, u32[]{:S(2)}) async-start(bf16[16,64,128]{2,1,0:T(8,128)(2,1)} %scan.1), calls=%async_computation.1 | async-start | bytes 524288 | tf_op jit(solution)/shard_map/all_to_all | solution.py:631
  29.7 7.5 %copy-start.14 = (f32[512]{0:T(512)S(1)}, f32[512]{0:T(512)}, u32[]{:S(2)}) copy-start(f32[512]{0:T(512)} %param.24) | copy-start | bytes 6148
  29.7 7.5 %copy-start.22 = (f32[1,512,8]{2,1,0:T(8,128)S(1)}, f32[1,512,8]{2,1,0:T(8,128)}, u32[]{:S(2)}) copy-start(f32[1,512,8]{2,1,0:T(8,128)} %copy-done.21) | copy-start | bytes 49156
  44.2 8.2 %collective-permute-start = (bf16[4,64,2048]{2,1,0:T(8,128)(2,1)}, bf16[4,64,2048]{2,1,0:T(8,128)(2,1)S(1)}, u32[]{:S(2)}, u32[]{:S(2)}) collective-permute-start(bf16[4,64,2048]{2,1,0:T(8,128)(2,1)} %get-tuple-element.65), channel_id=1, source_target_pairs={{0,1},{1,0},{2,3},{3,2},{4,5},{5,4},{6,7},{7,6},{8,9},{9,8},{10,11... | collective-permute-start | bytes 3145736 | tf_op jit(solution)/shard_map/ppermute | solution.py:529
  50.7 5.7 %collective-permute-start.1 = (bf16[4,64,2048]{2,1,0:T(8,128)(2,1)}, bf16[4,64,2048]{2,1,0:T(8,128)(2,1)}, u32[]{:S(2)}, u32[]{:S(2)}) collective-permute-start(bf16[4,64,2048]{2,1,0:T(8,128)(2,1)} %get-tuple-element.69), channel_id=1, source_target_pairs={{0,1},{1,0},{2,3},{3,2},{4,5},{5,4},{6,7},{7,6},{8,9},{9,8},{10,11... | collective-permute-start | bytes 3145736 | tf_op jit(solution)/shard_map/ppermute | solution.py:529
  52.4 5.8 %copy-start.31 = (s32[16,3]{0,1:T(4,128)}, s32[16,3]{0,1:T(4,128)S(1)}, u32[]{:S(2)}) copy-start(s32[16,3]{0,1:T(4,128)S(1)} %reduce-window.9) | copy-start | bytes 580
  53.2 22.8 %collective-permute-start.2 = (bf16[64,2048]{1,0:T(8,128)(2,1)}, bf16[64,2048]{1,0:T(8,128)(2,1)S(1)}, u32[]{:S(2)}, u32[]{:S(2)}) collective-permute-start(bf16[64,2048]{1,0:T(8,128)(2,1)} %get-tuple-element.118), channel_id=1, source_target_pairs={{0,6},{1,7},{2,0},{3,1},{4,2},{5,3},{6,4},{7,5},{8,14},{9,15},{10,... | collective-permute-start | bytes 786440 | tf_op jit(solution)/shard_map/ppermute | solution.py:524
  56.3 10.4 %collective-permute-start.3 = (bf16[64,2048]{1,0:T(8,128)(2,1)S(1)}, bf16[64,2048]{1,0:T(8,128)(2,1)S(1)}, u32[]{:S(2)}, u32[]{:S(2)}) collective-permute-start(bf16[64,2048]{1,0:T(8,128)(2,1)S(1)} %get-tuple-element.117), channel_id=1, source_target_pairs={{0,2},{1,3},{2,4},{3,5},{4,6},{5,7},{6,0},{7,1},{8,10},{9,11},{10,... | collective-permute-start | bytes 786440 | tf_op jit(solution)/shard_map/ppermute | solution.py:519
  58.2 15.2 %slice-start = ((s32[16,3]{0,1:T(4,128)}), s32[16,2]{0,1:T(2,128)S(1)}, s32[]{:S(2)}) async-start(s32[16,3]{0,1:T(4,128)} %copy-done.31), calls=%async_computation.4 | async-start | bytes 2048 | tf_op jit(solution)/shard_map/slice.1
  58.2 17.8 %collective-permute-start.5 = (bf16[64,2048]{1,0:T(8,128)(2,1)}, bf16[64,2048]{1,0:T(8,128)(2,1)}, u32[]{:S(2)}, u32[]{:S(2)}) collective-permute-start(bf16[64,2048]{1,0:T(8,128)(2,1)} %get-tuple-element.116), channel_id=1, source_target_pairs={{0,2},{1,3},{2,4},{3,5},{4,6},{5,7},{6,0},{7,1},{8,10},{9,11},{10,... | collective-permute-start | bytes 786440 | tf_op jit(solution)/shard_map/ppermute | solution.py:519
  58.7 19.9 %copy-start.5 = (f32[2048]{0:T(1024)S(1)}, f32[2048]{0:T(1024)}, u32[]{:S(2)}) copy-start(f32[2048]{0:T(1024)} %param.27) | copy-start | bytes 24580
  58.7 9.2 %collective-permute-start.6 = (bf16[64,2048]{1,0:T(8,128)(2,1)S(1)}, bf16[64,2048]{1,0:T(8,128)(2,1)S(1)}, u32[]{:S(2)}, u32[]{:S(2)}) collective-permute-start(bf16[64,2048]{1,0:T(8,128)(2,1)S(1)} %get-tuple-element.115), channel_id=1, source_target_pairs={{0,6},{1,7},{2,0},{3,1},{4,2},{5,3},{6,4},{7,5},{8,14},{9,15},{10,... | collective-permute-start | bytes 786440 | tf_op jit(solution)/shard_map/ppermute | solution.py:524
  67.5 9.3 %collective-permute-start.4 = (bf16[64,2048]{1,0:T(8,128)(2,1)}, bf16[64,2048]{1,0:T(8,128)(2,1)}, u32[]{:S(2)}, u32[]{:S(2)}) collective-permute-start(bf16[64,2048]{1,0:T(8,128)(2,1)} %fusion.1), channel_id=1, source_target_pairs={{0,2},{1,3},{2,4},{3,5},{4,6},{5,7},{6,0},{7,1},{8,10},{9,11},{10,... | collective-permute-start | bytes 786440 | tf_op jit(solution)/shard_map/ppermute | solution.py:519
  69.7 9.0 %collective-permute-start.7 = (bf16[64,2048]{1,0:T(8,128)(2,1)}, bf16[64,2048]{1,0:T(8,128)(2,1)}, u32[]{:S(2)}, u32[]{:S(2)}) collective-permute-start(bf16[64,2048]{1,0:T(8,128)(2,1)} %fusion), channel_id=1, source_target_pairs={{0,6},{1,7},{2,0},{3,1},{4,2},{5,3},{6,4},{7,5},{8,14},{9,15},{10,... | collective-permute-start | bytes 786440 | tf_op jit(solution)/shard_map/ppermute | solution.py:524
  79.7 26.7 %copy-start.7 = (bf16[1,2048,896]{2,1,0:T(8,128)(2,1)S(1)}, bf16[1,2048,896]{2,1,0:T(8,128)(2,1)}, u32[]{:S(2)}) copy-start(bf16[1,2048,896]{2,1,0:T(8,128)(2,1)} %param.29) | copy-start | bytes 11010052
  82.3 20.2 %copy-start.11 = (f32[128,2048]{1,0:T(8,128)}, f32[128,2048]{1,0:T(8,128)S(1)}, u32[]{:S(2)}) copy-start(f32[128,2048]{1,0:T(8,128)S(1)} %get-tuple-element.108.hidden) | copy-start | bytes 3145732
  82.3 24.1 %copy-start.6 = (bf16[1,2048,896]{2,1,0:T(8,128)(2,1)S(1)}, bf16[1,2048,896]{2,1,0:T(8,128)(2,1)}, u32[]{:S(2)}) copy-start(bf16[1,2048,896]{2,1,0:T(8,128)(2,1)} %param.28) | copy-start | bytes 11010052
  102.4 3.9 %collective-permute-start.10 = (bf16[256,2176]{1,0:T(8,128)(2,1)S(1)}, bf16[256,2176]{1,0:T(8,128)(2,1)S(1)}, u32[]{:S(2)}, u32[]{:S(2)}) collective-permute-start(bf16[256,2176]{1,0:T(8,128)(2,1)S(1)} %bitcast.73), channel_id=1, source_target_pairs={{0,1},{1,0},{2,3},{3,2},{4,5},{5,4},{6,7},{7,6},{8,9},{9,8},{10,11... | collective-permute-start | bytes 3342344 | tf_op jit(solution)/shard_map/ppermute | solution.py:529
  102.5 17.1 %collective-permute-start.8 = (bf16[128,2176]{1,0:T(8,128)(2,1)S(1)}, bf16[128,2176]{1,0:T(8,128)(2,1)S(1)}, u32[]{:S(2)}, u32[]{:S(2)}) collective-permute-start(bf16[128,2176]{1,0:T(8,128)(2,1)S(1)} %bitcast.101), channel_id=1, source_target_pairs={{0,2},{1,3},{2,4},{3,5},{4,6},{5,7},{6,0},{7,1},{8,10},{9,11},{10,... | collective-permute-start | bytes 1671176 | tf_op jit(solution)/shard_map/ppermute | solution.py:519
  102.6 17.0 %collective-permute-start.9 = (bf16[128,2176]{1,0:T(8,128)(2,1)S(1)}, bf16[128,2176]{1,0:T(8,128)(2,1)S(1)}, u32[]{:S(2)}, u32[]{:S(2)}) collective-permute-start(bf16[128,2176]{1,0:T(8,128)(2,1)S(1)} %bitcast.99), channel_id=1, source_target_pairs={{0,6},{1,7},{2,0},{3,1},{4,2},{5,3},{6,4},{7,5},{8,14},{9,15},{10,... | collective-permute-start | bytes 1671176 | tf_op jit(solution)/shard_map/ppermute | solution.py:524
  119.6 3.8 %collective-permute-start.14 = (bf16[128,2176]{1,0:T(8,128)(2,1)S(1)}, bf16[128,2176]{1,0:T(8,128)(2,1)S(1)}, u32[]{:S(2)}, u32[]{:S(2)}) collective-permute-start(bf16[128,2176]{1,0:T(8,128)(2,1)S(1)} %collective-permute-done.8.refs_0_), channel_id=1, source_target_pairs={{0,1},{1,0},{2,3},{3,2},{4,5},{5,4},{6,7},{7,6},{8,9},{9,8},{10,11... | collective-permute-start | bytes 1671176 | tf_op jit(solution)/shard_map/ppermute | solution.py:529
  119.6 3.8 %collective-permute-start.15 = (bf16[128,2176]{1,0:T(8,128)(2,1)S(1)}, bf16[128,2176]{1,0:T(8,128)(2,1)S(1)}, u32[]{:S(2)}, u32[]{:S(2)}) collective-permute-start(bf16[128,2176]{1,0:T(8,128)(2,1)S(1)} %collective-permute-done.9.refs_1_), channel_id=1, source_target_pairs={{0,1},{1,0},{2,3},{3,2},{4,5},{5,4},{6,7},{7,6},{8,9},{9,8},{10,11... | collective-permute-start | bytes 1671176 | tf_op jit(solution)/shard_map/ppermute | solution.py:529
  120.1 16.3 %collective-permute-start.13 = (bf16[256,2176]{1,0:T(8,128)(2,1)S(1)}, bf16[256,2176]{1,0:T(8,128)(2,1)S(1)}, u32[]{:S(2)}, u32[]{:S(2)}) collective-permute-start(bf16[256,2176]{1,0:T(8,128)(2,1)S(1)} %get-tuple-element.76), channel_id=1, source_target_pairs={{0,1},{1,0},{2,3},{3,2},{4,5},{5,4},{6,7},{7,6},{8,9},{9,8},{10,11... | collective-permute-start | bytes 3342344 | tf_op jit(solution)/shard_map/ppermute | solution.py:529
  120.1 16.3 %collective-permute-start.11 = (bf16[128,2176]{1,0:T(8,128)(2,1)S(1)}, bf16[128,2176]{1,0:T(8,128)(2,1)S(1)}, u32[]{:S(2)}, u32[]{:S(2)}) collective-permute-start(bf16[128,2176]{1,0:T(8,128)(2,1)S(1)} %collective-permute-done.8.refs_0_), channel_id=1, source_target_pairs={{0,2},{1,3},{2,4},{3,5},{4,6},{5,7},{6,0},{7,1},{8,10},{9,11},{10,... | collective-permute-start | bytes 1671176 | tf_op jit(solution)/shard_map/ppermute | solution.py:519
  121.2 15.2 %collective-permute-start.12 = (bf16[128,2176]{1,0:T(8,128)(2,1)S(1)}, bf16[128,2176]{1,0:T(8,128)(2,1)S(1)}, u32[]{:S(2)}, u32[]{:S(2)}) collective-permute-start(bf16[128,2176]{1,0:T(8,128)(2,1)S(1)} %collective-permute-done.9.refs_1_), channel_id=1, source_target_pairs={{0,6},{1,7},{2,0},{3,1},{4,2},{5,3},{6,4},{7,5},{8,14},{9,15},{10,... | collective-permute-start | bytes 1671176 | tf_op jit(solution)/shard_map/ppermute | solution.py:524
  136.4 3.5 %collective-permute-start.18 = (bf16[256,2176]{1,0:T(8,128)(2,1)S(1)}, bf16[256,2176]{1,0:T(8,128)(2,1)S(1)}, u32[]{:S(2)}, u32[]{:S(2)}) collective-permute-start(bf16[256,2176]{1,0:T(8,128)(2,1)S(1)} %get-tuple-element.83), channel_id=1, source_target_pairs={{0,1},{1,0},{2,3},{3,2},{4,5},{5,4},{6,7},{7,6},{8,9},{9,8},{10,11... | collective-permute-start | bytes 3342344 | tf_op jit(solution)/shard_map/ppermute | solution.py:529
  136.4 15.5 %collective-permute-start.16 = (bf16[128,2176]{1,0:T(8,128)(2,1)S(1)}, bf16[128,2176]{1,0:T(8,128)(2,1)S(1)}, u32[]{:S(2)}, u32[]{:S(2)}) collective-permute-start(bf16[128,2176]{1,0:T(8,128)(2,1)S(1)} %bitcast.102), channel_id=1, source_target_pairs={{0,6},{1,7},{2,0},{3,1},{4,2},{5,3},{6,4},{7,5},{8,14},{9,15},{10,... | collective-permute-start | bytes 1671176 | tf_op jit(solution)/shard_map/ppermute | solution.py:524
  139.4 16.0 %collective-permute-start.17 = (bf16[128,2176]{1,0:T(8,128)(2,1)S(1)}, bf16[128,2176]{1,0:T(8,128)(2,1)S(1)}, u32[]{:S(2)}, u32[]{:S(2)}) collective-permute-start(bf16[128,2176]{1,0:T(8,128)(2,1)S(1)} %bitcast.100), channel_id=1, source_target_pairs={{0,2},{1,3},{2,4},{3,5},{4,6},{5,7},{6,0},{7,1},{8,10},{9,11},{10,... | collective-permute-start | bytes 1671176 | tf_op jit(solution)/shard_map/ppermute | solution.py:519
  139.4 2.0 collective-permute-start.19
  139.6 2.5 %collective-permute-start.20 = (bf16[128,2176]{1,0:T(8,128)(2,1)S(1)}, bf16[128,2176]{1,0:T(8,128)(2,1)S(1)}, u32[]{:S(2)}, u32[]{:S(2)}) collective-permute-start(bf16[128,2176]{1,0:T(8,128)(2,1)S(1)} %collective-permute-done.12.refs_1_), channel_id=1, source_target_pairs={{0,1},{1,0},{2,3},{3,2},{4,5},{5,4},{6,7},{7,6},{8,9},{9,8},{10,11... | collective-permute-start | bytes 1671176 | tf_op jit(solution)/shard_map/ppermute | solution.py:529
  155.3 2.8 %collective-permute-start.21 = (bf16[256,2176]{1,0:T(8,128)(2,1)S(1)}, bf16[256,2176]{1,0:T(8,128)(2,1)S(1)}, u32[]{:S(2)}, u32[]{:S(2)}) collective-permute-start(bf16[256,2176]{1,0:T(8,128)(2,1)S(1)} %get-tuple-element.91), channel_id=1, source_target_pairs={{0,1},{1,0},{2,3},{3,2},{4,5},{5,4},{6,7},{7,6},{8,9},{9,8},{10,11... | collective-permute-start | bytes 3342344 | tf_op jit(solution)/shard_map/ppermute | solution.py:529
  155.3 15.4 %collective-permute-start.24 = (bf16[128,2176]{1,0:T(8,128)(2,1)S(1)}, bf16[128,2176]{1,0:T(8,128)(2,1)S(1)}, u32[]{:S(2)}, u32[]{:S(2)}) collective-permute-start(bf16[128,2176]{1,0:T(8,128)(2,1)S(1)} %get-tuple-element.96), channel_id=1, source_target_pairs={{0,6},{1,7},{2,0},{3,1},{4,2},{5,3},{6,4},{7,5},{8,14},{9,15},{10,... | collective-permute-start | bytes 1671176 | tf_op jit(solution)/shard_map/ppermute | solution.py:524
  155.6 16.7 %collective-permute-start.25 = (bf16[128,2176]{1,0:T(8,128)(2,1)S(1)}, bf16[128,2176]{1,0:T(8,128)(2,1)S(1)}, u32[]{:S(2)}, u32[]{:S(2)}) collective-permute-start(bf16[128,2176]{1,0:T(8,128)(2,1)S(1)} %get-tuple-element.97), channel_id=1, source_target_pairs={{0,2},{1,3},{2,4},{3,5},{4,6},{5,7},{6,0},{7,1},{8,10},{9,11},{10,... | collective-permute-start | bytes 1671176 | tf_op jit(solution)/shard_map/ppermute | solution.py:519
  157.4 2.0 collective-permute-start.26
  157.4 4.3 %collective-permute-start.27 = (bf16[128,2176]{1,0:T(8,128)(2,1)S(1)}, bf16[128,2176]{1,0:T(8,128)(2,1)S(1)}, u32[]{:S(2)}, u32[]{:S(2)}) collective-permute-start(bf16[128,2176]{1,0:T(8,128)(2,1)S(1)} %collective-permute-done.17.refs_1_), channel_id=1, source_target_pairs={{0,1},{1,0},{2,3},{3,2},{4,5},{5,4},{6,7},{7,6},{8,9},{9,8},{10,11... | collective-permute-start | bytes 1671176 | tf_op jit(solution)/shard_map/ppermute | solution.py:529
  158.3 25.2 %collective-permute-start.22 = (bf16[128,2176]{1,0:T(8,128)(2,1)S(1)}, bf16[128,2176]{1,0:T(8,128)(2,1)S(1)}, u32[]{:S(2)}, u32[]{:S(2)}) collective-permute-start(bf16[128,2176]{1,0:T(8,128)(2,1)S(1)} %get-tuple-element.94), channel_id=1, source_target_pairs={{0,2},{1,3},{2,4},{3,5},{4,6},{5,7},{6,0},{7,1},{8,10},{9,11},{10,... | collective-permute-start | bytes 1671176 | tf_op jit(solution)/shard_map/ppermute | solution.py:519
  159.3 24.2 %collective-permute-start.23 = (bf16[128,2176]{1,0:T(8,128)(2,1)S(1)}, bf16[128,2176]{1,0:T(8,128)(2,1)S(1)}, u32[]{:S(2)}, u32[]{:S(2)}) collective-permute-start(bf16[128,2176]{1,0:T(8,128)(2,1)S(1)} %get-tuple-element.95), channel_id=1, source_target_pairs={{0,6},{1,7},{2,0},{3,1},{4,2},{5,3},{6,4},{7,5},{8,14},{9,15},{10,... | collective-permute-start | bytes 1671176 | tf_op jit(solution)/shard_map/ppermute | solution.py:524
  183.5 2.8 %collective-permute-start.28 = (bf16[256,2176]{1,0:T(8,128)(2,1)S(1)}, bf16[256,2176]{1,0:T(8,128)(2,1)S(1)}, u32[]{:S(2)}, u32[]{:S(2)}) collective-permute-start(bf16[256,2176]{1,0:T(8,128)(2,1)S(1)} %get-tuple-element.104), channel_id=1, source_target_pairs={{0,1},{1,0},{2,3},{3,2},{4,5},{5,4},{6,7},{7,6},{8,9},{9,8},{10,11... | collective-permute-start | bytes 3342344 | tf_op jit(solution)/shard_map/ppermute | solution.py:529
  186.7 15.9 %collective-permute-start.29 = (bf16[128,2176]{1,0:T(8,128)(2,1)S(1)}, bf16[128,2176]{1,0:T(8,128)(2,1)S(1)}, u32[]{:S(2)}, u32[]{:S(2)}) collective-permute-start(bf16[128,2176]{1,0:T(8,128)(2,1)S(1)} %get-tuple-element.110), channel_id=1, source_target_pairs={{0,2},{1,3},{2,4},{3,5},{4,6},{5,7},{6,0},{7,1},{8,10},{9,11},{10,... | collective-permute-start | bytes 1671176 | tf_op jit(solution)/shard_map/ppermute | solution.py:519
  187.3 15.3 %collective-permute-start.30 = (bf16[128,2176]{1,0:T(8,128)(2,1)S(1)}, bf16[128,2176]{1,0:T(8,128)(2,1)S(1)}, u32[]{:S(2)}, u32[]{:S(2)}) collective-permute-start(bf16[128,2176]{1,0:T(8,128)(2,1)S(1)} %get-tuple-element.109), channel_id=1, source_target_pairs={{0,6},{1,7},{2,0},{3,1},{4,2},{5,3},{6,4},{7,5},{8,14},{9,15},{10,... | collective-permute-start | bytes 1671176 | tf_op jit(solution)/shard_map/ppermute | solution.py:524
  204.2 21.9 %copy-start.12 = (f32[128,2048]{1,0:T(8,128)S(1)}, f32[128,2048]{1,0:T(8,128)}, u32[]{:S(2)}) copy-start(f32[128,2048]{1,0:T(8,128)} %copy-done.11) | copy-start | bytes 3145732
  204.2 21.9 %copy-start.13 = (f32[4,2048]{1,0:T(4,128)S(1)}, f32[4,2048]{1,0:T(4,128)}, u32[]{:S(2)}) copy-start(f32[4,2048]{1,0:T(4,128)} %directions.1) | copy-start | bytes 98308
  204.2 21.9 %all-to-all-start.3 = ((bf16[16,16,2176]{2,1,0:T(8,128)(2,1)}), bf16[16,16,2176]{2,1,0:T(8,128)(2,1)S(1)}, u32[]{:S(2)}, u32[]{:S(2)}) async-start(bf16[16,16,2176]{2,1,0:T(8,128)(2,1)} %bitcast.27), calls=%async_computation.3 | async-start | bytes 2228224 | tf_op jit(solution)/shard_map/all_to_all | solution.py:676
  (21 other events, 40.6 us)
